TPU v7x, 32 devices: a whole 2x2x4 slice. The times are simulated.
32 devices in a mesh: flow: 8 (over z, x), grad: 4 (over y, core).
Axes of the slice: x: 2, y: 2, z: 4, core: 2. Of those that a mesh axis runs over, the one named last changes fastest.
Arguments:
- populations: float32 [19, 64, 32, 128], P(None, 'flow', 'grad'), may hold values from 0.008 to 1.01, as said below
- le_offset: int32 [1], replicated, may hold values from 0 to 63
- sphere_velocity: float32 [3, 8, 4, 64], P(None, 'flow', 'grad'), may hold values from -0.4 to 0.4
- link_cell: int32 [8, 4, 16384], P('flow', 'grad'), may hold values from 0 to 8191, as said below
- link_dir: int32 [8, 4, 16384], P('flow', 'grad'), may hold values from 1 to 18, as said below
- link_sphere: int32 [8, 4, 16384], P('flow', 'grad'), may hold values from 0 to 575
- link_count: int32 [8, 4], P('flow', 'grad'), may hold values from 4096 to 16384, as said below
- pair_first: int32 [8, 4, 256], P('flow', 'grad'), may hold values from 0 to 63
- pair_second: int32 [8, 4, 256], P('flow', 'grad'), may hold values from 0 to 575
- pair_count: int32 [8, 4], P('flow', 'grad'), may hold values from 64 to 256, as said below
- pair_gap: float32 [8, 4, 256], P('flow', 'grad'), may hold values from 0.02 to 1
- pair_normal: float32 [3, 8, 4, 256], P(None, 'flow', 'grad'), may hold values from -1 to 1
Outputs:
- populations_next: float32 [19, 64, 32, 128], P(None, 'flow', 'grad')
- sphere_force: float32 [3, 8, 4, 64], P(None, 'flow', 'grad')
- velocity_next: float32 [3, 8, 4, 64], P(None, 'flow', 'grad')
Inputs may be any that keep to these rules, and one draw needn't show every extreme that they name: `populations`: each population lies between 0.3 and 3 times its direction's lattice weight. `link_cell`: local cell numbers (x_local * 8 + y_local) * 128 + z; within one tile no two link slots name the same cell and direction, and a cell may carry several links. `link_dir`: within one tile no two link slots name the same cell and direction. Live links of a tile are its first link_count slots; in every draw some tile has all 16384 slots live. Live pairs of a tile are its first pair_count slots; in every draw some tile has all 256 slots live.
All inputs are finite; a program needn't handle non-finite values.
Results may differ from a plain program's by a relative error of at most 0.0003.
Values sent between devices are 32-bit elements; how exact they have to be, the bound alone decides.
No kernel may reach another device: no remote copies, remote signals or barrier semaphores. Data moves between devices by JAX's collectives and lax.ppermute only.
A program may use at most 64 MiB of HBM per device.

v0:
```python
import jax
import jax.numpy as jnp
from jax import lax
from jax.sharding import PartitionSpec as P

VELOCITIES = [
    (0, 0, 0),
    (1, 0, 0),
    (-1, 0, 0),
    (0, 1, 0),
    (0, -1, 0),
    (0, 0, 1),
    (0, 0, -1),
    (1, 1, 0),
    (-1, -1, 0),
    (1, -1, 0),
    (-1, 1, 0),
    (1, 0, 1),
    (-1, 0, -1),
    (1, 0, -1),
    (-1, 0, 1),
    (0, 1, 1),
    (0, -1, -1),
    (0, 1, -1),
    (0, -1, 1),
]
WEIGHTS = [1.0 / 3.0] + [1.0 / 18.0] * 6 + [1.0 / 36.0] * 12
XY_MOVING = [1, 2, 3, 4, 7, 8, 9, 10, 11, 12, 13, 14, 15, 16, 17, 18]
UPWARD = [3, 7, 10, 15, 17]
DOWNWARD = [4, 8, 9, 16, 18]
RIGHTWARD = [1, 7, 9, 11, 13]
LEFTWARD = [2, 8, 10, 12, 14]
RELAX_TIME = 0.8
SHEAR_SPEED = 0.1
LUB_COEF = 0.5
GAP_FLOOR = 0.1
GAP_CUTOFF = 1.0
INV_MASS = 1.0 / 523.6


def from_behind(block, axis, distance):
    devices = range(lax.axis_size(axis))
    route = [((i - distance) % len(devices), i) for i in devices]
    return lax.ppermute(block, axis, route)


def padded(block, sides, width):
    for axis, dim in sides:
        count = lax.axis_size(axis)
        forward = [(i, i + 1) for i in range(count - 1)]
        forward.append((count - 1, 0))
        backward = [(target, source) for source, target in forward]
        low = lax.ppermute(
            lax.slice_in_dim(block, block.shape[dim] - width, None, axis=dim), axis, forward
        )
        high = lax.ppermute(lax.slice_in_dim(block, 0, width, axis=dim), axis, backward)
        block = jnp.concatenate([low, block, high], axis=dim)
    return block


def collide(populations):
    density = jnp.sum(populations, axis=0)
    speeds = []
    for axis_id in range(3):
        running = None
        for direction, vector in enumerate(VELOCITIES):
            if vector[axis_id] != 0:
                addend = vector[axis_id] * populations[direction]
                running = addend if running is None else running + addend
        speeds.append(running / density)
    speed_sq = speeds[0] * speeds[0] + speeds[1] * speeds[1] + speeds[2] * speeds[2]
    relaxed = []
    for direction, vector in enumerate(VELOCITIES):
        c_dot = None
        for axis_id in range(3):
            if vector[axis_id] != 0:
                addend = vector[axis_id] * speeds[axis_id]
                c_dot = addend if c_dot is None else c_dot + addend
        if c_dot is None:
            equil = WEIGHTS[direction] * density * (1.0 - 1.5 * speed_sq)
        else:
            equil = (
                WEIGHTS[direction]
                * density
                * (1.0 + 3.0 * c_dot + 4.5 * c_dot * c_dot - 1.5 * speed_sq)
            )
        current = populations[direction]
        relaxed.append(current - (current - equil) / RELAX_TIME)
    return (relaxed, density)


def tile_links(
    relaxed,
    density,
    propagated,
    near_speed,
    link_cell,
    link_dir,
    link_sphere,
    link_count,
    pair_first,
    pair_second,
    pair_count,
    pair_gap,
    pair_normal,
):
    n_cells = relaxed.shape[1]
    slot_count = near_speed.shape[1] // 9
    onehot = (link_dir[None, :] == lax.iota(jnp.int32, 19)[:, None]).astype(relaxed.dtype)
    lookup = jnp.asarray(
        [[vector[k] for vector in VELOCITIES] for k in range(3)] + [WEIGHTS], relaxed.dtype
    )
    picked = jnp.dot(lookup, onehot, precision=lax.Precision.HIGHEST)
    leaving = jnp.sum(onehot * relaxed[:, link_cell], axis=0)
    wall_speed = near_speed[:, link_sphere]
    c_dot_u = jnp.sum(picked[:3] * wall_speed, axis=0)
    bounced = leaving - 6.0 * picked[3] * density[link_cell] * c_dot_u
    is_live = lax.iota(jnp.int32, link_dir.shape[0]) < link_count
    opposite = jnp.where(link_dir % 2 == 1, link_dir + 1, link_dir - 1)
    target = jnp.where(is_live, opposite * n_cells + link_cell, 19 * n_cells)
    updated = propagated.reshape(-1).at[target].set(bounced, mode="drop").reshape(19, n_cells)
    link_force = picked[:3] * (leaving + bounced) * is_live.astype(relaxed.dtype)
    pair_live = (lax.iota(jnp.int32, pair_first.shape[0]) < pair_count).astype(relaxed.dtype)
    first_ref = pair_first + 4 * slot_count
    first_speed = near_speed[:, first_ref]
    second_speed = near_speed[:, pair_second]
    normal_rate = jnp.sum((first_speed - second_speed) * pair_normal, axis=0)
    resist = LUB_COEF * (1.0 / jnp.maximum(pair_gap, GAP_FLOOR) - 1.0 / GAP_CUTOFF)
    lubrication = -resist * normal_rate * pair_normal * pair_live
    sphere_refs = jnp.concatenate([link_sphere, first_ref, pair_second])
    values = jnp.concatenate([link_force, lubrication, -lubrication], axis=1)
    partial_value = jax.ops.segment_sum(values.T, sphere_refs, num_segments=9 * slot_count).T
    return (updated, partial_value)


def edge_slice(behind, ahead, cell_rest):
    width_x = ahead.shape[1]
    joined = jnp.concatenate([behind, ahead], axis=1)
    return lax.dynamic_slice_in_dim(joined, width_x - cell_rest, width_x, 1)


def rows_of(directions):
    return [XY_MOVING.index(direction) for direction in directions]


def boosts_of(directions):
    return jnp.asarray(
        [6.0 * WEIGHTS[d] * VELOCITIES[d][0] * SHEAR_SPEED for d in directions], jnp.float32
    )[:, None, None]


def per_device(
    populations,
    le_offset,
    sphere_velocity,
    link_cell,
    link_dir,
    link_sphere,
    link_count,
    pair_first,
    pair_second,
    pair_count,
    pair_gap,
    pair_normal,
):
    relaxed, density = collide(populations)
    width_x = populations.shape[1]
    width_y = populations.shape[2]
    depth = populations.shape[3]
    moving = jnp.stack([relaxed[direction] for direction in XY_MOVING])
    up_rows = rows_of(UPWARD)
    down_rows = rows_of(DOWNWARD)
    top_layer = moving[jnp.asarray(up_rows)][:, :, width_y - 1, :]
    bottom_layer = moving[jnp.asarray(down_rows)][:, :, 0, :]
    offset_cells = le_offset[0]
    flow_count = lax.axis_size("flow")
    span_x = flow_count * width_x
    amounts = jnp.stack([(span_x - offset_cells) % span_x, offset_cells])
    device_hops = amounts // width_x
    cell_rest = amounts % width_x
    hop_counts = jnp.concatenate([device_hops, (device_hops + 1) % flow_count])
    layers_now = jnp.stack([top_layer, bottom_layer, top_layer, bottom_layer])
    for level in range(max(flow_count - 1, 1).bit_length()):
        arrived = from_behind(layers_now, "flow", 1 << level)
        selected = hop_counts // (1 << level) % 2 == 1
        layers_now = jnp.where(selected[:, None, None, None], arrived, layers_now)
    top_moved = edge_slice(layers_now[2], layers_now[0], cell_rest[0])
    bottom_moved = edge_slice(layers_now[3], layers_now[1], cell_rest[1])
    grad_index = lax.axis_index("grad")
    grad_count = lax.axis_size("grad")
    top_send = jnp.where(grad_index == grad_count - 1, top_moved - boosts_of(UPWARD), top_layer)
    bottom_send = jnp.where(grad_index == 0, bottom_moved + boosts_of(DOWNWARD), bottom_layer)
    from_below = from_behind(top_send, "grad", 1)
    from_above = from_behind(bottom_send, "grad", -1)
    blank_row = jnp.zeros((16, width_x, depth), jnp.float32)
    low_row = blank_row.at[jnp.asarray(up_rows)].set(from_below)
    high_row = blank_row.at[jnp.asarray(down_rows)].set(from_above)
    extended = jnp.concatenate([low_row[:, :, None], moving, high_row[:, :, None]], axis=2)
    right_rows = rows_of(RIGHTWARD)
    left_rows = rows_of(LEFTWARD)
    from_left = from_behind(extended[jnp.asarray(right_rows)][:, width_x - 1], "flow", 1)
    from_right = from_behind(extended[jnp.asarray(left_rows)][:, 0], "flow", -1)
    blank_col = jnp.zeros((16, width_y + 2, depth), jnp.float32)
    left_col = blank_col.at[jnp.asarray(right_rows)].set(from_left)
    right_col = blank_col.at[jnp.asarray(left_rows)].set(from_right)
    ghosted = jnp.concatenate([left_col[:, None], extended, right_col[:, None]], axis=1)
    propagated = []
    for direction, vector in enumerate(VELOCITIES):
        if direction in XY_MOVING:
            source = ghosted[
                XY_MOVING.index(direction),
                1 - vector[0] : 1 - vector[0] + width_x,
                1 - vector[1] : 1 - vector[1] + width_y,
                :,
            ]
        else:
            source = relaxed[direction]
        propagated.append(jnp.roll(source, vector[2], axis=2))
    slot_count = sphere_velocity.shape[3]
    rim_speed = padded(sphere_velocity, (("flow", 1), ("grad", 2)), 1)
    near_speed = rim_speed.reshape(3, 9 * slot_count)
    n_cells = width_x * width_y * depth
    updated, partial_value = tile_links(
        jnp.stack(relaxed).reshape(19, n_cells),
        density.reshape(n_cells),
        jnp.stack(propagated).reshape(19, n_cells),
        near_speed,
        link_cell[0, 0],
        link_dir[0, 0],
        link_sphere[0, 0],
        link_count[0, 0],
        pair_first[0, 0],
        pair_second[0, 0],
        pair_count[0, 0],
        pair_gap[0, 0],
        pair_normal[:, 0, 0],
    )
    gathered_parts = padded(
        partial_value.reshape(3, 1, 1, 9, slot_count), (("flow", 1), ("grad", 2)), 1
    )
    gathered_parts = jnp.flip(gathered_parts.reshape(3, 9, 9, slot_count), axis=2)
    own_force = jnp.sum(jnp.diagonal(gathered_parts, axis1=1, axis2=2), axis=-1)
    sphere_force = own_force[:, None, None, :]
    velocity_next = sphere_velocity + INV_MASS * sphere_force
    return (updated.reshape(19, width_x, width_y, depth), sphere_force, velocity_next)


def solution(mesh):
    in_specs = (
        P(None, "flow", "grad", None),
        P(),
        P(None, "flow", "grad", None),
        P("flow", "grad", None),
        P("flow", "grad", None),
        P("flow", "grad", None),
        P("flow", "grad"),
        P("flow", "grad", None),
        P("flow", "grad", None),
        P("flow", "grad"),
        P("flow", "grad", None),
        P(None, "flow", "grad", None),
    )
    out_specs = (
        P(None, "flow", "grad", None),
        P(None, "flow", "grad", None),
        P(None, "flow", "grad", None),
    )
    return jax.shard_map(
        per_device, mesh=mesh, in_specs=in_specs, out_specs=out_specs, check_vma=False
    )
```

profile of v0, /device:TPU:0, one launch (start us, length us, event | category | flops | bytes accessed | tf_op | source)
XLA Modules:
  0.0 449.1 jit_solution(1060411265500210193)
XLA Ops:
  0.7 3.0 collective-permute-start.7
  3.7 3.1 collective-permute-start.8
  6.8 1.1 reduce_sum.51
  7.9 1.1 multiply_subtract_fusion.1
  9.0 0.8 constant_dynamic-update-slice_fusion.15
  9.8 0.8 constant_dynamic-update-slice_fusion.14
  10.6 0.8 constant_dynamic-update-slice_fusion.13
  11.4 0.8 constant_dynamic-update-slice_fusion.12
  12.2 0.8 constant_dynamic-update-slice_fusion.11
  13.0 0.8 constant_dynamic-update-slice_fusion.10
  13.7 0.8 constant_dynamic-update-slice_fusion.9
  14.5 0.8 constant_dynamic-update-slice_fusion.8
  15.3 0.8 constant_dynamic-update-slice_fusion.7
  16.1 0.8 constant_dynamic-update-slice_fusion.6
  16.9 0.8 constant_dynamic-update-slice_fusion.5
  17.7 0.8 constant_dynamic-update-slice_fusion.4
  18.5 0.8 constant_dynamic-update-slice_fusion.3
  19.3 0.8 constant_dynamic-update-slice_fusion.2
  20.1 0.8 constant_dynamic-update-slice_fusion.1
  20.9 0.8 constant_dynamic-update-slice_fusion
  25.7 0.9 stack.164
  26.7 2.7 copy.94
  30.0 56.6 %gather_fusion.4 = f32[16384,19]{1,0:T(8,128)} fusion(f32[19,8192]{0,1:T(8,128)} %copy.94, s32[16384]{0:T(1024)S(1)} %get-tuple-element.93), kind=kCustom, calls=%fused_computation.4 | custom fusion | bytes 2555904 | tf_op jit(solution)/shard_map/gather | solution.py:114
  86.7 8.4 %fusion = f32[16384]{0:T(1024)S(1)} fusion(f32[16384,19]{1,0:T(8,128)} %gather_fusion.4, s32[16384]{0:T(1024)S(1)} %bitcast.458), kind=kLoop, calls=%fused_computation.17 | loop fusion | flops 917504 | bytes 1376256 | tf_op jit(solution)/shard_map/reduce_sum | solution.py:114
  95.1 5.8 %fusion.1 = f32[4,16384]{1,0:T(4,128)S(1)} fusion(f32[4,19]{1,0:T(4,128)S(1)} %copy-done.16, s32[16384]{0:T(1024)S(1)} %bitcast.459), kind=kOutput, calls=%fused_computation.19 | convolution fusion | flops 15253504 | bytes 327984 | tf_op jit(solution)/shard_map/dot_general | solution.py:113
  101.9 0.7 collective-permute-start.10
  105.5 90.5 %gather_fusion.5 = f32[16384]{0:T(1024)S(1)} fusion(f32[8192]{0:T(1024)S(1)} %bitcast.405, s32[16384]{0:T(1024)S(1)} %get-tuple-element.93), kind=kCustom, calls=%fused_computation.5 | custom fusion | bytes 196608 | tf_op jit(solution)/shard_map/gather | solution.py:117
  196.3 54.5 %gather_fusion.6 = f32[16384,3]{1,0:T(8,128)} fusion(f32[3,576]{0,1:T(8,128)S(1)} %bitcast.408, s32[16384]{0:T(1024)S(1)} %get-tuple-element.92), kind=kCustom, calls=%fused_computation.6 | custom fusion | bytes 458752 | tf_op jit(solution)/shard_map/gather | solution.py:115
  250.7 5.4 %copy.96 = f32[16384,3]{0,1:T(4,128)S(1)} copy(f32[16384,3]{1,0:T(8,128)} %gather_fusion.6) | data formatting | bytes 393216 | tf_op jit(solution)/shard_map/gather | solution.py:115
  256.2 0.7 gather_fusion.7
  257.0 0.7 gather_fusion.8
  258.5 4.9 %copy.99 = f32[16896,3]{1,0:T(8,128)} copy(f32[16896,3]{0,1:T(4,128)S(1)} %maximum_bitcast_fusion) | data formatting | bytes 405504 | tf_op jit(solution)/shard_map/transpose | solution.py:132
  263.4 90.4 %scatter_custom_fusion.5 = f32[576,3]{1,0:T(8,128)S(1)} fusion(s32[16896]{0:T(1024)S(1)} %pad_add_fusion, f32[16896,3]{1,0:T(8,128)} %copy.99, f32[]{:T(128)} %constant.187.clone.1), kind=kCustom, calls=%fused_computation.36 | custom fusion | flops 50688 | bytes 7424 | tf_op jit(solution)/shard_map/scatter-add | solution.py:132
  353.9 4.6 %collective-permute-start.12 = (f32[3,1,1,9,64]{4,2,3,1,0:T(1,128)S(1)}, f32[3,1,1,9,64]{4,2,3,1,0:T(1,128)S(1)}, u32[]{:S(2)}, u32[]{:S(2)}) collective-permute-start(f32[3,1,1,9,64]{4,2,3,1,0:T(1,128)S(1)} %copy.100), channel_id=1, source_target_pairs={{4,0},{8,4},{12,8},{16,12},{20,16},{24,20},{28,24},{0,28},{5,1},{9... | collective-permute-start | bytes 20744 | tf_op jit(solution)/shard_map/ppermute | solution.py:56
  358.6 1.3 collective-permute-done.12
  359.9 5.1 %collective-permute-done.11 = f32[3,1,1,9,64]{4,2,3,1,0:T(1,128)S(1)} collective-permute-done((f32[3,1,1,9,64]{4,2,3,1,0:T(1,128)S(1)}, f32[3,1,1,9,64]{4,2,3,1,0:T(1,128)S(1)}, u32[]{:S(2)}, u32[]{:S(2)}) %collective-permute-start.11) | collective-permute-done | bytes 6944 | tf_op jit(solution)/shard_map/ppermute | solution.py:53
  365.8 1.1 collective-permute-done.14
  366.9 2.0 collective-permute-done.13
  369.1 2.5 collective-permute-done.2
  373.4 0.7 scatter_fusion.1
  374.1 1.1 collective-permute-done.3
  375.2 0.7 scatter_fusion
  377.0 2.0 collective-permute-start.5
  380.8 2.9 collective-permute-start.6
  384.1 0.7 scatter_fusion.2
  385.4 0.7 scatter_fusion.3
  387.7 60.6 %scatter_fusion.4 = f32[155648]{0:T(1024)S(1)} fusion(f32[155648]{0:T(1024)S(1)} %bitcast.406, s32[16384]{0:T(1024)S(1)} %bitcast.457, f32[16384]{0:T(1024)S(1)} %multiply_subtract_fusion), kind=kCustom, calls=%fused_computation.14 | custom fusion | bytes 262144 | tf_op jit(solution)/shard_map/scatter | solution.py:121
  448.3 0.8 copy-done
  (150 shorter events, 12.9 us)
Async XLA Ops:
  0.6 28.7 %copy-start.3 = (s32[1,1,16384]{2,1,0:T(1,128)S(1)}, s32[1,1,16384]{2,1,0:T(1,128)}, u32[]{:S(2)}) copy-start(s32[1,1,16384]{2,1,0:T(1,128)} %param.28) | copy-start | bytes 196612
  0.6 28.8 %copy-start.4 = (s32[1,1,16384]{2,1,0:T(1,128)S(1)}, s32[1,1,16384]{2,1,0:T(1,128)}, u32[]{:S(2)}) copy-start(s32[1,1,16384]{2,1,0:T(1,128)} %param.26) | copy-start | bytes 196612
  0.7 28.8 %copy-start.2 = (s32[1,1,16384]{2,1,0:T(1,128)S(1)}, s32[1,1,16384]{2,1,0:T(1,128)}, u32[]{:S(2)}) copy-start(s32[1,1,16384]{2,1,0:T(1,128)} %param.27) | copy-start | bytes 196612
  0.7 101.2 %collective-permute-start.7 = (f32[3,1,1,64]{3,2,1,0:T(1,128)}, f32[3,1,1,64]{3,2,1,0:T(1,128)S(1)}, u32[]{:S(2)}, u32[]{:S(2)}) collective-permute-start(f32[3,1,1,64]{3,2,1,0:T(1,128)} %param.25), channel_id=1, source_target_pairs={{0,4},{4,8},{8,12},{12,16},{16,20},{20,24},{24,28},{28,0},{1,5},{5... | collective-permute-start | bytes 2312 | tf_op jit(solution)/shard_map/ppermute | solution.py:53
  3.7 98.2 %collective-permute-start.8 = (f32[3,1,1,64]{3,2,1,0:T(1,128)}, f32[3,1,1,64]{3,2,1,0:T(1,128)S(1)}, u32[]{:S(2)}, u32[]{:S(2)}) collective-permute-start(f32[3,1,1,64]{3,2,1,0:T(1,128)} %param.25), channel_id=1, source_target_pairs={{4,0},{8,4},{12,8},{16,12},{20,16},{24,20},{28,24},{0,28},{5,1},{9... | collective-permute-start | bytes 2312 | tf_op jit(solution)/shard_map/ppermute | solution.py:56
  23.6 335.0 %collective-permute-start = (f32[4,5,8,128]{3,2,1,0:T(8,128)S(1)}, f32[4,5,8,128]{3,2,1,0:T(8,128)S(1)}, u32[]{:S(2)}, u32[]{:S(2)}) collective-permute-start(f32[4,5,8,128]{3,2,1,0:T(8,128)S(1)} %pad_maximum_fusion.2), channel_id=1, source_target_pairs={{28,0},{0,4},{4,8},{8,12},{12,16},{16,20},{20,24},{24,28},{29,1},{... | collective-permute-start | bytes 245768 | tf_op jit(solution)/shard_map/ppermute | solution.py:44
  30.0 65.1 %copy-start.16 = (f32[4,19]{1,0:T(4,128)S(1)}, f32[4,19]{1,0:T(4,128)}, u32[]{:S(2)}) copy-start(f32[4,19]{1,0:T(4,128)} %constant.228.clone) | copy-start | bytes 916
  86.6 14.3 %copy-start.8 = (s32[1,1,256]{2,1,0:T(1,128)S(1)}, s32[1,1,256]{2,1,0:T(1,128)}, u32[]{:S(2)}) copy-start(s32[1,1,256]{2,1,0:T(1,128)} %param.30) | copy-start | bytes 3076
  86.6 15.0 %copy-start.13 = (f32[1,1,256]{2,1,0:T(1,128)S(1)}, f32[1,1,256]{2,1,0:T(1,128)}, u32[]{:S(2)}) copy-start(f32[1,1,256]{2,1,0:T(1,128)} %param.33) | copy-start | bytes 3076
  86.6 15.0 %copy-start.7 = (s32[1,1,256]{2,1,0:T(1,128)S(1)}, s32[1,1,256]{2,1,0:T(1,128)}, u32[]{:S(2)}) copy-start(s32[1,1,256]{2,1,0:T(1,128)} %param.31) | copy-start | bytes 3076
  86.6 15.0 %copy-start.9 = (s32[5]{0:T(128)S(1)}, s32[5]{0:T(128)}, u32[]{:S(2)}) copy-start(s32[5]{0:T(128)} %constant.275) | copy-start | bytes 64
  86.6 15.0 %copy-start.10 = (s32[5]{0:T(128)S(1)}, s32[5]{0:T(128)}, u32[]{:S(2)}) copy-start(s32[5]{0:T(128)} %constant.269) | copy-start | bytes 64
  86.6 15.1 %copy-start.1 = (f32[19,8,8,128]{3,2,1,0:T(8,128)S(1)}, f32[19,8,8,128]{3,2,1,0:T(8,128)}, u32[]{:S(2)}) copy-start(f32[19,8,8,128]{3,2,1,0:T(8,128)} %param.23) | copy-start | bytes 1867780
  86.6 15.2 %copy-start.6 = (f32[3,1,1,64]{3,2,1,0:T(1,128)S(1)}, f32[3,1,1,64]{3,2,1,0:T(1,128)}, u32[]{:S(2)}) copy-start(f32[3,1,1,64]{3,2,1,0:T(1,128)} %param.25) | copy-start | bytes 2308
  101.9 94.2 %collective-permute-start.10 = (f32[3,3,1,64]{3,2,1,0:T(1,128)S(1)}, f32[3,3,1,64]{3,2,1,0:T(1,128)S(1)}, u32[]{:S(2)}, u32[]{:S(2)}) collective-permute-start(f32[3,3,1,64]{3,2,1,0:T(1,128)S(1)} %constant_dynamic-update-slice_fusion.35), channel_id=1, source_target_pairs={{1,0},{2,1},{3,2},{0,3},{5,4},{6,5},{7,6},{4,7},{9,8},{10,9},{11,1... | collective-permute-start | bytes 6920 | tf_op jit(solution)/shard_map/ppermute | solution.py:56
  102.6 93.4 %collective-permute-start.9 = (f32[3,3,1,64]{3,2,1,0:T(1,128)S(1)}, f32[3,3,1,64]{3,2,1,0:T(1,128)S(1)}, u32[]{:S(2)}, u32[]{:S(2)}) collective-permute-start(f32[3,3,1,64]{3,2,1,0:T(1,128)S(1)} %constant_dynamic-update-slice_fusion.35), channel_id=1, source_target_pairs={{0,1},{1,2},{2,3},{3,0},{4,5},{5,6},{6,7},{7,4},{8,9},{9,10},{10,1... | collective-permute-start | bytes 6920 | tf_op jit(solution)/shard_map/ppermute | solution.py:53
  196.0 62.0 %copy-start.5 = (f32[3,1,1,256]{3,2,1,0:T(1,128)S(1)}, f32[3,1,1,256]{3,2,1,0:T(1,128)}, u32[]{:S(2)}) copy-start(f32[3,1,1,256]{3,2,1,0:T(1,128)} %param.34) | copy-start | bytes 9220
  256.2 115.6 %copy-start.15 = (f32[5]{0:T(128)S(1)}, f32[5]{0:T(128)}, u32[]{:S(2)}) copy-start(f32[5]{0:T(128)} %constant.225.clone) | copy-start | bytes 64
  256.2 115.7 %copy-start.14 = (f32[5]{0:T(128)S(1)}, f32[5]{0:T(128)}, u32[]{:S(2)}) copy-start(f32[5]{0:T(128)} %constant.251) | copy-start | bytes 64
  256.2 117.2 %copy-start.12 = (s32[5]{0:T(128)S(1)}, s32[5]{0:T(128)}, u32[]{:S(2)}) copy-start(s32[5]{0:T(128)} %constant.272) | copy-start | bytes 64
  256.2 119.0 %copy-start.11 = (s32[5]{0:T(128)S(1)}, s32[5]{0:T(128)}, u32[]{:S(2)}) copy-start(s32[5]{0:T(128)} %constant.270) | copy-start | bytes 64
  353.9 6.0 %collective-permute-start.12 = (f32[3,1,1,9,64]{4,2,3,1,0:T(1,128)S(1)}, f32[3,1,1,9,64]{4,2,3,1,0:T(1,128)S(1)}, u32[]{:S(2)}, u32[]{:S(2)}) collective-permute-start(f32[3,1,1,9,64]{4,2,3,1,0:T(1,128)S(1)} %copy.100), channel_id=1, source_target_pairs={{4,0},{8,4},{12,8},{16,12},{20,16},{24,20},{28,24},{0,28},{5,1},{9... | collective-permute-start | bytes 20744 | tf_op jit(solution)/shard_map/ppermute | solution.py:56
  358.5 6.5 %collective-permute-start.11 = (f32[3,1,1,9,64]{4,2,3,1,0:T(1,128)S(1)}, f32[3,1,1,9,64]{4,2,3,1,0:T(1,128)S(1)}, u32[]{:S(2)}, u32[]{:S(2)}) collective-permute-start(f32[3,1,1,9,64]{4,2,3,1,0:T(1,128)S(1)} %copy.100), channel_id=1, source_target_pairs={{0,4},{4,8},{8,12},{12,16},{16,20},{20,24},{24,28},{28,0},{1,5},{5... | collective-permute-start | bytes 20744 | tf_op jit(solution)/shard_map/ppermute | solution.py:53
  358.6 7.0 %collective-permute-start.1 = (f32[4,5,8,128]{3,2,1,0:T(8,128)S(1)}, f32[4,5,8,128]{3,2,1,0:T(8,128)S(1)}, u32[]{:S(2)}, u32[]{:S(2)}) collective-permute-start(f32[4,5,8,128]{3,2,1,0:T(8,128)S(1)} %broadcast_select_fusion), channel_id=1, source_target_pairs={{24,0},{28,4},{0,8},{4,12},{8,16},{12,20},{16,24},{20,28},{25,1},{... | collective-permute-start | bytes 245768 | tf_op jit(solution)/shard_map/ppermute | solution.py:44
  365.1 1.9 collective-permute-start.14
  365.2 3.7 collective-permute-start.13
  365.8 5.9 %collective-permute-start.2 = (f32[4,5,8,128]{3,2,1,0:T(8,128)S(1)}, f32[4,5,8,128]{3,2,1,0:T(8,128)S(1)}, u32[]{:S(2)}, u32[]{:S(2)}) collective-permute-start(f32[4,5,8,128]{3,2,1,0:T(8,128)S(1)} %broadcast_select_fusion.1), channel_id=1, source_target_pairs={{16,0},{20,4},{24,8},{28,12},{0,16},{4,20},{8,24},{12,28},{17,1},{... | collective-permute-start | bytes 245768 | tf_op jit(solution)/shard_map/ppermute | solution.py:44
  371.9 1.5 collective-permute-start.4
  372.0 3.2 collective-permute-start.3
  377.0 7.1 %collective-permute-start.5 = (f32[5,10,128]{2,1,0:T(8,128)S(1)}, f32[5,10,128]{2,1,0:T(8,128)S(1)}, u32[]{:S(2)}, u32[]{:S(2)}) collective-permute-start(f32[5,10,128]{2,1,0:T(8,128)S(1)} %bitcast.484), channel_id=1, source_target_pairs={{28,0},{0,4},{4,8},{8,12},{12,16},{16,20},{20,24},{24,28},{29,1},{... | collective-permute-start | bytes 76808 | tf_op jit(solution)/shard_map/ppermute | solution.py:44
  380.8 4.6 %collective-permute-start.6 = (f32[5,10,128]{2,1,0:T(8,128)S(1)}, f32[5,10,128]{2,1,0:T(8,128)S(1)}, u32[]{:S(2)}, u32[]{:S(2)}) collective-permute-start(f32[5,10,128]{2,1,0:T(8,128)S(1)} %bitcast.485), channel_id=1, source_target_pairs={{4,0},{8,4},{12,8},{16,12},{20,16},{24,20},{28,24},{0,28},{5,1},{9... | collective-permute-start | bytes 76808 | tf_op jit(solution)/shard_map/ppermute | solution.py:44
  448.3 0.8 copy-start
where the time goes:
time: 451 us; the launch traced here: 449 us
  local copies, waits for them, and re-layouts  288 us (64%)
  other arithmetic  118 us (26%)
  starting transfers between devices  17.5 us (4%)
  waiting for transfers between devices  14.2 us (3%)
  between operations  5.99 us (1%)
  matrix products  5.84 us (1%)
    gather x1, local copies, waits for them, and re-layouts, tile_links(): bounced = leaving - 6.0 * picked[3] * density[link_cell] * c_dot_u  90.5 us
    scatter-add x1, other arithmetic, tile_links(): jax.ops.segment_sum(values.T, sphere_refs, num_segments=9 * slot_count)  90.4 us
    scatter x1, local copies, waits for them, and re-layouts, tile_links(): propagated.reshape(-1).at[target].set(bounced, mode='drop')  60.6 us
    gather x2, local copies, waits for them, and re-layouts, tile_links(): wall_speed = near_speed[:, link_sphere]  59.9 us
    gather x1, local copies, waits for them, and re-layouts, tile_links(): leaving = jnp.sum(onehot * relaxed[:, link_cell], axis=0)  56.6 us
    unnamed x29, other arithmetic  12.6 us
  transfers between devices with their start and end apart: 15, of which 10 were waited for; matrix products, arithmetic and copies ran while one was open for 77% of the time, Pallas kernels for 0%

commit v1 on v0

v1 whole, which is shorter than its diff:
```python
import functools

import jax
import jax.numpy as jnp
from jax import lax
from jax.experimental import pallas as pl
from jax.experimental.pallas import tpu as pltpu
from jax.sharding import PartitionSpec as P

VELOCITIES = [
    (0, 0, 0),
    (1, 0, 0),
    (-1, 0, 0),
    (0, 1, 0),
    (0, -1, 0),
    (0, 0, 1),
    (0, 0, -1),
    (1, 1, 0),
    (-1, -1, 0),
    (1, -1, 0),
    (-1, 1, 0),
    (1, 0, 1),
    (-1, 0, -1),
    (1, 0, -1),
    (-1, 0, 1),
    (0, 1, 1),
    (0, -1, -1),
    (0, 1, -1),
    (0, -1, 1),
]
WEIGHTS = [1.0 / 3.0] + [1.0 / 18.0] * 6 + [1.0 / 36.0] * 12
UPWARD = [3, 7, 10, 15, 17]
DOWNWARD = [4, 8, 9, 16, 18]
RIGHTWARD = [1, 7, 9, 11, 13]
LEFTWARD = [2, 8, 10, 12, 14]
RELAX_TIME = 0.8
SHEAR_SPEED = 0.1
LUB_COEF = 0.5
GAP_FLOOR = 0.1
GAP_CUTOFF = 1.0
INV_MASS = 1.0 / 523.6
LANES = 128
SUBS = 8
NEAR = 9
NO_LINK = 1e30
BF16 = jnp.bfloat16
F32 = jnp.float32
NT = (((1,), (1,)), ((), ()))

VMEM = pl.BlockSpec(memory_space=pltpu.VMEM)
SMEM = pl.BlockSpec(memory_space=pltpu.SMEM)


def collide_kernel(pops, speed, relaxed, density, right_msg, left_msg):
    width_x, width_y = pops.shape[1], pops.shape[2]
    slots = speed.shape[3]
    for x in range(width_x):
        current = [pops[d, x] for d in range(19)]
        total = functools.reduce(lambda p, q: p + q, current)
        density[x] = total
        inverse = 1.0 / total
        speeds = []
        for axis_id in range(3):
            running = None
            for direction, vector in enumerate(VELOCITIES):
                if vector[axis_id] == 0:
                    continue
                if running is None:
                    running = current[direction]
                elif vector[axis_id] > 0:
                    running = running + current[direction]
                else:
                    running = running - current[direction]
            speeds.append(running * inverse)
        base = 1.0 - 1.5 * (
            speeds[0] * speeds[0] + speeds[1] * speeds[1] + speeds[2] * speeds[2]
        )
        for direction, vector in enumerate(VELOCITIES):
            c_dot = None
            for axis_id in range(3):
                if vector[axis_id] != 0:
                    addend = vector[axis_id] * speeds[axis_id]
                    c_dot = addend if c_dot is None else c_dot + addend
            shape = base if c_dot is None else base + c_dot * (3.0 + 4.5 * c_dot)
            equil = WEIGHTS[direction] * total * shape
            value = current[direction] - (current[direction] - equil) * (1.0 / RELAX_TIME)
            relaxed[direction, x] = value
            if x == width_x - 1 and direction in RIGHTWARD:
                right_msg[RIGHTWARD.index(direction)] = value
            if x == 0 and direction in LEFTWARD:
                left_msg[LEFTWARD.index(direction)] = value
            if direction in UPWARD:
                left_msg[5 + UPWARD.index(direction), x : x + 1, :] = value[width_y - 1 :, :]
            if direction in DOWNWARD:
                right_msg[5 + DOWNWARD.index(direction), x : x + 1, :] = value[:1, :]
    right_msg[10] = jnp.zeros((SUBS, LANES), F32)
    left_msg[10] = jnp.zeros((SUBS, LANES), F32)
    for k in range(3):
        row = speed[k, 0]
        twice = jnp.concatenate([row] * (LANES // slots), axis=1)
        right_msg[10, k : k + 1, :] = twice
        left_msg[10, k : k + 1, :] = twice


def prepare_kernel(shift, own_right, own_left, from_left, from_right, up_msg, down_msg, own_speed, rows):
    width_x = own_right.shape[1]
    up_rest, down_rest = shift[0], shift[1]
    top_edge, bottom_edge = shift[2], shift[3]
    for j, direction in enumerate(UPWARD):
        step = VELOCITIES[direction][0]
        boost = 6.0 * WEIGHTS[direction] * step * SHEAR_SPEED
        rows[j, SUBS : 2 * SUBS] = own_left[5 + j]
        rows[j, 2 * SUBS : 3 * SUBS] = from_right[5 + j]
        if step > 0:
            slab = from_left[RIGHTWARD.index(direction)]
            rows[j, SUBS - 1 : SUBS] = slab[SUBS - 1 :, :]
        moved = rows[j, pl.ds(SUBS - step + up_rest, width_x), :]
        if step != 0:
            moved = moved - boost * top_edge.astype(F32)
        up_msg[j] = moved
    for j, direction in enumerate(DOWNWARD):
        step = VELOCITIES[direction][0]
        boost = 6.0 * WEIGHTS[direction] * step * SHEAR_SPEED
        rows[5 + j, :SUBS] = from_left[5 + j]
        rows[5 + j, SUBS : 2 * SUBS] = own_right[5 + j]
        if step < 0:
            slab = from_right[LEFTWARD.index(direction)]
            rows[5 + j, 2 * SUBS : 2 * SUBS + 1] = slab[:1, :]
        moved = rows[5 + j, pl.ds(SUBS - step - down_rest, width_x), :]
        if step != 0:
            moved = moved + boost * bottom_edge.astype(F32)
        down_msg[j] = moved
    three = [from_left[10], own_right[10], from_right[10]]
    for out, first in ((up_msg, 5), (down_msg, 5), (own_speed, 0)):
        for f in range(3):
            for k in range(3):
                row = 3 * f + k
                out[first + row // SUBS, row % SUBS : row % SUBS + 1, :] = three[f][k : k + 1, :]


def to_bf16(value):
    return value.astype(F32).astype(BF16)


def mark_kernel(count, cell, direction, sphere, marks):
    step = pl.program_id(0)
    width = cell.shape[2]
    half_rows = marks.shape[0]
    q = cell[0]
    ref = sphere[0]
    row = (direction[0] - 1) * (2 * half_rows // 18) + q // LANES
    z = q % LANES
    half = (row >= half_rows).astype(jnp.int32)
    row = row - half * half_rows
    number = step * width + lax.broadcasted_iota(jnp.int32, (1, width), 1)
    level = ref // LANES
    scale = jnp.where(level == 0, 1.0, 0.0)
    for t in range(1, 5):
        scale = jnp.where(level == t, 2.0 ** (8 * t), scale)
    code = jnp.where(number < count[0, 0], (LANES + ref % LANES).astype(F32) * scale, 0.0)
    block = half_rows // 3
    parts = []
    for first in range(0, half_rows, block):
        local = row - first
        local = to_bf16(jnp.where((local >= 0) & (local < block), local, 255))
        index = to_bf16(lax.broadcasted_iota(jnp.int32, (block, width), 0))
        parts.append(
            jnp.where(
                index == jnp.broadcast_to(local, (block, width)), jnp.ones((), BF16), jnp.zeros((), BF16)
            )
        )
    rows_hot = jnp.concatenate(parts, axis=0)
    column = to_bf16(z + LANES * half)
    index = to_bf16(lax.broadcasted_iota(jnp.int32, (2 * LANES, width), 0))
    columns = jnp.where(
        index == jnp.broadcast_to(column, (2 * LANES, width)),
        jnp.broadcast_to(code.astype(BF16), (2 * LANES, width)),
        jnp.zeros((), BF16),
    )
    part = lax.dot_general(rows_hot, columns, NT, preferred_element_type=F32)

    @pl.when(step == 0)
    def _():
        marks[...] = part

    @pl.when(step > 0)
    def _():
        marks[...] += part


def split(value):
    high = value.astype(BF16)
    return high, (value - high.astype(F32)).astype(BF16)


def force_kernel(
    pair_count,
    relaxed,
    density,
    marks,
    own_speed,
    below_speed,
    above_speed,
    pair_first,
    pair_second,
    pair_gap,
    pair_normal,
    bounced,
    parts,
    link_table,
    first_of,
    second_of,
    value_of,
    sums,
):
    width_x = relaxed.shape[1]
    slots = LANES // 2
    half_rows = marks.shape[0]
    lane = lax.broadcasted_iota(jnp.int32, (1, LANES), 1)
    sources = [below_speed, own_speed, above_speed]

    def speed_row(code, k):
        row = 3 * (code // 3) + k
        source = sources[code % 3]
        first = 0 if source is own_speed else 5
        return source[first + row // SUBS, row % SUBS : row % SUBS + 1, :]

    tables = []
    for k in range(3):
        rows = []
        for t in range(5):
            low = speed_row(2 * t, k)
            high = speed_row(min(2 * t + 1, NEAR - 1), k)
            rows.append(jnp.where(lane < slots, low, high))
        tables.append(rows)
    for direction in range(1, 19):
        for t in range(5):
            total = None
            for k in range(3):
                if VELOCITIES[direction][k] != 0:
                    addend = VELOCITIES[direction][k] * tables[k][t]
                    total = addend if total is None else total + addend
            link_table[direction - 1, t : t + 1, :] = total

    index_a = to_bf16(lax.broadcasted_iota(jnp.int32, (48, LANES), 0))
    index_b = to_bf16(lax.broadcasted_iota(jnp.int32, (16, LANES), 0))
    one = jnp.ones((), BF16)
    zero = jnp.zeros((), BF16)

    def hot_rows(first_row, second_row, values):
        a = jnp.broadcast_to(to_bf16(first_row), (48, LANES))
        b = jnp.broadcast_to(to_bf16(second_row), (16, LANES))
        left = jnp.where(index_a == a, one, zero)
        mask = index_b == b
        right = []
        for value in values:
            high, low = split(value)
            right.append(
                jnp.concatenate(
                    [
                        jnp.where(mask, jnp.broadcast_to(high, (16, LANES)), zero),
                        jnp.where(mask, jnp.broadcast_to(low, (16, LANES)), zero),
                    ],
                    axis=0,
                )
            )
        return left, right

    def group(g, carry):
        for side in range(2):
            index = 2 * g + side
            half = index // 9
            first_row = (index - 9 * half) * (2 * half_rows // 18)
            weight6 = jnp.where(index < 6, 6.0 * WEIGHTS[1], 6.0 * WEIGHTS[7]).astype(F32)
            lookup = [
                jnp.broadcast_to(link_table[index, t : t + 1, :], (SUBS, LANES)) for t in range(5)
            ]
            for x in range(width_x):
                mark = marks[
                    pl.ds(pl.multiple_of(first_row + SUBS * x, SUBS), SUBS),
                    pl.ds(pl.multiple_of(half * LANES, LANES), LANES),
                ]
                live = mark > 0.0
                scaled = mark
                level = jnp.zeros((SUBS, LANES), F32)
                for t in range(1, 5):
                    above = mark > 2.0 ** (8 * t + 6)
                    scaled = jnp.where(above, mark * 2.0 ** (-8 * t), scaled)
                    level = jnp.where(above, float(t), level)
                place = jnp.where(live, scaled - float(LANES), 0.0).astype(jnp.int32)
                speed = jnp.take_along_axis(lookup[0], place, axis=1)
                for t in range(1, 5):
                    found = jnp.take_along_axis(lookup[t], place, axis=1)
                    speed = jnp.where(level == float(t), found, speed)
                leaving = relaxed[index + 1, x]
                back = leaving - weight6 * density[x] * speed
                bounced[index, x] = jnp.where(live, back, NO_LINK)
                force = leaving + back
                if side == 1:
                    force = -force
                high_part = place // 16
                first = jnp.where(live, level * 8.0 + high_part.astype(F32), -1.0)
                second = (place - 16 * high_part).astype(F32)
                where = side * width_x * SUBS + SUBS * x
                first_of[where : where + SUBS] = first
                second_of[where : where + SUBS] = second
                value_of[where : where + SUBS] = jnp.where(live, force, 0.0)
        lefts, rights = [], []
        for r in range(2 * width_x * SUBS):
            left, right = hot_rows(
                first_of[r : r + 1], second_of[r : r + 1], [value_of[r : r + 1]]
            )
            lefts.append(left)
            rights.append(right[0])
        sums[g] = lax.dot_general(
            jnp.concatenate(lefts, axis=1),
            jnp.concatenate(rights, axis=1),
            NT,
            preferred_element_type=F32,
        )
        return carry

    lax.fori_loop(0, 9, group, 0)

    totals = []
    for k in range(3):
        total = None
        for g in range(9):
            c = VELOCITIES[2 * g + 1][k]
            if c == 0:
                continue
            if total is None:
                total = sums[g] if c > 0 else -sums[g]
            else:
                total = total + sums[g] if c > 0 else total - sums[g]
        totals.append(total)

    pairs = pair_first.shape[2]
    lefts = []
    rights = [[], [], []]
    for start in range(0, pairs, LANES):
        here = slice(start, start + LANES)
        first = pair_first[0, :, here]
        second = pair_second[0, :, here]
        first_wide = jnp.broadcast_to(first, (SUBS, LANES))
        place = jnp.broadcast_to(second % LANES, (SUBS, LANES))
        level = second // LANES
        gap = pair_gap[0, :, here]
        rate = None
        for k in range(3):
            table = jnp.broadcast_to(tables[k][2], (SUBS, LANES))
            first_speed = jnp.take_along_axis(table, first_wide, axis=1)[:1]
            second_speed = None
            for t in range(5):
                table = jnp.broadcast_to(tables[k][t], (SUBS, LANES))
                found = jnp.take_along_axis(table, place, axis=1)[:1]
                second_speed = found if t == 0 else jnp.where(level == t, found, second_speed)
            addend = (first_speed - second_speed) * pair_normal[k, 0, :, here]
            rate = addend if rate is None else rate + addend
        resist = LUB_COEF * (1.0 / jnp.maximum(gap, GAP_FLOOR) - 1.0 / GAP_CUTOFF)
        number = start + lane
        factor = jnp.where(number < pair_count[0, 0], -resist * rate, 0.0)
        values = [factor * pair_normal[k, 0, :, here] for k in range(3)]
        first = first + 4 * slots
        for ref, these in ((first, values), (second, [-v for v in values])):
            left, right = hot_rows(ref // 16, ref % 16, these)
            lefts.append(left)
            for k in range(3):
                rights[k].append(right[k])
    left = jnp.concatenate(lefts, axis=1)
    for k in range(3):
        total = totals[k] + lax.dot_general(
            left, jnp.concatenate(rights[k], axis=1), NT, preferred_element_type=F32
        )
        value = total[:, :16] + total[:, 16:32]
        first_of[0:48] = jnp.concatenate([value, jnp.zeros((48, LANES - 16), F32)], axis=1)
        line = None
        for s in range(4):
            piece = first_of[pl.ds(s, NEAR, stride=4), :]
            if s:
                piece = pltpu.roll(piece, 16 * s, axis=1)
            line = piece if line is None else line + piece
        for code in range(NEAR):
            row = 3 * (code % 3) + k
            parts[code // 3, row : row + 1, :] = line[code : code + 1]


def stream_kernel(relaxed, bounced, from_left, from_right, below, above, out):
    width_x, width_y = relaxed.shape[1], relaxed.shape[2]
    for direction, (cx, cy, cz) in enumerate(VELOCITIES):
        for x in range(width_x):
            source = x - cx
            if source < 0:
                tile = from_left[RIGHTWARD.index(direction)]
            elif source >= width_x:
                tile = from_right[LEFTWARD.index(direction)]
            else:
                tile = relaxed[direction, source]
            if cy != 0:
                tile = pltpu.roll(tile, cy % width_y, axis=0)
                row = lax.broadcasted_iota(jnp.int32, tile.shape, 0)
                if cy > 0:
                    ghost = below[UPWARD.index(direction), x : x + 1, :]
                    tile = jnp.where(row == 0, jnp.broadcast_to(ghost, tile.shape), tile)
                else:
                    ghost = above[DOWNWARD.index(direction), x : x + 1, :]
                    tile = jnp.where(row == width_y - 1, jnp.broadcast_to(ghost, tile.shape), tile)
            if cz != 0:
                tile = pltpu.roll(tile, cz % LANES, axis=1)
            if direction > 0:
                opposite = direction + 1 if direction % 2 == 1 else direction - 1
                back = bounced[opposite - 1, x]
                tile = jnp.where(back < 0.5 * NO_LINK, back, tile)
            out[direction, x] = tile


def send(block, axis, distance):
    count = lax.axis_size(axis)
    return lax.ppermute(block, axis, [(i, (i + distance) % count) for i in range(count)])


def shape_of(*dims):
    return jax.ShapeDtypeStruct(dims, F32)


def per_device(
    populations,
    le_offset,
    sphere_velocity,
    link_cell,
    link_dir,
    link_sphere,
    link_count,
    pair_first,
    pair_second,
    pair_count,
    pair_gap,
    pair_normal,
):
    width_x, width_y, depth = populations.shape[1:]
    slots = sphere_velocity.shape[3]
    links = link_cell.shape[2]
    flow_count = lax.axis_size("flow")
    grad_count = lax.axis_size("grad")
    grad_index = lax.axis_index("grad")
    assert depth == LANES and width_y == SUBS and width_x == SUBS and 2 * slots == LANES

    relaxed, density, right_msg, left_msg = pl.pallas_call(
        collide_kernel,
        name="collide",
        in_specs=[VMEM, VMEM],
        out_specs=[VMEM] * 4,
        out_shape=[
            shape_of(19, width_x, width_y, depth),
            shape_of(width_x, width_y, depth),
            shape_of(11, SUBS, LANES),
            shape_of(11, SUBS, LANES),
        ],
    )(populations, sphere_velocity)

    from_left = send(right_msg, "flow", 1)
    from_right = send(left_msg, "flow", -1)

    half_rows = 9 * width_x * width_y
    width = links // 4
    link_spec = pl.BlockSpec((1, 1, width), lambda i: (0, 0, i))
    marks = pl.pallas_call(
        mark_kernel,
        name="mark",
        grid=(links // width,),
        in_specs=[SMEM, link_spec, link_spec, link_spec],
        out_specs=pl.BlockSpec((half_rows, 2 * LANES), lambda i: (0, 0)),
        out_shape=shape_of(half_rows, 2 * LANES),
    )(link_count, link_cell, link_dir, link_sphere)

    offset = le_offset[0]
    rest = offset % width_x
    at_top = (grad_index == grad_count - 1).astype(jnp.int32)
    at_bottom = (grad_index == 0).astype(jnp.int32)
    shift = jnp.stack([rest * at_top, rest * at_bottom, at_top, at_bottom])
    up_msg, down_msg, own_speed = pl.pallas_call(
        prepare_kernel,
        name="prepare",
        in_specs=[SMEM] + [VMEM] * 4,
        out_specs=[VMEM] * 3,
        out_shape=[shape_of(7, SUBS, LANES), shape_of(7, SUBS, LANES), shape_of(2, SUBS, LANES)],
        scratch_shapes=[pltpu.VMEM((10, 3 * SUBS, LANES), F32)],
    )(shift, right_msg, left_msg, from_left, from_right)

    below = send(up_msg, "grad", 1)
    above = send(down_msg, "grad", -1)

    hops = offset // width_x
    edge = jnp.where(at_bottom == 1, below[:5], above[:5])
    for level in range(max(flow_count - 1, 1).bit_length()):
        route = []
        for a in range(flow_count):
            far = 1 << level
            route.append((a * grad_count, (a - far) % flow_count * grad_count))
            route.append(
                (a * grad_count + grad_count - 1, (a + far) % flow_count * grad_count + grad_count - 1)
            )
        arrived = lax.ppermute(edge, ("flow", "grad"), route)
        edge = jnp.where(hops // (1 << level) % 2 == 1, arrived, edge)
    below_rows = jnp.where(at_bottom == 1, edge, below[:5])
    above_rows = jnp.where(at_top == 1, edge, above[:5])

    bounced, parts = pl.pallas_call(
        force_kernel,
        name="force",
        in_specs=[SMEM] + [VMEM] * 10,
        out_specs=[VMEM] * 2,
        out_shape=[shape_of(18, width_x, width_y, depth), shape_of(3, 2 * SUBS, LANES)],
        scratch_shapes=[
            pltpu.VMEM((18, SUBS, LANES), F32),
            pltpu.VMEM((2 * width_x * SUBS, LANES), F32),
            pltpu.VMEM((2 * width_x * SUBS, LANES), F32),
            pltpu.VMEM((2 * width_x * SUBS, LANES), F32),
            pltpu.VMEM((9, 48, 32), F32),
        ],
    )(
        pair_count,
        relaxed,
        density,
        marks,
        own_speed,
        below,
        above,
        pair_first,
        pair_second,
        pair_gap,
        pair_normal,
    )

    column = parts[1] + send(parts[0], "flow", -1) + send(parts[2], "flow", 1)
    column = column[:9].reshape(3, 3, LANES)
    own_force = column[1] + send(column[0], "grad", -1) + send(column[2], "grad", 1)
    sphere_force = own_force[:, None, None, :slots]
    velocity_next = sphere_velocity + INV_MASS * sphere_force

    updated = pl.pallas_call(
        stream_kernel,
        name="stream",
        in_specs=[VMEM] * 6,
        out_specs=VMEM,
        out_shape=shape_of(19, width_x, width_y, depth),
    )(relaxed, bounced, from_left, from_right, below_rows, above_rows)
    return updated, sphere_force, velocity_next


def solution(mesh):
    in_specs = (
        P(None, "flow", "grad", None),
        P(),
        P(None, "flow", "grad", None),
        P("flow", "grad", None),
        P("flow", "grad", None),
        P("flow", "grad", None),
        P("flow", "grad"),
        P("flow", "grad", None),
        P("flow", "grad", None),
        P("flow", "grad"),
        P("flow", "grad", None),
        P(None, "flow", "grad", None),
    )
    out_specs = (
        P(None, "flow", "grad", None),
        P(None, "flow", "grad", None),
        P(None, "flow", "grad", None),
    )
    return jax.shard_map(
        per_device, mesh=mesh, in_specs=in_specs, out_specs=out_specs, check_vma=False
    )
```

time: 451 us -> 67.6 us (0.15)
  local copies, waits for them, and re-layouts: 288 us -> 3.68 us
  other arithmetic: 118 us -> 1.99 us
  Pallas kernels: 0 us -> 22.4 us
  matrix products: 5.84 us -> 0 us
    gather x13 -> x0, local copies, waits for them, and re-layouts: 212 us -> none  [the longest x1 90.5 us: tile_links(): bounced = leaving - 6.0 * picked[3] * density[link_cell] * c_dot_u]
    scatter-add x1 -> x0, other arithmetic: 90.4 us -> none  [tile_links(): jax.ops.segment_sum(values.T, sphere_refs, num_segments=9 * slot_count)]
    scatter x5 -> x0, local copies, waits for them, and re-layouts: 63.4 us -> none  [the longest x1 60.6 us: tile_links(): propagated.reshape(-1).at[target].set(bounced, mode='drop')]
    pallas_call x0 -> x5, Pallas kernels: none -> 22.4 us  [the longest x1 8.79 us: per_device(): pl.pallas_call(force_kernel, name='force', in_specs=[SMEM] + [VMEM] * 10,...]
    unnamed x29 -> x0, other arithmetic: 12.6 us -> none
    reduce_sum x5 -> x0, other arithmetic: 9.72 us -> none  [the longest x1 8.37 us: tile_links(): leaving = jnp.sum(onehot * relaxed[:, link_cell], axis=0)]
    dot_general x1 -> x0, matrix products: 5.84 us -> none  [tile_links(): picked = jnp.dot(lookup, onehot, precision=lax.Precision.HIGHEST)]
    transpose x2 -> x0, local copies, waits for them, and re-layouts: 4.96 us -> none  [the longest x1 4.93 us: tile_links(): partial_value = jax.ops.segment_sum(values.T, sphere_refs, num_segments=9...]
  transfers between devices with their start and end apart: 15 -> 11, of which waited for: 10 -> 7; matrix products, arithmetic and copies ran while one was open for 77% -> 3% of each run, Pallas kernels for 0% -> 11%
where the time goes in v1:
time: 67.6 us; the launch traced here: 67.1 us
  Pallas kernels  22.4 us (33%)
  waiting for transfers between devices  18.2 us (27%)
  starting transfers between devices  18.1 us (27%)
  local copies, waits for them, and re-layouts  3.68 us (5%)
  between operations  2.7 us (4%)
  other arithmetic  1.99 us (3%)
    ppermute x8, starting transfers between devices, send(): lax.ppermute(block, axis, [(i, (i + distance) % count) for i in range(cou...  12.4 us
    ppermute x3, waiting for transfers between devices, per_device(): arrived = lax.ppermute(edge, ('flow', 'grad'), route)  10.3 us
    pallas_call x1, Pallas kernels, per_device(): pl.pallas_call(force_kernel, name='force', in_specs=[SMEM] + [VMEM] * 10,...  8.79 us
    ppermute x8, waiting for transfers between devices, send(): lax.ppermute(block, axis, [(i, (i + distance) % count) for i in range(cou...  7.88 us
    pallas_call x1, Pallas kernels, per_device(): pl.pallas_call(mark_kernel, name='mark', grid=(links // width,), in_specs...  7.6 us
    ppermute x3, starting transfers between devices, per_device(): arrived = lax.ppermute(edge, ('flow', 'grad'), route)  5.74 us
    unnamed x16, local copies, waits for them, and re-layouts  2.96 us
    pallas_call x1, Pallas kernels, per_device(): pl.pallas_call(stream_kernel, name='stream', in_specs=[VMEM] * 6, out_spe...  2.26 us
  transfers between devices with their start and end apart: 11, of which 7 were waited for; matrix products, arithmetic and copies ran while one was open for 3% of the time, Pallas kernels for 11%

profile of v1, /device:TPU:0, one launch (start us, length us, event | category | flops | bytes accessed | tf_op | source)
XLA Modules:
  0.0 67.1 jit_solution(10268325460312907932)
XLA Ops:
  0.6 2.2 %collide.1 = (f32[19,8,8,128]{3,2,1,0:T(8,128)}, f32[8,8,128]{2,1,0:T(8,128)}, f32[11,8,128]{2,1,0:T(8,128)}, f32[11,8,128]{2,1,0:T(8,128)}) custom-call(f32[19,8,8,128]{3,2,1,0:T(8,128)} %pops.1, f32[3,1,1,64]{3,2,1,0:T(1,128)} %speed.1), custom_call_target="tpu_custom_call" | custom-call | tf_op jit(solution)/shard_map/collide/pallas_call | solution.py:448
  2.8 3.0 %collective-permute-start = (f32[11,8,128]{2,1,0:T(8,128)}, f32[11,8,128]{2,1,0:T(8,128)S(1)}, u32[]{:S(2)}, u32[]{:S(2)}) collective-permute-start(f32[11,8,128]{2,1,0:T(8,128)} %get-tuple-element.14.own_right), channel_id=1, source_target_pairs={{0,4},{4,8},{8,12},{12,16},{16,20},{20,24},{24,28},{28,0},{1,5},{5... | collective-permute-start | bytes 135176 | tf_op jit(solution)/shard_map/ppermute | solution.py:419
  5.8 3.0 %collective-permute-start.1 = (f32[11,8,128]{2,1,0:T(8,128)}, f32[11,8,128]{2,1,0:T(8,128)S(1)}, u32[]{:S(2)}, u32[]{:S(2)}) collective-permute-start(f32[11,8,128]{2,1,0:T(8,128)} %get-tuple-element.15.own_left), channel_id=1, source_target_pairs={{0,28},{4,0},{8,4},{12,8},{16,12},{20,16},{24,20},{28,24},{1,29},{... | collective-permute-start | bytes 135176 | tf_op jit(solution)/shard_map/ppermute | solution.py:419
  9.5 0.7 pad_add_fusion.shift
  10.2 0.9 %collective-permute-done.from_left = f32[11,8,128]{2,1,0:T(8,128)S(1)} collective-permute-done((f32[11,8,128]{2,1,0:T(8,128)}, f32[11,8,128]{2,1,0:T(8,128)S(1)}, u32[]{:S(2)}, u32[]{:S(2)}) %collective-permute-start) | collective-permute-done | bytes 45088 | tf_op jit(solution)/shard_map/ppermute | solution.py:419
  11.1 0.0 copy-start
  11.1 0.0 collective-permute-done.1.from_right
  11.1 0.6 copy-done
  11.7 0.0 copy-start.1
  11.7 0.6 copy-done.1
  12.3 1.5 %prepare.1 = (f32[7,8,128]{2,1,0:T(8,128)}, f32[7,8,128]{2,1,0:T(8,128)}, f32[2,8,128]{2,1,0:T(8,128)}) custom-call(s32[4]{0:T(128)} %pad_add_fusion.shift, f32[11,8,128]{2,1,0:T(8,128)} %get-tuple-element.14.own_right, f32[11,8,128]{2,1,0:T(8,128)} %get-tuple-element.15.own_left, f32[11,8,128]{2,1,0:T(8,128)} %copy-done, f32[11,8,128]{2,1,0:T(8,128)} %copy-done.1), custom_call_target="tpu_custom_call" | custom-call | tf_op jit(solution)/shard_map/prepare/pallas_call | solution.py:481
  13.9 0.0 collective-permute-start.2
  13.9 1.7 %collective-permute-start.3 = (f32[7,8,128]{2,1,0:T(8,128)}, f32[7,8,128]{2,1,0:T(8,128)S(1)}, u32[]{:S(2)}, u32[]{:S(2)}) collective-permute-start(f32[7,8,128]{2,1,0:T(8,128)} %get-tuple-element.18), channel_id=1, source_target_pairs={{0,3},{1,0},{2,1},{3,2},{4,7},{5,4},{6,5},{7,6},{8,11},{9,8},{10,9... | collective-permute-start | bytes 86024 | tf_op jit(solution)/shard_map/ppermute | solution.py:419
  16.9 7.6 %mark.1.marks = f32[576,256]{1,0:T(8,128)} custom-call(s32[1,1]{1,0:T(1,128)S(6)} %copy.20.count, s32[1,1,16384]{2,1,0:T(1,128)} %cell.1, s32[1,1,16384]{2,1,0:T(1,128)} %direction.1, s32[1,1,16384]{2,1,0:T(1,128)} %sphere.1), custom_call_target="tpu_custom_call" | custom-call | tf_op jit(solution)/shard_map/mark/pallas_call | solution.py:467
  24.5 0.0 collective-permute-done.2.below_speed
  24.5 0.0 copy-start.2
  24.5 0.0 collective-permute-done.3.above_speed
  24.5 0.0 copy-start.4
  24.5 0.6 copy-done.2
  25.1 0.0 copy-done.4
  25.1 8.8 %force.1 = (f32[18,8,8,128]{3,2,1,0:T(8,128)}, f32[3,16,128]{2,1,0:T(8,128)}) custom-call(s32[1,1]{1,0:T(1,128)S(6)} %copy.21.pair_count, f32[19,8,8,128]{3,2,1,0:T(8,128)} %get-tuple-element.12.relaxed, f32[8,8,128]{2,1,0:T(8,128)} %get-tuple-element.13.density, f32[576,256]{1,0:T(8,128)} %mark.1.marks, f32[2,8,128]{2,1,0:T(8,128)} %get-tuple-element.16.own_speed, ...), custom_call_target="tpu_custom_call" | custom-call | tf_op jit(solution)/shard_map/force/pallas_call | solution.py:508
  33.9 0.7 %slice_bitcast_fusion.1 = (f32[16,128]{1,0:T(8,128)S(1)}, f32[16,128]{1,0:T(8,128)S(1)}) fusion(f32[3,16,128]{2,1,0:T(8,128)} %get-tuple-element.20), kind=kLoop, calls=%fused_computation.9 | loop fusion | bytes 32768 | tf_op jit(solution)/shard_map/squeeze | solution.py:535
  34.6 4.1 %collective-permute-start.7 = (f32[16,128]{1,0:T(8,128)S(1)}, f32[16,128]{1,0:T(8,128)S(1)}, u32[]{:S(2)}, u32[]{:S(2)}) collective-permute-start(f32[16,128]{1,0:T(8,128)S(1)} %get-tuple-element.26), channel_id=1, source_target_pairs={{0,28},{4,0},{8,4},{12,8},{16,12},{20,16},{24,20},{28,24},{1,29},{... | collective-permute-start | bytes 24584 | tf_op jit(solution)/shard_map/ppermute | solution.py:419
  38.7 0.0 collective-permute-start.8
  38.7 0.0 copy-start.5
  38.7 0.0 copy-start.3
  38.7 1.4 %collective-permute-done.7 = f32[16,128]{1,0:T(8,128)S(1)} collective-permute-done((f32[16,128]{1,0:T(8,128)S(1)}, f32[16,128]{1,0:T(8,128)S(1)}, u32[]{:S(2)}, u32[]{:S(2)}) %collective-permute-start.7) | collective-permute-done | bytes 8224 | tf_op jit(solution)/shard_map/ppermute | solution.py:419
  40.1 5.0 %collective-permute-done.8 = f32[16,128]{1,0:T(8,128)S(1)} collective-permute-done((f32[16,128]{1,0:T(8,128)S(1)}, f32[16,128]{1,0:T(8,128)S(1)}, u32[]{:S(2)}, u32[]{:S(2)}) %collective-permute-start.8) | collective-permute-done | bytes 8224 | tf_op jit(solution)/shard_map/ppermute | solution.py:419
  45.1 0.7 %fusion = f32[16,128]{1,0:T(8,128)S(1)} fusion(f32[16,128]{1,0:T(8,128)S(1)} %collective-permute-done.8, f32[16,128]{1,0:T(8,128)S(1)} %collective-permute-done.7, f32[3,16,128]{2,1,0:T(8,128)} %get-tuple-element.20), kind=kLoop, calls=%fused_computation.7 | loop fusion | flops 4096 | bytes 32768 | tf_op jit(solution)/shard_map/add | solution.py:535
  45.8 0.0 collective-permute-start.9
  45.8 0.5 collective-permute-start.10
  46.3 0.0 copy-done.5
  46.3 0.0 copy-done.3
  46.3 1.9 %collective-permute-start.4 = (f32[5,8,128]{2,1,0:T(8,128)S(1)}, f32[5,8,128]{2,1,0:T(8,128)S(1)}, u32[]{:S(2)}, u32[]{:S(2)}) collective-permute-start(f32[5,8,128]{2,1,0:T(8,128)S(1)} %slice_select_fusion.1), channel_id=1, source_target_pairs={{0,28},{3,7},{4,0},{7,11},{8,4},{11,15},{12,8},{15,19},{16,12},{19... | collective-permute-start | bytes 61448 | tf_op jit(solution)/shard_map/ppermute | solution.py:503
  48.2 0.0 collective-permute-done.9
  48.2 0.6 collective-permute-done.10
  48.9 0.0 copy-start.6
  48.9 3.1 %collective-permute-done.4 = f32[5,8,128]{2,1,0:T(8,128)S(1)} collective-permute-done((f32[5,8,128]{2,1,0:T(8,128)S(1)}, f32[5,8,128]{2,1,0:T(8,128)S(1)}, u32[]{:S(2)}, u32[]{:S(2)}) %collective-permute-start.4) | collective-permute-done | bytes 20512 | tf_op jit(solution)/shard_map/ppermute | solution.py:503
  52.0 1.9 %collective-permute-start.5 = (f32[5,8,128]{2,1,0:T(8,128)S(1)}, f32[5,8,128]{2,1,0:T(8,128)S(1)}, u32[]{:S(2)}, u32[]{:S(2)}) collective-permute-start(f32[5,8,128]{2,1,0:T(8,128)S(1)} %broadcast_select_fusion), channel_id=1, source_target_pairs={{0,24},{3,11},{4,28},{7,15},{8,0},{11,19},{12,4},{15,23},{16,8},{1... | collective-permute-start | bytes 61448 | tf_op jit(solution)/shard_map/ppermute | solution.py:503
  53.9 0.0 copy-done.6
  53.9 3.7 %collective-permute-done.5 = f32[5,8,128]{2,1,0:T(8,128)S(1)} collective-permute-done((f32[5,8,128]{2,1,0:T(8,128)S(1)}, f32[5,8,128]{2,1,0:T(8,128)S(1)}, u32[]{:S(2)}, u32[]{:S(2)}) %collective-permute-start.5) | collective-permute-done | bytes 20512 | tf_op jit(solution)/shard_map/ppermute | solution.py:503
  57.7 1.9 %collective-permute-start.6 = (f32[5,8,128]{2,1,0:T(8,128)S(1)}, f32[5,8,128]{2,1,0:T(8,128)S(1)}, u32[]{:S(2)}, u32[]{:S(2)}) collective-permute-start(f32[5,8,128]{2,1,0:T(8,128)S(1)} %broadcast_select_fusion.1), channel_id=1, source_target_pairs={{0,16},{3,19},{4,20},{7,23},{8,24},{11,27},{12,28},{15,31},{16,0},... | collective-permute-start | bytes 61448 | tf_op jit(solution)/shard_map/ppermute | solution.py:503
  59.6 0.6 copy.17
  60.2 0.6 copy.16
  60.7 3.5 %collective-permute-done.6 = f32[5,8,128]{2,1,0:T(8,128)S(1)} collective-permute-done((f32[5,8,128]{2,1,0:T(8,128)S(1)}, f32[5,8,128]{2,1,0:T(8,128)S(1)}, u32[]{:S(2)}, u32[]{:S(2)}) %collective-permute-start.6) | collective-permute-done | bytes 20512 | tf_op jit(solution)/shard_map/ppermute | solution.py:503
  64.2 0.6 slice_select_fusion
  64.8 2.3 %stream.1 = f32[19,8,8,128]{3,2,1,0:T(8,128)} custom-call(f32[19,8,8,128]{3,2,1,0:T(8,128)} %get-tuple-element.12.relaxed, f32[18,8,8,128]{3,2,1,0:T(8,128)} %get-tuple-element.19.bounced, f32[11,8,128]{2,1,0:T(8,128)} %copy-done, f32[11,8,128]{2,1,0:T(8,128)} %copy-done.1, f32[5,8,128]{2,1,0:T(8,128)} %get-tuple-element.25.below, ...), custom_call_target="tpu_custom_call" | custom-call | tf_op jit(solution)/shard_map/stream/pallas_call | solution.py:541
  (7 shorter events, 0.0 us)
Async XLA Ops:
  2.8 8.2 %collective-permute-start = (f32[11,8,128]{2,1,0:T(8,128)}, f32[11,8,128]{2,1,0:T(8,128)S(1)}, u32[]{:S(2)}, u32[]{:S(2)}) collective-permute-start(f32[11,8,128]{2,1,0:T(8,128)} %get-tuple-element.14.own_right), channel_id=1, source_target_pairs={{0,4},{4,8},{8,12},{12,16},{16,20},{20,24},{24,28},{28,0},{1,5},{5... | collective-permute-start | bytes 135176 | tf_op jit(solution)/shard_map/ppermute | solution.py:419
  5.8 5.3 %collective-permute-start.1 = (f32[11,8,128]{2,1,0:T(8,128)}, f32[11,8,128]{2,1,0:T(8,128)S(1)}, u32[]{:S(2)}, u32[]{:S(2)}) collective-permute-start(f32[11,8,128]{2,1,0:T(8,128)} %get-tuple-element.15.own_left), channel_id=1, source_target_pairs={{0,28},{4,0},{8,4},{12,8},{16,12},{20,16},{24,20},{28,24},{1,29},{... | collective-permute-start | bytes 135176 | tf_op jit(solution)/shard_map/ppermute | solution.py:419
  11.1 0.6 copy-start
  11.7 0.6 copy-start.1
  13.9 10.6 %collective-permute-start.2 = (f32[7,8,128]{2,1,0:T(8,128)}, f32[7,8,128]{2,1,0:T(8,128)S(1)}, u32[]{:S(2)}, u32[]{:S(2)}) collective-permute-start(f32[7,8,128]{2,1,0:T(8,128)} %get-tuple-element.17), channel_id=1, source_target_pairs={{0,1},{1,2},{2,3},{3,0},{4,5},{5,6},{6,7},{7,4},{8,9},{9,10},{10,1... | collective-permute-start | bytes 86024 | tf_op jit(solution)/shard_map/ppermute | solution.py:419
  13.9 10.6 %collective-permute-start.3 = (f32[7,8,128]{2,1,0:T(8,128)}, f32[7,8,128]{2,1,0:T(8,128)S(1)}, u32[]{:S(2)}, u32[]{:S(2)}) collective-permute-start(f32[7,8,128]{2,1,0:T(8,128)} %get-tuple-element.18), channel_id=1, source_target_pairs={{0,3},{1,0},{2,1},{3,2},{4,7},{5,4},{6,5},{7,6},{8,11},{9,8},{10,9... | collective-permute-start | bytes 86024 | tf_op jit(solution)/shard_map/ppermute | solution.py:419
  24.5 0.6 copy-start.2
  24.5 0.6 copy-start.4
  34.6 5.5 %collective-permute-start.7 = (f32[16,128]{1,0:T(8,128)S(1)}, f32[16,128]{1,0:T(8,128)S(1)}, u32[]{:S(2)}, u32[]{:S(2)}) collective-permute-start(f32[16,128]{1,0:T(8,128)S(1)} %get-tuple-element.26), channel_id=1, source_target_pairs={{0,28},{4,0},{8,4},{12,8},{16,12},{20,16},{24,20},{28,24},{1,29},{... | collective-permute-start | bytes 24584 | tf_op jit(solution)/shard_map/ppermute | solution.py:419
  38.7 6.3 %collective-permute-start.8 = (f32[16,128]{1,0:T(8,128)S(1)}, f32[16,128]{1,0:T(8,128)S(1)}, u32[]{:S(2)}, u32[]{:S(2)}) collective-permute-start(f32[16,128]{1,0:T(8,128)S(1)} %get-tuple-element.27), channel_id=1, source_target_pairs={{0,4},{4,8},{8,12},{12,16},{16,20},{20,24},{24,28},{28,0},{1,5},{5... | collective-permute-start | bytes 24584 | tf_op jit(solution)/shard_map/ppermute | solution.py:419
  38.7 7.6 %copy-start.5 = (f32[7,8,128]{2,1,0:T(8,128)S(1)}, f32[7,8,128]{2,1,0:T(8,128)}, u32[]{:S(2)}) copy-start(f32[7,8,128]{2,1,0:T(8,128)} %copy-done.4) | copy-start | bytes 86020
  38.7 7.6 %copy-start.3 = (f32[7,8,128]{2,1,0:T(8,128)S(1)}, f32[7,8,128]{2,1,0:T(8,128)}, u32[]{:S(2)}) copy-start(f32[7,8,128]{2,1,0:T(8,128)} %copy-done.2) | copy-start | bytes 86020
  45.8 2.5 %collective-permute-start.9 = (f32[3,128]{1,0:T(4,128)S(1)}, f32[3,128]{1,0:T(4,128)S(1)}, u32[]{:S(2)}, u32[]{:S(2)}) collective-permute-start(f32[3,128]{1,0:T(4,128)S(1)} %get-tuple-element.28), channel_id=1, source_target_pairs={{0,3},{1,0},{2,1},{3,2},{4,7},{5,4},{6,5},{7,6},{8,11},{9,8},{10,9... | collective-permute-start | bytes 4616 | tf_op jit(solution)/shard_map/ppermute | solution.py:419
  45.8 3.1 %collective-permute-start.10 = (f32[3,128]{1,0:T(4,128)S(1)}, f32[3,128]{1,0:T(4,128)S(1)}, u32[]{:S(2)}, u32[]{:S(2)}) collective-permute-start(f32[3,128]{1,0:T(4,128)S(1)} %get-tuple-element.29), channel_id=1, source_target_pairs={{0,1},{1,2},{2,3},{3,0},{4,5},{5,6},{6,7},{7,4},{8,9},{9,10},{10,1... | collective-permute-start | bytes 4616 | tf_op jit(solution)/shard_map/ppermute | solution.py:419
  46.3 5.7 %collective-permute-start.4 = (f32[5,8,128]{2,1,0:T(8,128)S(1)}, f32[5,8,128]{2,1,0:T(8,128)S(1)}, u32[]{:S(2)}, u32[]{:S(2)}) collective-permute-start(f32[5,8,128]{2,1,0:T(8,128)S(1)} %slice_select_fusion.1), channel_id=1, source_target_pairs={{0,28},{3,7},{4,0},{7,11},{8,4},{11,15},{12,8},{15,19},{16,12},{19... | collective-permute-start | bytes 61448 | tf_op jit(solution)/shard_map/ppermute | solution.py:503
  48.9 5.0 %copy-start.6 = (f32[3,1,1,64]{3,2,1,0:T(1,128)S(1)}, f32[3,1,1,64]{3,2,1,0:T(1,128)}, u32[]{:S(2)}) copy-start(f32[3,1,1,64]{3,2,1,0:T(1,128)} %speed.1) | copy-start | bytes 2308
  52.0 5.7 %collective-permute-start.5 = (f32[5,8,128]{2,1,0:T(8,128)S(1)}, f32[5,8,128]{2,1,0:T(8,128)S(1)}, u32[]{:S(2)}, u32[]{:S(2)}) collective-permute-start(f32[5,8,128]{2,1,0:T(8,128)S(1)} %broadcast_select_fusion), channel_id=1, source_target_pairs={{0,24},{3,11},{4,28},{7,15},{8,0},{11,19},{12,4},{15,23},{16,8},{1... | collective-permute-start | bytes 61448 | tf_op jit(solution)/shard_map/ppermute | solution.py:503
  57.7 6.6 %collective-permute-start.6 = (f32[5,8,128]{2,1,0:T(8,128)S(1)}, f32[5,8,128]{2,1,0:T(8,128)S(1)}, u32[]{:S(2)}, u32[]{:S(2)}) collective-permute-start(f32[5,8,128]{2,1,0:T(8,128)S(1)} %broadcast_select_fusion.1), channel_id=1, source_target_pairs={{0,16},{3,19},{4,20},{7,23},{8,24},{11,27},{12,28},{15,31},{16,0},... | collective-permute-start | bytes 61448 | tf_op jit(solution)/shard_map/ppermute | solution.py:503

commit v2 on v1

--- a/solution.py
+++ b/solution.py
@@ -48,7 +48,6 @@
 NT = (((1,), (1,)), ((), ()))
 
 VMEM = pl.BlockSpec(memory_space=pltpu.VMEM)
-SMEM = pl.BlockSpec(memory_space=pltpu.SMEM)
 
 
 def collide_kernel(pops, speed, relaxed, density, right_msg, left_msg):
@@ -102,10 +101,26 @@
         left_msg[10, k : k + 1, :] = twice
 
 
-def prepare_kernel(shift, own_right, own_left, from_left, from_right, up_msg, down_msg, own_speed, rows):
+def prepare_kernel(
+    offset, own_right, own_left, from_left, from_right, up_msg, down_msg, edge_msg, own_speed, rows
+):
     width_x = own_right.shape[1]
-    up_rest, down_rest = shift[0], shift[1]
-    top_edge, bottom_edge = shift[2], shift[3]
+    grad_index = lax.axis_index("grad")
+    at_top = grad_index == lax.axis_size("grad") - 1
+    at_bottom = grad_index == 0
+    rest = jnp.broadcast_to(lax.rem(offset[...], width_x), (width_x, LANES))
+    up_rest = jnp.where(at_top, rest, 0)
+    down_rest = jnp.where(at_bottom, rest, 0)
+    top_boost = jnp.where(at_top, 1.0, 0.0)
+    bottom_boost = jnp.where(at_bottom, 1.0, 0.0)
+
+    def window(j, start, sign, amount):
+        moved = rows[j, start : start + width_x, :]
+        for r in range(1, width_x):
+            first = start + sign * r
+            moved = jnp.where(amount == r, rows[j, first : first + width_x, :], moved)
+        return moved
+
     for j, direction in enumerate(UPWARD):
         step = VELOCITIES[direction][0]
         boost = 6.0 * WEIGHTS[direction] * step * SHEAR_SPEED
@@ -114,10 +129,11 @@
         if step > 0:
             slab = from_left[RIGHTWARD.index(direction)]
             rows[j, SUBS - 1 : SUBS] = slab[SUBS - 1 :, :]
-        moved = rows[j, pl.ds(SUBS - step + up_rest, width_x), :]
+        moved = window(j, SUBS - step, 1, up_rest)
         if step != 0:
-            moved = moved - boost * top_edge.astype(F32)
+            moved = moved - boost * top_boost
         up_msg[j] = moved
+        edge_msg[j] = moved
     for j, direction in enumerate(DOWNWARD):
         step = VELOCITIES[direction][0]
         boost = 6.0 * WEIGHTS[direction] * step * SHEAR_SPEED
@@ -126,10 +142,11 @@
         if step < 0:
             slab = from_right[LEFTWARD.index(direction)]
             rows[5 + j, 2 * SUBS : 2 * SUBS + 1] = slab[:1, :]
-        moved = rows[5 + j, pl.ds(SUBS - step - down_rest, width_x), :]
+        moved = window(5 + j, SUBS - step, -1, down_rest)
         if step != 0:
-            moved = moved + boost * bottom_edge.astype(F32)
+            moved = moved + boost * bottom_boost
         down_msg[j] = moved
+        edge_msg[j] = jnp.where(at_bottom, moved, edge_msg[j])
     three = [from_left[10], own_right[10], from_right[10]]
     for out, first in ((up_msg, 5), (down_msg, 5), (own_speed, 0)):
         for f in range(3):
@@ -142,7 +159,8 @@
     return value.astype(F32).astype(BF16)
 
 
-def mark_kernel(count, cell, direction, sphere, marks):
+def mark_kernel(first_step, count, cell, direction, sphere, *refs):
+    marks = refs[-1]
     step = pl.program_id(0)
     width = cell.shape[2]
     half_rows = marks.shape[0]
@@ -152,12 +170,12 @@
     z = q % LANES
     half = (row >= half_rows).astype(jnp.int32)
     row = row - half * half_rows
-    number = step * width + lax.broadcasted_iota(jnp.int32, (1, width), 1)
+    number = (first_step + step) * width + lax.broadcasted_iota(jnp.int32, (1, width), 1)
     level = ref // LANES
     scale = jnp.where(level == 0, 1.0, 0.0)
     for t in range(1, 5):
         scale = jnp.where(level == t, 2.0 ** (8 * t), scale)
-    code = jnp.where(number < count[0, 0], (LANES + ref % LANES).astype(F32) * scale, 0.0)
+    code = jnp.where(number < count[...], (LANES + ref % LANES).astype(F32) * scale, 0.0)
     block = half_rows // 3
     parts = []
     for first in range(0, half_rows, block):
@@ -181,7 +199,7 @@
 
     @pl.when(step == 0)
     def _():
-        marks[...] = part
+        marks[...] = refs[0][...] + part if len(refs) == 2 else part
 
     @pl.when(step > 0)
     def _():
@@ -206,7 +224,9 @@
     pair_gap,
     pair_normal,
     bounced,
-    parts,
+    to_left,
+    to_self,
+    to_right,
     link_table,
     first_of,
     second_of,
@@ -322,6 +342,8 @@
 
     lax.fori_loop(0, 9, group, 0)
 
+    for out in (to_left, to_self, to_right):
+        out[...] = jnp.zeros(out.shape, F32)
     totals = []
     for k in range(3):
         total = None
@@ -359,7 +381,7 @@
             rate = addend if rate is None else rate + addend
         resist = LUB_COEF * (1.0 / jnp.maximum(gap, GAP_FLOOR) - 1.0 / GAP_CUTOFF)
         number = start + lane
-        factor = jnp.where(number < pair_count[0, 0], -resist * rate, 0.0)
+        factor = jnp.where(number < pair_count[...], -resist * rate, 0.0)
         values = [factor * pair_normal[k, 0, :, here] for k in range(3)]
         first = first + 4 * slots
         for ref, these in ((first, values), (second, [-v for v in values])):
@@ -381,11 +403,16 @@
                 piece = pltpu.roll(piece, 16 * s, axis=1)
             line = piece if line is None else line + piece
         for code in range(NEAR):
-            row = 3 * (code % 3) + k
-            parts[code // 3, row : row + 1, :] = line[code : code + 1]
-
-
-def stream_kernel(relaxed, bounced, from_left, from_right, below, above, out):
+            row = SUBS * (code % 3) + k
+            [to_left, to_self, to_right][code // 3][row : row + 1, :] = line[code : code + 1]
+
+
+def stream_kernel(relaxed, bounced, from_left, from_right, below, above, edge, out):
+    grad_index = lax.axis_index("grad")
+    at_top = grad_index == lax.axis_size("grad") - 1
+    at_bottom = grad_index == 0
+    low_rows = [jnp.where(at_bottom, edge[j], below[j]) for j in range(5)]
+    high_rows = [jnp.where(at_top, edge[j], above[j]) for j in range(5)]
     width_x, width_y = relaxed.shape[1], relaxed.shape[2]
     for direction, (cx, cy, cz) in enumerate(VELOCITIES):
         for x in range(width_x):
@@ -400,10 +427,10 @@
                 tile = pltpu.roll(tile, cy % width_y, axis=0)
                 row = lax.broadcasted_iota(jnp.int32, tile.shape, 0)
                 if cy > 0:
-                    ghost = below[UPWARD.index(direction), x : x + 1, :]
+                    ghost = low_rows[UPWARD.index(direction)][x : x + 1, :]
                     tile = jnp.where(row == 0, jnp.broadcast_to(ghost, tile.shape), tile)
                 else:
-                    ghost = above[DOWNWARD.index(direction), x : x + 1, :]
+                    ghost = high_rows[DOWNWARD.index(direction)][x : x + 1, :]
                     tile = jnp.where(row == width_y - 1, jnp.broadcast_to(ghost, tile.shape), tile)
             if cz != 0:
                 tile = pltpu.roll(tile, cz % LANES, axis=1)
@@ -414,6 +441,15 @@
             out[direction, x] = tile
 
 
+def finish_kernel(own, one, other, speed, force, moved):
+    slots = speed.shape[3]
+    total = own[...] + one[...] + other[...]
+    for k in range(3):
+        line = total[k : k + 1, :slots]
+        force[k, 0] = line
+        moved[k, 0] = speed[k, 0] + INV_MASS * line
+
+
 def send(block, axis, distance):
     count = lax.axis_size(axis)
     return lax.ppermute(block, axis, [(i, (i + distance) % count) for i in range(count)])
@@ -421,6 +457,30 @@
 
 def shape_of(*dims):
     return jax.ShapeDtypeStruct(dims, F32)
+
+
+def local_of(*dims):
+    return pltpu.VMEM(dims, F32)
+
+
+def local(*arrays):
+    return [pltpu.with_memory_space_constraint(array, pltpu.VMEM) for array in arrays]
+
+
+def mark_links(first, steps, half_rows, count, link_arrays, *before):
+    links = link_arrays[0].shape[2]
+    width = links // 4
+    link_spec = pl.BlockSpec((1, 1, width), lambda i: (0, 0, i + first))
+    whole = pl.BlockSpec((half_rows, 2 * LANES), lambda i: (0, 0))
+    one = pl.BlockSpec((1, 1), lambda i: (0, 0))
+    return pl.pallas_call(
+        functools.partial(mark_kernel, first),
+        name="mark",
+        grid=(steps,),
+        in_specs=[one, link_spec, link_spec, link_spec] + [whole] * len(before),
+        out_specs=whole,
+        out_shape=local_of(half_rows, 2 * LANES),
+    )(count, *link_arrays, *local(*before))
 
 
 def per_device(
@@ -439,10 +499,8 @@
 ):
     width_x, width_y, depth = populations.shape[1:]
     slots = sphere_velocity.shape[3]
-    links = link_cell.shape[2]
     flow_count = lax.axis_size("flow")
     grad_count = lax.axis_size("grad")
-    grad_index = lax.axis_index("grad")
     assert depth == LANES and width_y == SUBS and width_x == SUBS and 2 * slots == LANES
 
     relaxed, density, right_msg, left_msg = pl.pallas_call(
@@ -451,10 +509,10 @@
         in_specs=[VMEM, VMEM],
         out_specs=[VMEM] * 4,
         out_shape=[
-            shape_of(19, width_x, width_y, depth),
-            shape_of(width_x, width_y, depth),
-            shape_of(11, SUBS, LANES),
-            shape_of(11, SUBS, LANES),
+            local_of(19, width_x, width_y, depth),
+            local_of(width_x, width_y, depth),
+            local_of(11, SUBS, LANES),
+            local_of(11, SUBS, LANES),
         ],
     )(populations, sphere_velocity)
 
@@ -462,55 +520,52 @@
     from_right = send(left_msg, "flow", -1)
 
     half_rows = 9 * width_x * width_y
-    width = links // 4
-    link_spec = pl.BlockSpec((1, 1, width), lambda i: (0, 0, i))
-    marks = pl.pallas_call(
-        mark_kernel,
-        name="mark",
-        grid=(links // width,),
-        in_specs=[SMEM, link_spec, link_spec, link_spec],
-        out_specs=pl.BlockSpec((half_rows, 2 * LANES), lambda i: (0, 0)),
-        out_shape=shape_of(half_rows, 2 * LANES),
-    )(link_count, link_cell, link_dir, link_sphere)
-
-    offset = le_offset[0]
-    rest = offset % width_x
-    at_top = (grad_index == grad_count - 1).astype(jnp.int32)
-    at_bottom = (grad_index == 0).astype(jnp.int32)
-    shift = jnp.stack([rest * at_top, rest * at_bottom, at_top, at_bottom])
-    up_msg, down_msg, own_speed = pl.pallas_call(
+    link_arrays = [link_cell, link_dir, link_sphere]
+    marks = mark_links(0, 2, half_rows, link_count, link_arrays)
+
+    up_msg, down_msg, edge_msg, own_speed = pl.pallas_call(
         prepare_kernel,
         name="prepare",
-        in_specs=[SMEM] + [VMEM] * 4,
-        out_specs=[VMEM] * 3,
-        out_shape=[shape_of(7, SUBS, LANES), shape_of(7, SUBS, LANES), shape_of(2, SUBS, LANES)],
+        in_specs=[VMEM] * 5,
+        out_specs=[VMEM] * 4,
+        out_shape=[
+            local_of(7, SUBS, LANES),
+            local_of(7, SUBS, LANES),
+            local_of(5, SUBS, LANES),
+            local_of(2, SUBS, LANES),
+        ],
         scratch_shapes=[pltpu.VMEM((10, 3 * SUBS, LANES), F32)],
-    )(shift, right_msg, left_msg, from_left, from_right)
-
-    below = send(up_msg, "grad", 1)
-    above = send(down_msg, "grad", -1)
-
-    hops = offset // width_x
-    edge = jnp.where(at_bottom == 1, below[:5], above[:5])
-    for level in range(max(flow_count - 1, 1).bit_length()):
+    )(le_offset.reshape(1, 1), *local(right_msg, left_msg, from_left, from_right))
+
+    def exchange(hops, up_msg, down_msg, edge_msg, marks, link_count, *link_arrays):
+        below = send(up_msg, "grad", 1)
+        above = send(down_msg, "grad", -1)
         route = []
         for a in range(flow_count):
-            far = 1 << level
-            route.append((a * grad_count, (a - far) % flow_count * grad_count))
-            route.append(
-                (a * grad_count + grad_count - 1, (a + far) % flow_count * grad_count + grad_count - 1)
-            )
-        arrived = lax.ppermute(edge, ("flow", "grad"), route)
-        edge = jnp.where(hops // (1 << level) % 2 == 1, arrived, edge)
-    below_rows = jnp.where(at_bottom == 1, edge, below[:5])
-    above_rows = jnp.where(at_top == 1, edge, above[:5])
-
-    bounced, parts = pl.pallas_call(
+            top = grad_count - 1
+            route.append(((a + hops) % flow_count * grad_count + top, a * grad_count))
+            route.append(((a - hops) % flow_count * grad_count, a * grad_count + top))
+        edge = lax.ppermute(edge_msg, ("flow", "grad"), route)
+        marks = mark_links(2, 2, half_rows, link_count, link_arrays, marks)
+        return below, above, edge, marks
+
+    below, above, edge, marks = lax.switch(
+        lax.div(le_offset[0], width_x),
+        [functools.partial(exchange, hops) for hops in range(flow_count)],
+        up_msg,
+        down_msg,
+        edge_msg,
+        marks,
+        link_count,
+        *link_arrays,
+    )
+
+    bounced, to_left, to_self, to_right = pl.pallas_call(
         force_kernel,
         name="force",
-        in_specs=[SMEM] + [VMEM] * 10,
-        out_specs=[VMEM] * 2,
-        out_shape=[shape_of(18, width_x, width_y, depth), shape_of(3, 2 * SUBS, LANES)],
+        in_specs=[VMEM] * 11,
+        out_specs=[VMEM] * 4,
+        out_shape=[local_of(18, width_x, width_y, depth)] + [local_of(3 * SUBS, LANES)] * 3,
         scratch_shapes=[
             pltpu.VMEM((18, SUBS, LANES), F32),
             pltpu.VMEM((2 * width_x * SUBS, LANES), F32),
@@ -520,31 +575,32 @@
         ],
     )(
         pair_count,
-        relaxed,
-        density,
-        marks,
-        own_speed,
-        below,
-        above,
+        *local(relaxed, density, marks, own_speed, below, above),
         pair_first,
         pair_second,
         pair_gap,
         pair_normal,
     )
 
-    column = parts[1] + send(parts[0], "flow", -1) + send(parts[2], "flow", 1)
-    column = column[:9].reshape(3, 3, LANES)
-    own_force = column[1] + send(column[0], "grad", -1) + send(column[2], "grad", 1)
-    sphere_force = own_force[:, None, None, :slots]
-    velocity_next = sphere_velocity + INV_MASS * sphere_force
+    column = to_self + send(to_left, "flow", -1) + send(to_right, "flow", 1)
+    from_above = send(column[:SUBS], "grad", -1)
+    from_below = send(column[2 * SUBS :], "grad", 1)
+    line = shape_of(3, 1, 1, slots)
+    sphere_force, velocity_next = pl.pallas_call(
+        finish_kernel,
+        name="finish",
+        in_specs=[VMEM] * 4,
+        out_specs=[VMEM] * 2,
+        out_shape=[line, line],
+    )(*local(column[SUBS : 2 * SUBS], from_above, from_below), sphere_velocity)
 
     updated = pl.pallas_call(
         stream_kernel,
         name="stream",
-        in_specs=[VMEM] * 6,
+        in_specs=[VMEM] * 7,
         out_specs=VMEM,
         out_shape=shape_of(19, width_x, width_y, depth),
-    )(relaxed, bounced, from_left, from_right, below_rows, above_rows)
+    )(*local(relaxed, bounced, from_left, from_right, below, above, edge))
     return updated, sphere_force, velocity_next
 
 

time: 67.6 us -> 43.5 us (0.64)
  waiting for transfers between devices: 18.2 us -> 7.57 us
  starting transfers between devices: 18.1 us -> 14.2 us
  local copies, waits for them, and re-layouts: 3.68 us -> 0.02 us
  Pallas kernels: 22.4 us -> 19.1 us
  other arithmetic: 1.99 us -> 0.01 us
    ppermute x3 -> x1, waiting for transfers between devices: 10.3 us -> 0.35 us  [exchange(): edge = lax.ppermute(edge_msg, ('flow', 'grad'), route)]
    ppermute x3 -> x1, starting transfers between devices: 5.74 us -> 1.91 us  [exchange(): edge = lax.ppermute(edge_msg, ('flow', 'grad'), route)]
    unnamed x16 -> x6, local copies, waits for them, and re-layouts: 2.96 us -> 0.01 us
    pallas_call x4 -> x6, Pallas kernels: 20.2 us -> 17.7 us  [the longest x1 7.64 us: per_device(): pl.pallas_call(force_kernel, name='force', in_specs=[VMEM] * 11, out_spec...]
    pallas_call x1, Pallas kernels: 2.22 us -> 1.39 us  [per_device(): pl.pallas_call(collide_kernel, name='collide', in_specs=[VMEM, VMEM], out...]
    squeeze x1 -> x0, local copies, waits for them, and re-layouts: 0.72 us -> none  [per_device(): column = parts[1] + send(parts[0], 'flow', -1) + send(parts[2], 'flow', 1)]
    add x3 -> x1, other arithmetic: 0.71 us -> 0.01 us  [per_device(): column = to_self + send(to_left, 'flow', -1) + send(to_right, 'flow', 1)]
  transfers between devices with their start and end apart: 11 -> 9, of which waited for: 7 -> 4; matrix products, arithmetic and copies ran while one was open for 3% -> 0% of each run, Pallas kernels for 11% -> 20%
where the time goes in v2:
time: 43.5 us; the launch traced here: 43.6 us
  Pallas kernels  19.1 us (44%)
  starting transfers between devices  14.2 us (33%)
  waiting for transfers between devices  7.57 us (17%)
  between operations  2.69 us (6%)
    ppermute x8, starting transfers between devices, send(): lax.ppermute(block, axis, [(i, (i + distance) % count) for i in range(cou...  12.2 us
    pallas_call x1, Pallas kernels, per_device(): pl.pallas_call(force_kernel, name='force', in_specs=[VMEM] * 11, out_spec...  7.64 us
    ppermute x8, waiting for transfers between devices, send(): lax.ppermute(block, axis, [(i, (i + distance) % count) for i in range(cou...  7.23 us
    pallas_call x2, Pallas kernels, mark_links(): pl.pallas_call(functools.partial(mark_kernel, first), name='mark', grid=(...  6.93 us
    ppermute x1, starting transfers between devices, exchange(): edge = lax.ppermute(edge_msg, ('flow', 'grad'), route)  1.91 us
    pallas_call x1, Pallas kernels, per_device(): pl.pallas_call(stream_kernel, name='stream', in_specs=[VMEM] * 7, out_spe...  1.75 us
    pallas_call x1, Pallas kernels, per_device(): pl.pallas_call(collide_kernel, name='collide', in_specs=[VMEM, VMEM], out...  1.39 us
    pallas_call x1, Pallas kernels, per_device(): pl.pallas_call(finish_kernel, name='finish', in_specs=[VMEM] * 4, out_spe...  1.25 us
  transfers between devices with their start and end apart: 9, of which 4 were waited for; matrix products, arithmetic and copies ran while one was open for 0% of the time, Pallas kernels for 20%

profile of v2, /device:TPU:0, one launch (start us, length us, event | category | flops | bytes accessed | tf_op | source)
XLA Modules:
  0.0 43.6 jit_solution(17906984691522302337)
XLA Ops:
  0.6 0.0 copy-start
  0.6 0.0 copy-start.1
  0.7 0.0 copy-start.2
  0.7 1.4 %collide.1 = (f32[19,8,8,128]{3,2,1,0:T(8,128)S(1)}, f32[8,8,128]{2,1,0:T(8,128)S(1)}, f32[11,8,128]{2,1,0:T(8,128)S(1)}, f32[11,8,128]{2,1,0:T(8,128)S(1)}) custom-call(f32[19,8,8,128]{3,2,1,0:T(8,128)} %pops.1, f32[3,1,1,64]{3,2,1,0:T(1,128)} %speed.3), custom_call_target="tpu_custom_call" | custom-call | tf_op jit(solution)/shard_map/collide/pallas_call | solution.py:506
  2.1 3.0 %collective-permute-start.24 = (f32[11,8,128]{2,1,0:T(8,128)S(1)}, f32[11,8,128]{2,1,0:T(8,128)S(1)}, u32[]{:S(2)}, u32[]{:S(2)}) collective-permute-start(f32[11,8,128]{2,1,0:T(8,128)S(1)} %get-tuple-element.215.own_right), channel_id=1, source_target_pairs={{0,4},{4,8},{8,12},{12,16},{16,20},{20,24},{24,28},{28,0},{1,5},{5... | collective-permute-start | bytes 135176 | tf_op jit(solution)/shard_map/ppermute | solution.py:455
  5.1 3.1 %collective-permute-start.25 = (f32[11,8,128]{2,1,0:T(8,128)S(1)}, f32[11,8,128]{2,1,0:T(8,128)S(1)}, u32[]{:S(2)}, u32[]{:S(2)}) collective-permute-start(f32[11,8,128]{2,1,0:T(8,128)S(1)} %get-tuple-element.216.own_left), channel_id=1, source_target_pairs={{0,28},{4,0},{8,4},{12,8},{16,12},{20,16},{24,20},{28,24},{1,29},{... | collective-permute-start | bytes 135176 | tf_op jit(solution)/shard_map/ppermute | solution.py:455
  10.1 0.0 copy-done
  10.2 0.0 copy-done.1
  10.2 0.0 copy-done.2
  10.2 3.1 %mark.17 = f32[576,256]{1,0:T(8,128)S(1)} custom-call(s32[1,1]{1,0:T(1,128)S(6)} %copy.48.count, s32[1,1,16384]{2,1,0:T(1,128)S(1)} %copy-done, s32[1,1,16384]{2,1,0:T(1,128)S(1)} %copy-done.1, s32[1,1,16384]{2,1,0:T(1,128)S(1)} %copy-done.2), custom_call_target="tpu_custom_call" | custom-call | tf_op jit(solution)/shard_map/mark/pallas_call | solution.py:476
  13.3 0.0 collective-permute-done.24.from_left
  13.3 0.0 collective-permute-done.25.from_right
  13.3 0.1 prepare.1
  13.4 7.9 %conditional.1 = (f32[7,8,128]{2,1,0:T(8,128)}, f32[7,8,128]{2,1,0:T(8,128)}, f32[5,8,128]{2,1,0:T(8,128)}, f32[576,256]{1,0:T(8,128)S(1)}) conditional(s32[]{:T(128)} %clamp.3, (f32[7,8,128]{2,1,0:T(8,128)S(1)}, f32[7,8,128]{2,1,0:T(8,128)S(1)}, f32[5,8,128]{2,1,0:T(8,128)S(1)}, s32[1,1]{1,0:T(1,128)}, ...), branch_computations={%region_0.0_spmd, %region_1.0_spmd, %region_2.0_spmd, %region_3.0_... | conditional | bytes 311448 | solution.py:552
  13.4 0.1 collective-permute-start.6
  13.5 1.7 %collective-permute-start.7 = (f32[7,8,128]{2,1,0:T(8,128)S(1)}, f32[7,8,128]{2,1,0:T(8,128)}, u32[]{:S(2)}, u32[]{:S(2)}) collective-permute-start(f32[7,8,128]{2,1,0:T(8,128)S(1)} %get-tuple-element.145), channel_id=1, source_target_pairs={{0,3},{1,0},{2,1},{3,2},{4,7},{5,4},{6,5},{7,6},{8,11},{9,8},{10,9... | collective-permute-start | bytes 86024 | tf_op jit(solution)/shard_map/cond/branch_2_fun/ppermute | solution.py:455
  15.2 1.9 %collective-permute-start.8 = (f32[5,8,128]{2,1,0:T(8,128)S(1)}, f32[5,8,128]{2,1,0:T(8,128)}, u32[]{:S(2)}, u32[]{:S(2)}) collective-permute-start(f32[5,8,128]{2,1,0:T(8,128)S(1)} %get-tuple-element.146), channel_id=1, source_target_pairs={{11,0},{24,3},{15,4},{28,7},{19,8},{0,11},{23,12},{4,15},{27,16},{... | collective-permute-start | bytes 61448 | tf_op jit(solution)/shard_map/cond/branch_2_fun/ppermute | solution.py:548
  17.2 3.8 %mark.11 = f32[576,256]{1,0:T(8,128)S(1)} custom-call(s32[1,1]{1,0:T(1,128)} %get-tuple-element.147.count, s32[1,1,16384]{2,1,0:T(1,128)S(1)} %get-tuple-element.148.cell, s32[1,1,16384]{2,1,0:T(1,128)S(1)} %get-tuple-element.149.direction, s32[1,1,16384]{2,1,0:T(1,128)S(1)} %get-tuple-element.150.sphere, f32[576,256]{1,0:T(8,128)S(1)} %get-tuple-element.151.refs_0_), custom_call_target="tpu_custom_call" | custom-call | tf_op jit(solution)/shard_map/cond/branch_2_fun/mark/pallas_call | solution.py:476
  21.0 0.3 collective-permute-done.8
  21.3 0.0 collective-permute-done.6
  21.3 0.0 collective-permute-done.7
  21.3 7.6 %force.1 = (f32[18,8,8,128]{3,2,1,0:T(8,128)S(1)}, f32[24,128]{1,0:T(8,128)S(1)}, f32[24,128]{1,0:T(8,128)S(1)}, f32[24,128]{1,0:T(8,128)S(1)}) custom-call(s32[1,1]{1,0:T(1,128)S(6)} %copy.49.pair_count, f32[19,8,8,128]{3,2,1,0:T(8,128)S(1)} %get-tuple-element.213.relaxed, f32[8,8,128]{2,1,0:T(8,128)S(1)} %get-tuple-element.214.density, ...), custom_call_target="tpu_custom_call" | custom-call | tf_op jit(solution)/shard_map/force/pallas_call | solution.py:563
  29.0 3.8 %collective-permute-start.26 = (f32[24,128]{1,0:T(8,128)S(1)}, f32[24,128]{1,0:T(8,128)S(1)}, u32[]{:S(2)}, u32[]{:S(2)}) collective-permute-start(f32[24,128]{1,0:T(8,128)S(1)} %get-tuple-element.227), channel_id=1, source_target_pairs={{0,28},{4,0},{8,4},{12,8},{16,12},{20,16},{24,20},{28,24},{1,29},{... | collective-permute-start | bytes 36872 | tf_op jit(solution)/shard_map/ppermute | solution.py:455
  32.8 0.0 collective-permute-start.27
  32.8 1.4 %collective-permute-done.26 = f32[24,128]{1,0:T(8,128)S(1)} collective-permute-done((f32[24,128]{1,0:T(8,128)S(1)}, f32[24,128]{1,0:T(8,128)S(1)}, u32[]{:S(2)}, u32[]{:S(2)}) %collective-permute-start.26) | collective-permute-done | bytes 12320 | tf_op jit(solution)/shard_map/ppermute | solution.py:455
  34.2 5.0 %collective-permute-done.27 = f32[24,128]{1,0:T(8,128)S(1)} collective-permute-done((f32[24,128]{1,0:T(8,128)S(1)}, f32[24,128]{1,0:T(8,128)S(1)}, u32[]{:S(2)}, u32[]{:S(2)}) %collective-permute-start.27) | collective-permute-done | bytes 12320 | tf_op jit(solution)/shard_map/ppermute | solution.py:455
  39.2 0.0 collective-permute-start.28
  39.2 0.5 %collective-permute-start.29 = (f32[8,128]{1,0:T(8,128)S(1)}, f32[8,128]{1,0:T(8,128)S(1)}, u32[]{:S(2)}, u32[]{:S(2)}) collective-permute-start(f32[8,128]{1,0:T(8,128)S(1)} %get-tuple-element.231), channel_id=1, source_target_pairs={{0,1},{1,2},{2,3},{3,0},{4,5},{5,6},{6,7},{7,4},{8,9},{9,10},{10,1... | collective-permute-start | bytes 12296 | tf_op jit(solution)/shard_map/ppermute | solution.py:455
  39.7 1.8 %stream.1 = f32[19,8,8,128]{3,2,1,0:T(8,128)} custom-call(f32[19,8,8,128]{3,2,1,0:T(8,128)S(1)} %get-tuple-element.213.relaxed, f32[18,8,8,128]{3,2,1,0:T(8,128)S(1)} %get-tuple-element.224.bounced, f32[11,8,128]{2,1,0:T(8,128)S(1)} %collective-permute-done.24.from_left, f32[11,8,128]{2,1,0:T(8,128)S(1)} %collective-permute-done.25.from_right, ...), custom_call_target="tpu_custom_call" | custom-call | tf_op jit(solution)/shard_map/stream/pallas_call | solution.py:597
  41.5 0.0 collective-permute-done.28.one
  41.5 0.8 %collective-permute-done.29.other = f32[8,128]{1,0:T(8,128)S(1)} collective-permute-done((f32[8,128]{1,0:T(8,128)S(1)}, f32[8,128]{1,0:T(8,128)S(1)}, u32[]{:S(2)}, u32[]{:S(2)}) %collective-permute-start.29) | collective-permute-done | bytes 4128 | tf_op jit(solution)/shard_map/ppermute | solution.py:455
  42.3 1.3 %finish.1 = (f32[3,1,1,64]{3,2,1,0:T(1,128)}, f32[3,1,1,64]{3,2,1,0:T(1,128)}) custom-call(f32[8,128]{1,0:T(8,128)S(1)} %get-tuple-element.233.own, f32[8,128]{1,0:T(8,128)S(1)} %collective-permute-done.28.one, f32[8,128]{1,0:T(8,128)S(1)} %collective-permute-done.29.other, f32[3,1,1,64]{3,2,1,0:T(1,128)} %speed.3), custom_call_target="tpu_custom_call" | custom-call | tf_op jit(solution)/shard_map/finish/pallas_call | solution.py:589
  (2 shorter events, 0.0 us)
Async XLA Ops:
  0.6 9.5 %copy-start = (s32[1,1,16384]{2,1,0:T(1,128)S(1)}, s32[1,1,16384]{2,1,0:T(1,128)}, u32[]{:S(2)}) copy-start(s32[1,1,16384]{2,1,0:T(1,128)} %cell.1) | copy-start | bytes 196612
  0.6 9.5 %copy-start.1 = (s32[1,1,16384]{2,1,0:T(1,128)S(1)}, s32[1,1,16384]{2,1,0:T(1,128)}, u32[]{:S(2)}) copy-start(s32[1,1,16384]{2,1,0:T(1,128)} %direction.1) | copy-start | bytes 196612
  0.7 9.5 %copy-start.2 = (s32[1,1,16384]{2,1,0:T(1,128)S(1)}, s32[1,1,16384]{2,1,0:T(1,128)}, u32[]{:S(2)}) copy-start(s32[1,1,16384]{2,1,0:T(1,128)} %sphere.1) | copy-start | bytes 196612
  2.1 11.2 %collective-permute-start.24 = (f32[11,8,128]{2,1,0:T(8,128)S(1)}, f32[11,8,128]{2,1,0:T(8,128)S(1)}, u32[]{:S(2)}, u32[]{:S(2)}) collective-permute-start(f32[11,8,128]{2,1,0:T(8,128)S(1)} %get-tuple-element.215.own_right), channel_id=1, source_target_pairs={{0,4},{4,8},{8,12},{12,16},{16,20},{20,24},{24,28},{28,0},{1,5},{5... | collective-permute-start | bytes 135176 | tf_op jit(solution)/shard_map/ppermute | solution.py:455
  5.1 8.2 %collective-permute-start.25 = (f32[11,8,128]{2,1,0:T(8,128)S(1)}, f32[11,8,128]{2,1,0:T(8,128)S(1)}, u32[]{:S(2)}, u32[]{:S(2)}) collective-permute-start(f32[11,8,128]{2,1,0:T(8,128)S(1)} %get-tuple-element.216.own_left), channel_id=1, source_target_pairs={{0,28},{4,0},{8,4},{12,8},{16,12},{20,16},{24,20},{28,24},{1,29},{... | collective-permute-start | bytes 135176 | tf_op jit(solution)/shard_map/ppermute | solution.py:455
  13.4 7.9 %collective-permute-start.6 = (f32[7,8,128]{2,1,0:T(8,128)S(1)}, f32[7,8,128]{2,1,0:T(8,128)}, u32[]{:S(2)}, u32[]{:S(2)}) collective-permute-start(f32[7,8,128]{2,1,0:T(8,128)S(1)} %get-tuple-element.144), channel_id=1, source_target_pairs={{0,1},{1,2},{2,3},{3,0},{4,5},{5,6},{6,7},{7,4},{8,9},{9,10},{10,1... | collective-permute-start | bytes 86024 | tf_op jit(solution)/shard_map/cond/branch_2_fun/ppermute | solution.py:455
  13.5 7.8 %collective-permute-start.7 = (f32[7,8,128]{2,1,0:T(8,128)S(1)}, f32[7,8,128]{2,1,0:T(8,128)}, u32[]{:S(2)}, u32[]{:S(2)}) collective-permute-start(f32[7,8,128]{2,1,0:T(8,128)S(1)} %get-tuple-element.145), channel_id=1, source_target_pairs={{0,3},{1,0},{2,1},{3,2},{4,7},{5,4},{6,5},{7,6},{8,11},{9,8},{10,9... | collective-permute-start | bytes 86024 | tf_op jit(solution)/shard_map/cond/branch_2_fun/ppermute | solution.py:455
  15.2 6.1 %collective-permute-start.8 = (f32[5,8,128]{2,1,0:T(8,128)S(1)}, f32[5,8,128]{2,1,0:T(8,128)}, u32[]{:S(2)}, u32[]{:S(2)}) collective-permute-start(f32[5,8,128]{2,1,0:T(8,128)S(1)} %get-tuple-element.146), channel_id=1, source_target_pairs={{11,0},{24,3},{15,4},{28,7},{19,8},{0,11},{23,12},{4,15},{27,16},{... | collective-permute-start | bytes 61448 | tf_op jit(solution)/shard_map/cond/branch_2_fun/ppermute | solution.py:548
  29.0 5.2 %collective-permute-start.26 = (f32[24,128]{1,0:T(8,128)S(1)}, f32[24,128]{1,0:T(8,128)S(1)}, u32[]{:S(2)}, u32[]{:S(2)}) collective-permute-start(f32[24,128]{1,0:T(8,128)S(1)} %get-tuple-element.227), channel_id=1, source_target_pairs={{0,28},{4,0},{8,4},{12,8},{16,12},{20,16},{24,20},{28,24},{1,29},{... | collective-permute-start | bytes 36872 | tf_op jit(solution)/shard_map/ppermute | solution.py:455
  32.8 6.4 %collective-permute-start.27 = (f32[24,128]{1,0:T(8,128)S(1)}, f32[24,128]{1,0:T(8,128)S(1)}, u32[]{:S(2)}, u32[]{:S(2)}) collective-permute-start(f32[24,128]{1,0:T(8,128)S(1)} %get-tuple-element.228), channel_id=1, source_target_pairs={{0,4},{4,8},{8,12},{12,16},{16,20},{20,24},{24,28},{28,0},{1,5},{5... | collective-permute-start | bytes 36872 | tf_op jit(solution)/shard_map/ppermute | solution.py:455
  39.2 2.3 %collective-permute-start.28 = (f32[8,128]{1,0:T(8,128)S(1)}, f32[8,128]{1,0:T(8,128)S(1)}, u32[]{:S(2)}, u32[]{:S(2)}) collective-permute-start(f32[8,128]{1,0:T(8,128)S(1)} %get-tuple-element.232), channel_id=1, source_target_pairs={{0,3},{1,0},{2,1},{3,2},{4,7},{5,4},{6,5},{7,6},{8,11},{9,8},{10,9... | collective-permute-start | bytes 12296 | tf_op jit(solution)/shard_map/ppermute | solution.py:455
  39.2 3.1 %collective-permute-start.29 = (f32[8,128]{1,0:T(8,128)S(1)}, f32[8,128]{1,0:T(8,128)S(1)}, u32[]{:S(2)}, u32[]{:S(2)}) collective-permute-start(f32[8,128]{1,0:T(8,128)S(1)} %get-tuple-element.231), channel_id=1, source_target_pairs={{0,1},{1,2},{2,3},{3,0},{4,5},{5,6},{6,7},{7,4},{8,9},{9,10},{10,1... | collective-permute-start | bytes 12296 | tf_op jit(solution)/shard_map/ppermute | solution.py:455

commit v3 on v2

--- a/solution.py
+++ b/solution.py
@@ -50,7 +50,7 @@
 VMEM = pl.BlockSpec(memory_space=pltpu.VMEM)
 
 
-def collide_kernel(pops, speed, relaxed, density, right_msg, left_msg):
+def collide_kernel(pops, speed, relaxed, density, right_msg, left_msg, own_line):
     width_x, width_y = pops.shape[1], pops.shape[2]
     slots = speed.shape[3]
     for x in range(width_x):
@@ -99,6 +99,7 @@
         twice = jnp.concatenate([row] * (LANES // slots), axis=1)
         right_msg[10, k : k + 1, :] = twice
         left_msg[10, k : k + 1, :] = twice
+        own_line[k : k + 1, :] = twice
 
 
 def prepare_kernel(
@@ -231,6 +232,7 @@
     first_of,
     second_of,
     value_of,
+    rest_of,
     sums,
 ):
     width_x = relaxed.shape[1]
@@ -266,6 +268,20 @@
     index_b = to_bf16(lax.broadcasted_iota(jnp.int32, (16, LANES), 0))
     one = jnp.ones((), BF16)
     zero = jnp.zeros((), BF16)
+
+    def spread(ref, r):
+        row = ref[pl.ds(r, SUBS, stride=0), :]
+        return jnp.concatenate([row, row], axis=0).astype(BF16)
+
+    def slot_rows(r):
+        a = spread(first_of, r)
+        b = spread(second_of, r)
+        high = spread(value_of, r)
+        low = spread(rest_of, r)
+        left = [jnp.where(index_a[16 * i : 16 * i + 16] == a, one, zero) for i in range(3)]
+        mask = index_b == b
+        right = [jnp.where(mask, high, zero), jnp.where(mask, low, zero)]
+        return jnp.concatenate(left, axis=0), jnp.concatenate(right, axis=0)
 
     def hot_rows(first_row, second_row, values):
         a = jnp.broadcast_to(to_bf16(first_row), (48, LANES))
@@ -324,14 +340,15 @@
                 where = side * width_x * SUBS + SUBS * x
                 first_of[where : where + SUBS] = first
                 second_of[where : where + SUBS] = second
-                value_of[where : where + SUBS] = jnp.where(live, force, 0.0)
+                force = jnp.where(live, force, 0.0)
+                high = force.astype(BF16).astype(F32)
+                value_of[where : where + SUBS] = high
+                rest_of[where : where + SUBS] = force - high
         lefts, rights = [], []
         for r in range(2 * width_x * SUBS):
-            left, right = hot_rows(
-                first_of[r : r + 1], second_of[r : r + 1], [value_of[r : r + 1]]
-            )
+            left, right = slot_rows(r)
             lefts.append(left)
-            rights.append(right[0])
+            rights.append(right)
         sums[g] = lax.dot_general(
             jnp.concatenate(lefts, axis=1),
             jnp.concatenate(rights, axis=1),
@@ -442,12 +459,12 @@
 
 
 def finish_kernel(own, one, other, speed, force, moved):
-    slots = speed.shape[3]
+    slots = force.shape[3]
     total = own[...] + one[...] + other[...]
     for k in range(3):
         line = total[k : k + 1, :slots]
         force[k, 0] = line
-        moved[k, 0] = speed[k, 0] + INV_MASS * line
+        moved[k, 0] = speed[k : k + 1, :slots] + INV_MASS * line
 
 
 def send(block, axis, distance):
@@ -469,7 +486,7 @@
 
 def mark_links(first, steps, half_rows, count, link_arrays, *before):
     links = link_arrays[0].shape[2]
-    width = links // 4
+    width = links // 2
     link_spec = pl.BlockSpec((1, 1, width), lambda i: (0, 0, i + first))
     whole = pl.BlockSpec((half_rows, 2 * LANES), lambda i: (0, 0))
     one = pl.BlockSpec((1, 1), lambda i: (0, 0))
@@ -503,16 +520,17 @@
     grad_count = lax.axis_size("grad")
     assert depth == LANES and width_y == SUBS and width_x == SUBS and 2 * slots == LANES
 
-    relaxed, density, right_msg, left_msg = pl.pallas_call(
+    relaxed, density, right_msg, left_msg, own_line = pl.pallas_call(
         collide_kernel,
         name="collide",
         in_specs=[VMEM, VMEM],
-        out_specs=[VMEM] * 4,
+        out_specs=[VMEM] * 5,
         out_shape=[
             local_of(19, width_x, width_y, depth),
             local_of(width_x, width_y, depth),
             local_of(11, SUBS, LANES),
             local_of(11, SUBS, LANES),
+            local_of(3, LANES),
         ],
     )(populations, sphere_velocity)
 
@@ -521,7 +539,7 @@
 
     half_rows = 9 * width_x * width_y
     link_arrays = [link_cell, link_dir, link_sphere]
-    marks = mark_links(0, 2, half_rows, link_count, link_arrays)
+    marks = mark_links(0, 1, half_rows, link_count, link_arrays)
 
     up_msg, down_msg, edge_msg, own_speed = pl.pallas_call(
         prepare_kernel,
@@ -546,7 +564,7 @@
             route.append(((a + hops) % flow_count * grad_count + top, a * grad_count))
             route.append(((a - hops) % flow_count * grad_count, a * grad_count + top))
         edge = lax.ppermute(edge_msg, ("flow", "grad"), route)
-        marks = mark_links(2, 2, half_rows, link_count, link_arrays, marks)
+        marks = mark_links(1, 1, half_rows, link_count, link_arrays, marks)
         return below, above, edge, marks
 
     below, above, edge, marks = lax.switch(
@@ -568,6 +586,7 @@
         out_shape=[local_of(18, width_x, width_y, depth)] + [local_of(3 * SUBS, LANES)] * 3,
         scratch_shapes=[
             pltpu.VMEM((18, SUBS, LANES), F32),
+            pltpu.VMEM((2 * width_x * SUBS, LANES), F32),
             pltpu.VMEM((2 * width_x * SUBS, LANES), F32),
             pltpu.VMEM((2 * width_x * SUBS, LANES), F32),
             pltpu.VMEM((2 * width_x * SUBS, LANES), F32),
@@ -582,6 +601,14 @@
         pair_normal,
     )
 
+    updated = pl.pallas_call(
+        stream_kernel,
+        name="stream",
+        in_specs=[VMEM] * 7,
+        out_specs=VMEM,
+        out_shape=shape_of(19, width_x, width_y, depth),
+    )(*local(relaxed, bounced, from_left, from_right, below, above, edge))
+
     column = to_self + send(to_left, "flow", -1) + send(to_right, "flow", 1)
     from_above = send(column[:SUBS], "grad", -1)
     from_below = send(column[2 * SUBS :], "grad", 1)
@@ -592,15 +619,8 @@
         in_specs=[VMEM] * 4,
         out_specs=[VMEM] * 2,
         out_shape=[line, line],
-    )(*local(column[SUBS : 2 * SUBS], from_above, from_below), sphere_velocity)
-
-    updated = pl.pallas_call(
-        stream_kernel,
-        name="stream",
-        in_specs=[VMEM] * 7,
-        out_specs=VMEM,
-        out_shape=shape_of(19, width_x, width_y, depth),
-    )(*local(relaxed, bounced, from_left, from_right, below, above, edge))
+    )(*local(column[SUBS : 2 * SUBS], from_above, from_below, own_line))
+
     return updated, sphere_force, velocity_next
 
 

time: 43.5 us -> 42 us (0.966)
  Pallas kernels: 19.1 us -> 17.2 us
    ppermute x1, waiting for transfers between devices: 0.35 us -> 1.99 us  [exchange(): edge = lax.ppermute(edge_msg, ('flow', 'grad'), route)]
    ppermute x1, starting transfers between devices: 1.91 us -> 3.42 us  [exchange(): edge = lax.ppermute(edge_msg, ('flow', 'grad'), route)]
    ppermute x8, waiting for transfers between devices: 7.23 us -> 5.72 us  [send(): lax.ppermute(block, axis, [(i, (i + distance) % count) for i in range(cou...]
    ppermute x8, starting transfers between devices: 12.2 us -> 10.9 us  [send(): lax.ppermute(block, axis, [(i, (i + distance) % count) for i in range(cou...]
    pallas_call x2, Pallas kernels: 6.93 us -> 6.08 us  [mark_links(): pl.pallas_call(functools.partial(mark_kernel, first), name='mark', grid=(...]
    pallas_call x1, Pallas kernels: 1.25 us -> 0.57 us  [per_device(): pl.pallas_call(finish_kernel, name='finish', in_specs=[VMEM] * 4, out_spe...]
  transfers between devices with their start and end apart: 9 -> 9, of which waited for: 4 -> 4; matrix products, arithmetic and copies ran while one was open for 0% -> 0% of each run, Pallas kernels for 20% -> 19%
where the time goes in v3:
time: 42 us; the launch traced here: 42.3 us
  Pallas kernels  17.2 us (41%)
  starting transfers between devices  14.3 us (34%)
  waiting for transfers between devices  7.71 us (18%)
  between operations  2.7 us (6%)
    ppermute x8, starting transfers between devices, send(): lax.ppermute(block, axis, [(i, (i + distance) % count) for i in range(cou...  10.9 us
    pallas_call x1, Pallas kernels, per_device(): pl.pallas_call(force_kernel, name='force', in_specs=[VMEM] * 11, out_spec...  7.33 us
    pallas_call x2, Pallas kernels, mark_links(): pl.pallas_call(functools.partial(mark_kernel, first), name='mark', grid=(...  6.08 us
    ppermute x8, waiting for transfers between devices, send(): lax.ppermute(block, axis, [(i, (i + distance) % count) for i in range(cou...  5.72 us
    ppermute x1, starting transfers between devices, exchange(): edge = lax.ppermute(edge_msg, ('flow', 'grad'), route)  3.42 us
    ppermute x1, waiting for transfers between devices, exchange(): edge = lax.ppermute(edge_msg, ('flow', 'grad'), route)  1.99 us
    pallas_call x1, Pallas kernels, per_device(): pl.pallas_call(stream_kernel, name='stream', in_specs=[VMEM] * 7, out_spe...  1.75 us
    pallas_call x1, Pallas kernels, per_device(): pl.pallas_call(collide_kernel, name='collide', in_specs=[VMEM, VMEM], out...  1.39 us
  transfers between devices with their start and end apart: 9, of which 4 were waited for; matrix products, arithmetic and copies ran while one was open for 0% of the time, Pallas kernels for 19%

profile of v3, /device:TPU:0, one launch (start us, length us, event | category | flops | bytes accessed | tf_op | source)
XLA Modules:
  0.0 42.3 jit_solution(9851647656239390977)
XLA Ops:
  0.6 0.0 copy-start
  0.6 0.0 copy-start.1
  0.7 0.0 copy-start.2
  0.7 1.4 %collide.1 = (f32[19,8,8,128]{3,2,1,0:T(8,128)S(1)}, f32[8,8,128]{2,1,0:T(8,128)S(1)}, f32[11,8,128]{2,1,0:T(8,128)S(1)}, f32[11,8,128]{2,1,0:T(8,128)S(1)}, f32[3,128]{1,0:T(4,128)S(1)}) custom-call(f32[19,8,8,128]{3,2,1,0:T(8,128)} %pops.1, f32[3,1,1,64]{3,2,1,0:T(1,128)} %speed.1), custom_call_target="tpu_custom_call" | custom-call | tf_op jit(solution)/shard_map/collide/pallas_call | solution.py:523
  2.1 3.0 %collective-permute-start.24 = (f32[11,8,128]{2,1,0:T(8,128)S(1)}, f32[11,8,128]{2,1,0:T(8,128)S(1)}, u32[]{:S(2)}, u32[]{:S(2)}) collective-permute-start(f32[11,8,128]{2,1,0:T(8,128)S(1)} %get-tuple-element.216.own_right), channel_id=1, source_target_pairs={{0,4},{4,8},{8,12},{12,16},{16,20},{20,24},{24,28},{28,0},{1,5},{5... | collective-permute-start | bytes 135176 | tf_op jit(solution)/shard_map/ppermute | solution.py:472
  5.1 3.1 %collective-permute-start.25 = (f32[11,8,128]{2,1,0:T(8,128)S(1)}, f32[11,8,128]{2,1,0:T(8,128)S(1)}, u32[]{:S(2)}, u32[]{:S(2)}) collective-permute-start(f32[11,8,128]{2,1,0:T(8,128)S(1)} %get-tuple-element.217.own_left), channel_id=1, source_target_pairs={{0,28},{4,0},{8,4},{12,8},{16,12},{20,16},{24,20},{28,24},{1,29},{... | collective-permute-start | bytes 135176 | tf_op jit(solution)/shard_map/ppermute | solution.py:472
  10.1 0.0 copy-done
  10.2 0.0 copy-done.1
  10.2 0.0 copy-done.2
  10.2 2.7 %mark.17 = f32[576,256]{1,0:T(8,128)S(1)} custom-call(s32[1,1]{1,0:T(1,128)S(6)} %copy.48.count, s32[1,1,16384]{2,1,0:T(1,128)S(1)} %copy-done, s32[1,1,16384]{2,1,0:T(1,128)S(1)} %copy-done.1, s32[1,1,16384]{2,1,0:T(1,128)S(1)} %copy-done.2), custom_call_target="tpu_custom_call" | custom-call | tf_op jit(solution)/shard_map/mark/pallas_call | solution.py:493
  12.9 0.0 collective-permute-done.24.from_left
  12.9 0.0 collective-permute-done.25.from_right
  12.9 0.1 prepare.1
  13.0 10.8 %conditional.1 = (f32[7,8,128]{2,1,0:T(8,128)}, f32[7,8,128]{2,1,0:T(8,128)}, f32[5,8,128]{2,1,0:T(8,128)}, f32[576,256]{1,0:T(8,128)S(1)}) conditional(s32[]{:T(128)} %clamp.3, (f32[7,8,128]{2,1,0:T(8,128)S(1)}, f32[7,8,128]{2,1,0:T(8,128)S(1)}, f32[5,8,128]{2,1,0:T(8,128)S(1)}, s32[1,1]{1,0:T(1,128)}, ...), branch_computations={%region_0.0_spmd, %region_1.0_spmd, %region_2.0_spmd, %region_3.0_... | conditional | bytes 311448 | solution.py:570
  13.3 0.1 collective-permute-start.21
  13.3 1.7 %collective-permute-start.22 = (f32[7,8,128]{2,1,0:T(8,128)S(1)}, f32[7,8,128]{2,1,0:T(8,128)}, u32[]{:S(2)}, u32[]{:S(2)}) collective-permute-start(f32[7,8,128]{2,1,0:T(8,128)S(1)} %get-tuple-element.185), channel_id=1, source_target_pairs={{0,3},{1,0},{2,1},{3,2},{4,7},{5,4},{6,5},{7,6},{8,11},{9,8},{10,9... | collective-permute-start | bytes 86024 | tf_op jit(solution)/shard_map/cond/branch_7_fun/ppermute | solution.py:472
  15.1 3.4 %collective-permute-start.23 = (f32[5,8,128]{2,1,0:T(8,128)S(1)}, f32[5,8,128]{2,1,0:T(8,128)}, u32[]{:S(2)}, u32[]{:S(2)}) collective-permute-start(f32[5,8,128]{2,1,0:T(8,128)S(1)} %get-tuple-element.186), channel_id=1, source_target_pairs={{31,0},{4,3},{3,4},{8,7},{7,8},{12,11},{11,12},{16,15},{15,16},{20... | collective-permute-start | bytes 61448 | tf_op jit(solution)/shard_map/cond/branch_7_fun/ppermute | solution.py:566
  18.5 3.4 %mark.16 = f32[576,256]{1,0:T(8,128)S(1)} custom-call(s32[1,1]{1,0:T(1,128)} %get-tuple-element.187.count, s32[1,1,16384]{2,1,0:T(1,128)S(1)} %get-tuple-element.188.cell, s32[1,1,16384]{2,1,0:T(1,128)S(1)} %get-tuple-element.189.direction, s32[1,1,16384]{2,1,0:T(1,128)S(1)} %get-tuple-element.190.sphere, f32[576,256]{1,0:T(8,128)S(1)} %get-tuple-element.191.refs_0_), custom_call_target="tpu_custom_call" | custom-call | tf_op jit(solution)/shard_map/cond/branch_7_fun/mark/pallas_call | solution.py:493
  21.9 2.0 %collective-permute-done.23 = f32[5,8,128]{2,1,0:T(8,128)} collective-permute-done((f32[5,8,128]{2,1,0:T(8,128)S(1)}, f32[5,8,128]{2,1,0:T(8,128)}, u32[]{:S(2)}, u32[]{:S(2)}) %collective-permute-start.23) | collective-permute-done | bytes 20512 | tf_op jit(solution)/shard_map/cond/branch_7_fun/ppermute | solution.py:566
  23.8 0.0 collective-permute-done.21
  23.8 0.0 collective-permute-done.22
  23.9 7.3 %force.1 = (f32[18,8,8,128]{3,2,1,0:T(8,128)S(1)}, f32[24,128]{1,0:T(8,128)S(1)}, f32[24,128]{1,0:T(8,128)S(1)}, f32[24,128]{1,0:T(8,128)S(1)}) custom-call(s32[1,1]{1,0:T(1,128)S(6)} %copy.49.pair_count, f32[19,8,8,128]{3,2,1,0:T(8,128)S(1)} %get-tuple-element.214.relaxed, f32[8,8,128]{2,1,0:T(8,128)S(1)} %get-tuple-element.215.density, ...), custom_call_target="tpu_custom_call" | custom-call | tf_op jit(solution)/shard_map/force/pallas_call | solution.py:581
  31.2 0.1 collective-permute-start.26
  31.3 2.0 %collective-permute-start.27 = (f32[24,128]{1,0:T(8,128)S(1)}, f32[24,128]{1,0:T(8,128)S(1)}, u32[]{:S(2)}, u32[]{:S(2)}) collective-permute-start(f32[24,128]{1,0:T(8,128)S(1)} %get-tuple-element.229), channel_id=1, source_target_pairs={{0,4},{4,8},{8,12},{12,16},{16,20},{20,24},{24,28},{28,0},{1,5},{5... | collective-permute-start | bytes 36872 | tf_op jit(solution)/shard_map/ppermute | solution.py:472
  33.3 1.7 %collective-permute-done.26 = f32[24,128]{1,0:T(8,128)S(1)} collective-permute-done((f32[24,128]{1,0:T(8,128)S(1)}, f32[24,128]{1,0:T(8,128)S(1)}, u32[]{:S(2)}, u32[]{:S(2)}) %collective-permute-start.26) | collective-permute-done | bytes 12320 | tf_op jit(solution)/shard_map/ppermute | solution.py:472
  34.9 2.8 %collective-permute-done.27 = f32[24,128]{1,0:T(8,128)S(1)} collective-permute-done((f32[24,128]{1,0:T(8,128)S(1)}, f32[24,128]{1,0:T(8,128)S(1)}, u32[]{:S(2)}, u32[]{:S(2)}) %collective-permute-start.27) | collective-permute-done | bytes 12320 | tf_op jit(solution)/shard_map/ppermute | solution.py:472
  37.7 0.9 %collective-permute-start.28 = (f32[8,128]{1,0:T(8,128)S(1)}, f32[8,128]{1,0:T(8,128)S(1)}, u32[]{:S(2)}, u32[]{:S(2)}) collective-permute-start(f32[8,128]{1,0:T(8,128)S(1)} %get-tuple-element.234), channel_id=1, source_target_pairs={{0,3},{1,0},{2,1},{3,2},{4,7},{5,4},{6,5},{7,6},{8,11},{9,8},{10,9... | collective-permute-start | bytes 12296 | tf_op jit(solution)/shard_map/ppermute | solution.py:472
  38.7 0.0 collective-permute-start.29
  38.7 1.8 %stream.1 = f32[19,8,8,128]{3,2,1,0:T(8,128)} custom-call(f32[19,8,8,128]{3,2,1,0:T(8,128)S(1)} %get-tuple-element.214.relaxed, f32[18,8,8,128]{3,2,1,0:T(8,128)S(1)} %get-tuple-element.225.bounced, f32[11,8,128]{2,1,0:T(8,128)S(1)} %collective-permute-done.24.from_left, f32[11,8,128]{2,1,0:T(8,128)S(1)} %collective-permute-done.25.from_right, ...), custom_call_target="tpu_custom_call" | custom-call | tf_op jit(solution)/shard_map/stream/pallas_call | solution.py:604
  40.4 0.0 collective-permute-done.28.one
  40.4 1.3 %collective-permute-done.29.other = f32[8,128]{1,0:T(8,128)S(1)} collective-permute-done((f32[8,128]{1,0:T(8,128)S(1)}, f32[8,128]{1,0:T(8,128)S(1)}, u32[]{:S(2)}, u32[]{:S(2)}) %collective-permute-start.29) | collective-permute-done | bytes 4128 | tf_op jit(solution)/shard_map/ppermute | solution.py:472
  41.7 0.6 %finish.1 = (f32[3,1,1,64]{3,2,1,0:T(1,128)}, f32[3,1,1,64]{3,2,1,0:T(1,128)}) custom-call(f32[8,128]{1,0:T(8,128)S(1)} %get-tuple-element.235.own, f32[8,128]{1,0:T(8,128)S(1)} %collective-permute-done.28.one, f32[8,128]{1,0:T(8,128)S(1)} %collective-permute-done.29.other, f32[3,128]{1,0:T(4,128)S(1)} %get-tuple-element.230.speed), custom_call_target="tpu_custom_call" | custom-call | tf_op jit(solution)/shard_map/finish/pallas_call | solution.py:616
  (2 shorter events, 0.0 us)
Async XLA Ops:
  0.6 9.5 %copy-start = (s32[1,1,16384]{2,1,0:T(1,128)S(1)}, s32[1,1,16384]{2,1,0:T(1,128)}, u32[]{:S(2)}) copy-start(s32[1,1,16384]{2,1,0:T(1,128)} %cell.1) | copy-start | bytes 196612
  0.6 9.5 %copy-start.1 = (s32[1,1,16384]{2,1,0:T(1,128)S(1)}, s32[1,1,16384]{2,1,0:T(1,128)}, u32[]{:S(2)}) copy-start(s32[1,1,16384]{2,1,0:T(1,128)} %direction.1) | copy-start | bytes 196612
  0.7 9.5 %copy-start.2 = (s32[1,1,16384]{2,1,0:T(1,128)S(1)}, s32[1,1,16384]{2,1,0:T(1,128)}, u32[]{:S(2)}) copy-start(s32[1,1,16384]{2,1,0:T(1,128)} %sphere.1) | copy-start | bytes 196612
  2.1 10.8 %collective-permute-start.24 = (f32[11,8,128]{2,1,0:T(8,128)S(1)}, f32[11,8,128]{2,1,0:T(8,128)S(1)}, u32[]{:S(2)}, u32[]{:S(2)}) collective-permute-start(f32[11,8,128]{2,1,0:T(8,128)S(1)} %get-tuple-element.216.own_right), channel_id=1, source_target_pairs={{0,4},{4,8},{8,12},{12,16},{16,20},{20,24},{24,28},{28,0},{1,5},{5... | collective-permute-start | bytes 135176 | tf_op jit(solution)/shard_map/ppermute | solution.py:472
  5.1 7.8 %collective-permute-start.25 = (f32[11,8,128]{2,1,0:T(8,128)S(1)}, f32[11,8,128]{2,1,0:T(8,128)S(1)}, u32[]{:S(2)}, u32[]{:S(2)}) collective-permute-start(f32[11,8,128]{2,1,0:T(8,128)S(1)} %get-tuple-element.217.own_left), channel_id=1, source_target_pairs={{0,28},{4,0},{8,4},{12,8},{16,12},{20,16},{24,20},{28,24},{1,29},{... | collective-permute-start | bytes 135176 | tf_op jit(solution)/shard_map/ppermute | solution.py:472
  13.3 10.6 %collective-permute-start.21 = (f32[7,8,128]{2,1,0:T(8,128)S(1)}, f32[7,8,128]{2,1,0:T(8,128)}, u32[]{:S(2)}, u32[]{:S(2)}) collective-permute-start(f32[7,8,128]{2,1,0:T(8,128)S(1)} %get-tuple-element.184), channel_id=1, source_target_pairs={{0,1},{1,2},{2,3},{3,0},{4,5},{5,6},{6,7},{7,4},{8,9},{9,10},{10,1... | collective-permute-start | bytes 86024 | tf_op jit(solution)/shard_map/cond/branch_7_fun/ppermute | solution.py:472
  13.3 10.5 %collective-permute-start.22 = (f32[7,8,128]{2,1,0:T(8,128)S(1)}, f32[7,8,128]{2,1,0:T(8,128)}, u32[]{:S(2)}, u32[]{:S(2)}) collective-permute-start(f32[7,8,128]{2,1,0:T(8,128)S(1)} %get-tuple-element.185), channel_id=1, source_target_pairs={{0,3},{1,0},{2,1},{3,2},{4,7},{5,4},{6,5},{7,6},{8,11},{9,8},{10,9... | collective-permute-start | bytes 86024 | tf_op jit(solution)/shard_map/cond/branch_7_fun/ppermute | solution.py:472
  15.1 8.8 %collective-permute-start.23 = (f32[5,8,128]{2,1,0:T(8,128)S(1)}, f32[5,8,128]{2,1,0:T(8,128)}, u32[]{:S(2)}, u32[]{:S(2)}) collective-permute-start(f32[5,8,128]{2,1,0:T(8,128)S(1)} %get-tuple-element.186), channel_id=1, source_target_pairs={{31,0},{4,3},{3,4},{8,7},{7,8},{12,11},{11,12},{16,15},{15,16},{20... | collective-permute-start | bytes 61448 | tf_op jit(solution)/shard_map/cond/branch_7_fun/ppermute | solution.py:566
  31.2 3.7 %collective-permute-start.26 = (f32[24,128]{1,0:T(8,128)S(1)}, f32[24,128]{1,0:T(8,128)S(1)}, u32[]{:S(2)}, u32[]{:S(2)}) collective-permute-start(f32[24,128]{1,0:T(8,128)S(1)} %get-tuple-element.228), channel_id=1, source_target_pairs={{0,28},{4,0},{8,4},{12,8},{16,12},{20,16},{24,20},{28,24},{1,29},{... | collective-permute-start | bytes 36872 | tf_op jit(solution)/shard_map/ppermute | solution.py:472
  31.3 6.4 %collective-permute-start.27 = (f32[24,128]{1,0:T(8,128)S(1)}, f32[24,128]{1,0:T(8,128)S(1)}, u32[]{:S(2)}, u32[]{:S(2)}) collective-permute-start(f32[24,128]{1,0:T(8,128)S(1)} %get-tuple-element.229), channel_id=1, source_target_pairs={{0,4},{4,8},{8,12},{12,16},{16,20},{20,24},{24,28},{28,0},{1,5},{5... | collective-permute-start | bytes 36872 | tf_op jit(solution)/shard_map/ppermute | solution.py:472
  37.7 2.7 %collective-permute-start.28 = (f32[8,128]{1,0:T(8,128)S(1)}, f32[8,128]{1,0:T(8,128)S(1)}, u32[]{:S(2)}, u32[]{:S(2)}) collective-permute-start(f32[8,128]{1,0:T(8,128)S(1)} %get-tuple-element.234), channel_id=1, source_target_pairs={{0,3},{1,0},{2,1},{3,2},{4,7},{5,4},{6,5},{7,6},{8,11},{9,8},{10,9... | collective-permute-start | bytes 12296 | tf_op jit(solution)/shard_map/ppermute | solution.py:472
  38.7 3.0 %collective-permute-start.29 = (f32[8,128]{1,0:T(8,128)S(1)}, f32[8,128]{1,0:T(8,128)S(1)}, u32[]{:S(2)}, u32[]{:S(2)}) collective-permute-start(f32[8,128]{1,0:T(8,128)S(1)} %get-tuple-element.233), channel_id=1, source_target_pairs={{0,1},{1,2},{2,3},{3,0},{4,5},{5,6},{6,7},{7,4},{8,9},{9,10},{10,1... | collective-permute-start | bytes 12296 | tf_op jit(solution)/shard_map/ppermute | solution.py:472

commit v4 on v3

--- a/solution.py
+++ b/solution.py
@@ -103,12 +103,13 @@
 
 
 def prepare_kernel(
-    offset, own_right, own_left, from_left, from_right, up_msg, down_msg, edge_msg, own_speed, rows
+    offset, own_right, own_left, from_left, from_right, msg_pair, msg_cross, own_speed, rows
 ):
     width_x = own_right.shape[1]
     grad_index = lax.axis_index("grad")
     at_top = grad_index == lax.axis_size("grad") - 1
     at_bottom = grad_index == 0
+    even = lax.rem(grad_index, 2) == 0
     rest = jnp.broadcast_to(lax.rem(offset[...], width_x), (width_x, LANES))
     up_rest = jnp.where(at_top, rest, 0)
     down_rest = jnp.where(at_bottom, rest, 0)
@@ -122,6 +123,7 @@
             moved = jnp.where(amount == r, rows[j, first : first + width_x, :], moved)
         return moved
 
+    ups = []
     for j, direction in enumerate(UPWARD):
         step = VELOCITIES[direction][0]
         boost = 6.0 * WEIGHTS[direction] * step * SHEAR_SPEED
@@ -133,8 +135,7 @@
         moved = window(j, SUBS - step, 1, up_rest)
         if step != 0:
             moved = moved - boost * top_boost
-        up_msg[j] = moved
-        edge_msg[j] = moved
+        ups.append(moved)
     for j, direction in enumerate(DOWNWARD):
         step = VELOCITIES[direction][0]
         boost = 6.0 * WEIGHTS[direction] * step * SHEAR_SPEED
@@ -146,10 +147,10 @@
         moved = window(5 + j, SUBS - step, -1, down_rest)
         if step != 0:
             moved = moved + boost * bottom_boost
-        down_msg[j] = moved
-        edge_msg[j] = jnp.where(at_bottom, moved, edge_msg[j])
+        msg_pair[j] = jnp.where(even, ups[j], moved)
+        msg_cross[j] = jnp.where(even, moved, ups[j])
     three = [from_left[10], own_right[10], from_right[10]]
-    for out, first in ((up_msg, 5), (down_msg, 5), (own_speed, 0)):
+    for out, first in ((msg_pair, 5), (msg_cross, 5), (own_speed, 0)):
         for f in range(3):
             for k in range(3):
                 row = 3 * f + k
@@ -218,8 +219,9 @@
     density,
     marks,
     own_speed,
-    below_speed,
-    above_speed,
+    from_pair,
+    from_cross,
+    from_wrap,
     pair_first,
     pair_second,
     pair_gap,
@@ -229,23 +231,28 @@
     to_self,
     to_right,
     link_table,
-    first_of,
-    second_of,
-    value_of,
-    rest_of,
-    sums,
+    *scratch,
 ):
     width_x = relaxed.shape[1]
     slots = LANES // 2
+    even_buffers, odd_buffers, sums = scratch[:4], scratch[4:8], scratch[8]
+    first_of = odd_buffers[0]
     half_rows = marks.shape[0]
     lane = lax.broadcasted_iota(jnp.int32, (1, LANES), 1)
-    sources = [below_speed, own_speed, above_speed]
+    grad_index = lax.axis_index("grad")
+    even = lax.rem(grad_index, 2) == 0
+    at_edge = (grad_index == 0) | (grad_index == lax.axis_size("grad") - 1)
+    sources = [[], [], []]
+    for tile in range(2):
+        near = from_pair[5 + tile]
+        far = jnp.where(at_edge, from_wrap[tile], from_cross[5 + tile])
+        sources[0].append(jnp.where(even, far, near))
+        sources[1].append(own_speed[tile])
+        sources[2].append(jnp.where(even, near, far))
 
     def speed_row(code, k):
         row = 3 * (code // 3) + k
-        source = sources[code % 3]
-        first = 0 if source is own_speed else 5
-        return source[first + row // SUBS, row % SUBS : row % SUBS + 1, :]
+        return sources[code % 3][row // SUBS][row % SUBS : row % SUBS + 1, :]
 
     tables = []
     for k in range(3):
@@ -273,7 +280,8 @@
         row = ref[pl.ds(r, SUBS, stride=0), :]
         return jnp.concatenate([row, row], axis=0).astype(BF16)
 
-    def slot_rows(r):
+    def slot_rows(buffers, r):
+        first_of, second_of, value_of, rest_of = buffers
         a = spread(first_of, r)
         b = spread(second_of, r)
         high = spread(value_of, r)
@@ -302,7 +310,8 @@
             )
         return left, right
 
-    def group(g, carry):
+    def look_up(g, buffers):
+        first_of, second_of, value_of, rest_of = buffers
         for side in range(2):
             index = 2 * g + side
             half = index // 9
@@ -344,9 +353,11 @@
                 high = force.astype(BF16).astype(F32)
                 value_of[where : where + SUBS] = high
                 rest_of[where : where + SUBS] = force - high
+
+    def add_up(g, buffers):
         lefts, rights = [], []
         for r in range(2 * width_x * SUBS):
-            left, right = slot_rows(r)
+            left, right = slot_rows(buffers, r)
             lefts.append(left)
             rights.append(right)
         sums[g] = lax.dot_general(
@@ -355,9 +366,18 @@
             NT,
             preferred_element_type=F32,
         )
+
+    look_up(0, even_buffers)
+
+    def two_groups(i, carry):
+        look_up(2 * i + 1, odd_buffers)
+        add_up(2 * i, even_buffers)
+        look_up(2 * i + 2, even_buffers)
+        add_up(2 * i + 1, odd_buffers)
         return carry
 
-    lax.fori_loop(0, 9, group, 0)
+    lax.fori_loop(0, 4, two_groups, 0)
+    add_up(8, even_buffers)
 
     for out in (to_left, to_self, to_right):
         out[...] = jnp.zeros(out.shape, F32)
@@ -424,12 +444,10 @@
             [to_left, to_self, to_right][code // 3][row : row + 1, :] = line[code : code + 1]
 
 
-def stream_kernel(relaxed, bounced, from_left, from_right, below, above, edge, out):
-    grad_index = lax.axis_index("grad")
-    at_top = grad_index == lax.axis_size("grad") - 1
-    at_bottom = grad_index == 0
-    low_rows = [jnp.where(at_bottom, edge[j], below[j]) for j in range(5)]
-    high_rows = [jnp.where(at_top, edge[j], above[j]) for j in range(5)]
+def stream_kernel(relaxed, bounced, from_left, from_right, from_pair, from_cross, out):
+    even = lax.rem(lax.axis_index("grad"), 2) == 0
+    low_rows = [jnp.where(even, from_cross[j], from_pair[j]) for j in range(5)]
+    high_rows = [jnp.where(even, from_pair[j], from_cross[j]) for j in range(5)]
     width_x, width_y = relaxed.shape[1], relaxed.shape[2]
     for direction, (cx, cy, cz) in enumerate(VELOCITIES):
         for x in range(width_x):
@@ -519,6 +537,7 @@
     flow_count = lax.axis_size("flow")
     grad_count = lax.axis_size("grad")
     assert depth == LANES and width_y == SUBS and width_x == SUBS and 2 * slots == LANES
+    assert grad_count % 2 == 0
 
     relaxed, density, right_msg, left_msg, own_line = pl.pallas_call(
         collide_kernel,
@@ -534,45 +553,51 @@
         ],
     )(populations, sphere_velocity)
 
+    from_right = send(left_msg, "flow", -1)
     from_left = send(right_msg, "flow", 1)
-    from_right = send(left_msg, "flow", -1)
 
     half_rows = 9 * width_x * width_y
     link_arrays = [link_cell, link_dir, link_sphere]
     marks = mark_links(0, 1, half_rows, link_count, link_arrays)
 
-    up_msg, down_msg, edge_msg, own_speed = pl.pallas_call(
+    msg_pair, msg_cross, own_speed = pl.pallas_call(
         prepare_kernel,
         name="prepare",
         in_specs=[VMEM] * 5,
-        out_specs=[VMEM] * 4,
+        out_specs=[VMEM] * 3,
         out_shape=[
             local_of(7, SUBS, LANES),
             local_of(7, SUBS, LANES),
-            local_of(5, SUBS, LANES),
             local_of(2, SUBS, LANES),
         ],
         scratch_shapes=[pltpu.VMEM((10, 3 * SUBS, LANES), F32)],
     )(le_offset.reshape(1, 1), *local(right_msg, left_msg, from_left, from_right))
 
-    def exchange(hops, up_msg, down_msg, edge_msg, marks, link_count, *link_arrays):
-        below = send(up_msg, "grad", 1)
-        above = send(down_msg, "grad", -1)
-        route = []
+    def exchange(hops, msg_pair, msg_cross, own_speed, marks, link_count, *link_arrays):
+        top = grad_count - 1
+        pairs, cross, wrap = [], [], []
         for a in range(flow_count):
-            top = grad_count - 1
-            route.append(((a + hops) % flow_count * grad_count + top, a * grad_count))
-            route.append(((a - hops) % flow_count * grad_count, a * grad_count + top))
-        edge = lax.ppermute(edge_msg, ("flow", "grad"), route)
+            line = a * grad_count
+            for b in range(grad_count):
+                pairs.append((line + b, line + (b ^ 1)))
+                if 0 < b < top:
+                    cross.append((line + b, line + b + (1 if b % 2 else -1)))
+            cross.append(((a + hops) % flow_count * grad_count + top, line))
+            cross.append(((a - hops) % flow_count * grad_count, line + top))
+            wrap += [(line, line + top), (line + top, line)]
+        axes = ("flow", "grad")
+        from_pair = lax.ppermute(msg_pair, axes, pairs)
+        from_wrap = lax.ppermute(own_speed, axes, wrap)
+        from_cross = lax.ppermute(msg_cross, axes, cross)
         marks = mark_links(1, 1, half_rows, link_count, link_arrays, marks)
-        return below, above, edge, marks
-
-    below, above, edge, marks = lax.switch(
+        return from_pair, from_cross, from_wrap, marks
+
+    from_pair, from_cross, from_wrap, marks = lax.switch(
         lax.div(le_offset[0], width_x),
         [functools.partial(exchange, hops) for hops in range(flow_count)],
-        up_msg,
-        down_msg,
-        edge_msg,
+        msg_pair,
+        msg_cross,
+        own_speed,
         marks,
         link_count,
         *link_arrays,
@@ -581,20 +606,17 @@
     bounced, to_left, to_self, to_right = pl.pallas_call(
         force_kernel,
         name="force",
-        in_specs=[VMEM] * 11,
+        in_specs=[VMEM] * 12,
         out_specs=[VMEM] * 4,
         out_shape=[local_of(18, width_x, width_y, depth)] + [local_of(3 * SUBS, LANES)] * 3,
         scratch_shapes=[
             pltpu.VMEM((18, SUBS, LANES), F32),
-            pltpu.VMEM((2 * width_x * SUBS, LANES), F32),
-            pltpu.VMEM((2 * width_x * SUBS, LANES), F32),
-            pltpu.VMEM((2 * width_x * SUBS, LANES), F32),
-            pltpu.VMEM((2 * width_x * SUBS, LANES), F32),
+            *[pltpu.VMEM((2 * width_x * SUBS, LANES), F32)] * 8,
             pltpu.VMEM((9, 48, 32), F32),
         ],
     )(
         pair_count,
-        *local(relaxed, density, marks, own_speed, below, above),
+        *local(relaxed, density, marks, own_speed, from_pair, from_cross, from_wrap),
         pair_first,
         pair_second,
         pair_gap,
@@ -604,10 +626,10 @@
     updated = pl.pallas_call(
         stream_kernel,
         name="stream",
-        in_specs=[VMEM] * 7,
+        in_specs=[VMEM] * 6,
         out_specs=VMEM,
         out_shape=shape_of(19, width_x, width_y, depth),
-    )(*local(relaxed, bounced, from_left, from_right, below, above, edge))
+    )(*local(relaxed, bounced, from_left, from_right, from_pair, from_cross))
 
     column = to_self + send(to_left, "flow", -1) + send(to_right, "flow", 1)
     from_above = send(column[:SUBS], "grad", -1)

time: 42 us -> 39.3 us (0.936); the launches traced: 42.3 us -> 38.6 us
  starting transfers between devices: 14.3 us -> 12.8 us
  Pallas kernels: 17.2 us -> 16 us
  waiting for transfers between devices: 7.71 us -> 6.8 us
    ppermute x8 -> x6, starting transfers between devices: 10.9 us -> 8.71 us  [send(): lax.ppermute(block, axis, [(i, (i + distance) % count) for i in range(cou...]
    ppermute x1 -> x3, waiting for transfers between devices: 1.99 us -> 0.01 us  [the longest x1 0.01 us: exchange(): from_wrap = lax.ppermute(own_speed, axes, wrap)]
    pallas_call x2, Pallas kernels: 9.08 us -> 7.82 us  [the longest x1 6.07 us: per_device(): pl.pallas_call(force_kernel, name='force', in_specs=[VMEM] * 12, out_spec...]
    ppermute x8 -> x6, waiting for transfers between devices: 5.72 us -> 6.79 us  [send(): lax.ppermute(block, axis, [(i, (i + distance) % count) for i in range(cou...]
    ppermute x1 -> x3, starting transfers between devices: 3.42 us -> 4.14 us  [the longest x1 2.09 us: exchange(): from_wrap = lax.ppermute(own_speed, axes, wrap)]
  transfers between devices with their start and end apart: 9 -> 9, of which waited for: 4 -> 3; matrix products, arithmetic and copies ran while one was open for 0% -> 0% of each run, Pallas kernels for 19% -> 20%
where the time goes in v4:
time: 39.3 us; the launch traced here: 38.6 us
  Pallas kernels  16 us (41%)
  starting transfers between devices  12.8 us (33%)
  waiting for transfers between devices  6.8 us (17%)
  between operations  2.7 us (7%)
    ppermute x6, starting transfers between devices, send(): lax.ppermute(block, axis, [(i, (i + distance) % count) for i in range(cou...  8.71 us
    ppermute x6, waiting for transfers between devices, send(): lax.ppermute(block, axis, [(i, (i + distance) % count) for i in range(cou...  6.79 us
    pallas_call x2, Pallas kernels, mark_links(): pl.pallas_call(functools.partial(mark_kernel, first), name='mark', grid=(...  6.08 us
    pallas_call x1, Pallas kernels, per_device(): pl.pallas_call(force_kernel, name='force', in_specs=[VMEM] * 12, out_spec...  6.07 us
    ppermute x1, starting transfers between devices, exchange(): from_wrap = lax.ppermute(own_speed, axes, wrap)  2.09 us
    ppermute x1, starting transfers between devices, exchange(): from_cross = lax.ppermute(msg_cross, axes, cross)  1.98 us
    pallas_call x1, Pallas kernels, per_device(): pl.pallas_call(stream_kernel, name='stream', in_specs=[VMEM] * 6, out_spe...  1.75 us
    pallas_call x1, Pallas kernels, per_device(): pl.pallas_call(collide_kernel, name='collide', in_specs=[VMEM, VMEM], out...  1.39 us
  transfers between devices with their start and end apart: 9, of which 3 were waited for; matrix products, arithmetic and copies ran while one was open for 0% of the time, Pallas kernels for 20%

profile of v4, /device:TPU:0, one launch (start us, length us, event | category | flops | bytes accessed | tf_op | source)
XLA Modules:
  0.0 38.6 jit_solution(2113495562587863110)
XLA Ops:
  0.6 0.0 copy-start
  0.6 0.0 copy-start.1
  0.7 0.0 copy-start.2
  0.7 1.4 %collide.1 = (f32[19,8,8,128]{3,2,1,0:T(8,128)S(1)}, f32[8,8,128]{2,1,0:T(8,128)S(1)}, f32[11,8,128]{2,1,0:T(8,128)S(1)}, f32[11,8,128]{2,1,0:T(8,128)S(1)}, f32[3,128]{1,0:T(4,128)S(1)}) custom-call(f32[19,8,8,128]{3,2,1,0:T(8,128)} %pops.1, f32[3,1,1,64]{3,2,1,0:T(1,128)} %speed.1), custom_call_target="tpu_custom_call" | custom-call | tf_op jit(solution)/shard_map/collide/pallas_call | solution.py:542
  2.1 3.0 %collective-permute-start.24 = (f32[11,8,128]{2,1,0:T(8,128)S(1)}, f32[11,8,128]{2,1,0:T(8,128)S(1)}, u32[]{:S(2)}, u32[]{:S(2)}) collective-permute-start(f32[11,8,128]{2,1,0:T(8,128)S(1)} %get-tuple-element.215.own_right), channel_id=1, source_target_pairs={{0,4},{4,8},{8,12},{12,16},{16,20},{20,24},{24,28},{28,0},{1,5},{5... | collective-permute-start | bytes 135176 | tf_op jit(solution)/shard_map/ppermute | solution.py:490
  5.1 3.1 %collective-permute-start.25 = (f32[11,8,128]{2,1,0:T(8,128)S(1)}, f32[11,8,128]{2,1,0:T(8,128)S(1)}, u32[]{:S(2)}, u32[]{:S(2)}) collective-permute-start(f32[11,8,128]{2,1,0:T(8,128)S(1)} %get-tuple-element.216.own_left), channel_id=1, source_target_pairs={{0,28},{4,0},{8,4},{12,8},{16,12},{20,16},{24,20},{28,24},{1,29},{... | collective-permute-start | bytes 135176 | tf_op jit(solution)/shard_map/ppermute | solution.py:490
  10.1 0.0 copy-done
  10.2 0.0 copy-done.1
  10.2 0.0 copy-done.2
  10.2 2.7 %mark.17 = f32[576,256]{1,0:T(8,128)S(1)} custom-call(s32[1,1]{1,0:T(1,128)S(6)} %copy.48.count, s32[1,1,16384]{2,1,0:T(1,128)S(1)} %copy-done, s32[1,1,16384]{2,1,0:T(1,128)S(1)} %copy-done.1, s32[1,1,16384]{2,1,0:T(1,128)S(1)} %copy-done.2), custom_call_target="tpu_custom_call" | custom-call | tf_op jit(solution)/shard_map/mark/pallas_call | solution.py:511
  12.9 0.0 collective-permute-done.24.from_left
  12.9 0.0 collective-permute-done.25.from_right
  12.9 0.1 prepare.1
  13.0 7.8 %conditional.1 = (f32[7,8,128]{2,1,0:T(8,128)}, f32[7,8,128]{2,1,0:T(8,128)}, f32[2,8,128]{2,1,0:T(8,128)}, f32[576,256]{1,0:T(8,128)S(1)}) conditional(s32[]{:T(128)} %clamp.3, (f32[7,8,128]{2,1,0:T(8,128)S(1)}, f32[7,8,128]{2,1,0:T(8,128)S(1)}, f32[2,8,128]{2,1,0:T(8,128)S(1)}, s32[1,1]{1,0:T(1,128)}, ...), branch_computations={%region_0.0_spmd, %region_1.0_spmd, %region_2.0_spmd, %region_3.0_... | conditional | bytes 262296 | solution.py:595
  13.2 0.1 collective-permute-start.12
  13.3 2.0 %collective-permute-start.13 = (f32[7,8,128]{2,1,0:T(8,128)S(1)}, f32[7,8,128]{2,1,0:T(8,128)}, u32[]{:S(2)}, u32[]{:S(2)}) collective-permute-start(f32[7,8,128]{2,1,0:T(8,128)S(1)} %get-tuple-element.161), channel_id=1, source_target_pairs={{1,2},{2,1},{19,0},{16,3},{5,6},{6,5},{23,4},{20,7},{9,10},{10,9},... | collective-permute-start | bytes 86024 | tf_op jit(solution)/shard_map/cond/branch_4_fun/ppermute | solution.py:591
  15.3 2.1 %collective-permute-start.14 = (f32[2,8,128]{2,1,0:T(8,128)S(1)}, f32[2,8,128]{2,1,0:T(8,128)}, u32[]{:S(2)}, u32[]{:S(2)}) collective-permute-start(f32[2,8,128]{2,1,0:T(8,128)S(1)} %get-tuple-element.162), channel_id=1, source_target_pairs={{0,3},{3,0},{4,7},{7,4},{8,11},{11,8},{12,15},{15,12},{16,19},{19,... | collective-permute-start | bytes 24584 | tf_op jit(solution)/shard_map/cond/branch_4_fun/ppermute | solution.py:590
  17.4 3.4 %mark.13 = f32[576,256]{1,0:T(8,128)S(1)} custom-call(s32[1,1]{1,0:T(1,128)} %get-tuple-element.163.count, s32[1,1,16384]{2,1,0:T(1,128)S(1)} %get-tuple-element.164.cell, s32[1,1,16384]{2,1,0:T(1,128)S(1)} %get-tuple-element.165.direction, s32[1,1,16384]{2,1,0:T(1,128)S(1)} %get-tuple-element.166.sphere, f32[576,256]{1,0:T(8,128)S(1)} %get-tuple-element.167.refs_0_), custom_call_target="tpu_custom_call" | custom-call | tf_op jit(solution)/shard_map/cond/branch_4_fun/mark/pallas_call | solution.py:511
  20.8 0.0 collective-permute-done.14
  20.8 0.0 collective-permute-done.12
  20.8 0.0 collective-permute-done.13
  20.8 6.1 %force.1 = (f32[18,8,8,128]{3,2,1,0:T(8,128)S(1)}, f32[24,128]{1,0:T(8,128)S(1)}, f32[24,128]{1,0:T(8,128)S(1)}, f32[24,128]{1,0:T(8,128)S(1)}) custom-call(s32[1,1]{1,0:T(1,128)S(6)} %copy.49.pair_count, f32[19,8,8,128]{3,2,1,0:T(8,128)S(1)} %get-tuple-element.213.relaxed, f32[8,8,128]{2,1,0:T(8,128)S(1)} %get-tuple-element.214.density, ...), custom_call_target="tpu_custom_call" | custom-call | tf_op jit(solution)/shard_map/force/pallas_call | solution.py:606
  26.9 1.6 %collective-permute-start.26 = (f32[24,128]{1,0:T(8,128)S(1)}, f32[24,128]{1,0:T(8,128)S(1)}, u32[]{:S(2)}, u32[]{:S(2)}) collective-permute-start(f32[24,128]{1,0:T(8,128)S(1)} %get-tuple-element.226), channel_id=1, source_target_pairs={{0,28},{4,0},{8,4},{12,8},{16,12},{20,16},{24,20},{28,24},{1,29},{... | collective-permute-start | bytes 36872 | tf_op jit(solution)/shard_map/ppermute | solution.py:490
  28.5 0.4 %collective-permute-start.27 = (f32[24,128]{1,0:T(8,128)S(1)}, f32[24,128]{1,0:T(8,128)S(1)}, u32[]{:S(2)}, u32[]{:S(2)}) collective-permute-start(f32[24,128]{1,0:T(8,128)S(1)} %get-tuple-element.227), channel_id=1, source_target_pairs={{0,4},{4,8},{8,12},{12,16},{16,20},{20,24},{24,28},{28,0},{1,5},{5... | collective-permute-start | bytes 36872 | tf_op jit(solution)/shard_map/ppermute | solution.py:490
  29.0 1.7 %collective-permute-done.26 = f32[24,128]{1,0:T(8,128)S(1)} collective-permute-done((f32[24,128]{1,0:T(8,128)S(1)}, f32[24,128]{1,0:T(8,128)S(1)}, u32[]{:S(2)}, u32[]{:S(2)}) %collective-permute-start.26) | collective-permute-done | bytes 12320 | tf_op jit(solution)/shard_map/ppermute | solution.py:490
  30.6 4.3 %collective-permute-done.27 = f32[24,128]{1,0:T(8,128)S(1)} collective-permute-done((f32[24,128]{1,0:T(8,128)S(1)}, f32[24,128]{1,0:T(8,128)S(1)}, u32[]{:S(2)}, u32[]{:S(2)}) %collective-permute-start.27) | collective-permute-done | bytes 12320 | tf_op jit(solution)/shard_map/ppermute | solution.py:490
  34.9 0.0 collective-permute-start.28
  34.9 0.5 %collective-permute-start.29 = (f32[8,128]{1,0:T(8,128)S(1)}, f32[8,128]{1,0:T(8,128)S(1)}, u32[]{:S(2)}, u32[]{:S(2)}) collective-permute-start(f32[8,128]{1,0:T(8,128)S(1)} %get-tuple-element.231), channel_id=1, source_target_pairs={{0,1},{1,2},{2,3},{3,0},{4,5},{5,6},{6,7},{7,4},{8,9},{9,10},{10,1... | collective-permute-start | bytes 12296 | tf_op jit(solution)/shard_map/ppermute | solution.py:490
  35.5 1.8 %stream.1 = f32[19,8,8,128]{3,2,1,0:T(8,128)} custom-call(f32[19,8,8,128]{3,2,1,0:T(8,128)S(1)} %get-tuple-element.213.relaxed, f32[18,8,8,128]{3,2,1,0:T(8,128)S(1)} %get-tuple-element.224.bounced, f32[11,8,128]{2,1,0:T(8,128)S(1)} %collective-permute-done.24.from_left, f32[11,8,128]{2,1,0:T(8,128)S(1)} %collective-permute-done.25.from_right, ...), custom_call_target="tpu_custom_call" | custom-call | tf_op jit(solution)/shard_map/stream/pallas_call | solution.py:626
  37.2 0.0 collective-permute-done.28.one
  37.2 0.8 %collective-permute-done.29.other = f32[8,128]{1,0:T(8,128)S(1)} collective-permute-done((f32[8,128]{1,0:T(8,128)S(1)}, f32[8,128]{1,0:T(8,128)S(1)}, u32[]{:S(2)}, u32[]{:S(2)}) %collective-permute-start.29) | collective-permute-done | bytes 4128 | tf_op jit(solution)/shard_map/ppermute | solution.py:490
  38.0 0.6 %finish.1 = (f32[3,1,1,64]{3,2,1,0:T(1,128)}, f32[3,1,1,64]{3,2,1,0:T(1,128)}) custom-call(f32[8,128]{1,0:T(8,128)S(1)} %get-tuple-element.233.own, f32[8,128]{1,0:T(8,128)S(1)} %collective-permute-done.28.one, f32[8,128]{1,0:T(8,128)S(1)} %collective-permute-done.29.other, f32[3,128]{1,0:T(4,128)S(1)} %get-tuple-element.228.speed), custom_call_target="tpu_custom_call" | custom-call | tf_op jit(solution)/shard_map/finish/pallas_call | solution.py:638
  (2 shorter events, 0.0 us)
Async XLA Ops:
  0.6 9.5 %copy-start = (s32[1,1,16384]{2,1,0:T(1,128)S(1)}, s32[1,1,16384]{2,1,0:T(1,128)}, u32[]{:S(2)}) copy-start(s32[1,1,16384]{2,1,0:T(1,128)} %cell.1) | copy-start | bytes 196612
  0.6 9.5 %copy-start.1 = (s32[1,1,16384]{2,1,0:T(1,128)S(1)}, s32[1,1,16384]{2,1,0:T(1,128)}, u32[]{:S(2)}) copy-start(s32[1,1,16384]{2,1,0:T(1,128)} %direction.1) | copy-start | bytes 196612
  0.7 9.5 %copy-start.2 = (s32[1,1,16384]{2,1,0:T(1,128)S(1)}, s32[1,1,16384]{2,1,0:T(1,128)}, u32[]{:S(2)}) copy-start(s32[1,1,16384]{2,1,0:T(1,128)} %sphere.1) | copy-start | bytes 196612
  2.1 10.8 %collective-permute-start.24 = (f32[11,8,128]{2,1,0:T(8,128)S(1)}, f32[11,8,128]{2,1,0:T(8,128)S(1)}, u32[]{:S(2)}, u32[]{:S(2)}) collective-permute-start(f32[11,8,128]{2,1,0:T(8,128)S(1)} %get-tuple-element.215.own_right), channel_id=1, source_target_pairs={{0,4},{4,8},{8,12},{12,16},{16,20},{20,24},{24,28},{28,0},{1,5},{5... | collective-permute-start | bytes 135176 | tf_op jit(solution)/shard_map/ppermute | solution.py:490
  5.1 7.8 %collective-permute-start.25 = (f32[11,8,128]{2,1,0:T(8,128)S(1)}, f32[11,8,128]{2,1,0:T(8,128)S(1)}, u32[]{:S(2)}, u32[]{:S(2)}) collective-permute-start(f32[11,8,128]{2,1,0:T(8,128)S(1)} %get-tuple-element.216.own_left), channel_id=1, source_target_pairs={{0,28},{4,0},{8,4},{12,8},{16,12},{20,16},{24,20},{28,24},{1,29},{... | collective-permute-start | bytes 135176 | tf_op jit(solution)/shard_map/ppermute | solution.py:490
  13.2 7.5 %collective-permute-start.12 = (f32[7,8,128]{2,1,0:T(8,128)S(1)}, f32[7,8,128]{2,1,0:T(8,128)}, u32[]{:S(2)}, u32[]{:S(2)}) collective-permute-start(f32[7,8,128]{2,1,0:T(8,128)S(1)} %get-tuple-element.160), channel_id=1, source_target_pairs={{0,1},{1,0},{2,3},{3,2},{4,5},{5,4},{6,7},{7,6},{8,9},{9,8},{10,11... | collective-permute-start | bytes 86024 | tf_op jit(solution)/shard_map/cond/branch_4_fun/ppermute | solution.py:589
  13.3 7.5 %collective-permute-start.13 = (f32[7,8,128]{2,1,0:T(8,128)S(1)}, f32[7,8,128]{2,1,0:T(8,128)}, u32[]{:S(2)}, u32[]{:S(2)}) collective-permute-start(f32[7,8,128]{2,1,0:T(8,128)S(1)} %get-tuple-element.161), channel_id=1, source_target_pairs={{1,2},{2,1},{19,0},{16,3},{5,6},{6,5},{23,4},{20,7},{9,10},{10,9},... | collective-permute-start | bytes 86024 | tf_op jit(solution)/shard_map/cond/branch_4_fun/ppermute | solution.py:591
  15.3 5.5 %collective-permute-start.14 = (f32[2,8,128]{2,1,0:T(8,128)S(1)}, f32[2,8,128]{2,1,0:T(8,128)}, u32[]{:S(2)}, u32[]{:S(2)}) collective-permute-start(f32[2,8,128]{2,1,0:T(8,128)S(1)} %get-tuple-element.162), channel_id=1, source_target_pairs={{0,3},{3,0},{4,7},{7,4},{8,11},{11,8},{12,15},{15,12},{16,19},{19,... | collective-permute-start | bytes 24584 | tf_op jit(solution)/shard_map/cond/branch_4_fun/ppermute | solution.py:590
  26.9 3.7 %collective-permute-start.26 = (f32[24,128]{1,0:T(8,128)S(1)}, f32[24,128]{1,0:T(8,128)S(1)}, u32[]{:S(2)}, u32[]{:S(2)}) collective-permute-start(f32[24,128]{1,0:T(8,128)S(1)} %get-tuple-element.226), channel_id=1, source_target_pairs={{0,28},{4,0},{8,4},{12,8},{16,12},{20,16},{24,20},{28,24},{1,29},{... | collective-permute-start | bytes 36872 | tf_op jit(solution)/shard_map/ppermute | solution.py:490
  28.5 6.4 %collective-permute-start.27 = (f32[24,128]{1,0:T(8,128)S(1)}, f32[24,128]{1,0:T(8,128)S(1)}, u32[]{:S(2)}, u32[]{:S(2)}) collective-permute-start(f32[24,128]{1,0:T(8,128)S(1)} %get-tuple-element.227), channel_id=1, source_target_pairs={{0,4},{4,8},{8,12},{12,16},{16,20},{20,24},{24,28},{28,0},{1,5},{5... | collective-permute-start | bytes 36872 | tf_op jit(solution)/shard_map/ppermute | solution.py:490
  34.9 2.3 %collective-permute-start.28 = (f32[8,128]{1,0:T(8,128)S(1)}, f32[8,128]{1,0:T(8,128)S(1)}, u32[]{:S(2)}, u32[]{:S(2)}) collective-permute-start(f32[8,128]{1,0:T(8,128)S(1)} %get-tuple-element.232), channel_id=1, source_target_pairs={{0,3},{1,0},{2,1},{3,2},{4,7},{5,4},{6,5},{7,6},{8,11},{9,8},{10,9... | collective-permute-start | bytes 12296 | tf_op jit(solution)/shard_map/ppermute | solution.py:490
  34.9 3.1 %collective-permute-start.29 = (f32[8,128]{1,0:T(8,128)S(1)}, f32[8,128]{1,0:T(8,128)S(1)}, u32[]{:S(2)}, u32[]{:S(2)}) collective-permute-start(f32[8,128]{1,0:T(8,128)S(1)} %get-tuple-element.231), channel_id=1, source_target_pairs={{0,1},{1,2},{2,3},{3,0},{4,5},{5,6},{6,7},{7,4},{8,9},{9,10},{10,1... | collective-permute-start | bytes 12296 | tf_op jit(solution)/shard_map/ppermute | solution.py:490

commit v5 on v4

--- a/solution.py
+++ b/solution.py
@@ -6,6 +6,7 @@
 from jax.experimental import pallas as pl
 from jax.experimental.pallas import tpu as pltpu
 from jax.sharding import PartitionSpec as P
+
 
 VELOCITIES = [
     (0, 0, 0),
@@ -50,7 +51,9 @@
 VMEM = pl.BlockSpec(memory_space=pltpu.VMEM)
 
 
-def collide_kernel(pops, speed, relaxed, density, right_msg, left_msg, own_line):
+def collide_kernel(
+    pops, speed, relaxed, density, right_msg, left_msg, near_msg, far_msg, own_line
+):
     width_x, width_y = pops.shape[1], pops.shape[2]
     slots = speed.shape[3]
     for x in range(width_x):
@@ -100,12 +103,26 @@
         right_msg[10, k : k + 1, :] = twice
         left_msg[10, k : k + 1, :] = twice
         own_line[k : k + 1, :] = twice
+    even = lax.rem(lax.axis_index("flow"), 2) == 0
+    for i in range(11):
+        near_msg[i] = jnp.where(even, right_msg[i], left_msg[i])
+        far_msg[i] = jnp.where(even, left_msg[i], right_msg[i])
+
+
+def sort_sides(axis, near, far):
+    even = lax.rem(lax.axis_index(axis), 2) == 0
+    near = [near[i] for i in range(near.shape[0])]
+    far = [far[i] for i in range(far.shape[0])]
+    lower = [jnp.where(even, q, p) for p, q in zip(near, far)]
+    higher = [jnp.where(even, p, q) for p, q in zip(near, far)]
+    return lower, higher
 
 
 def prepare_kernel(
-    offset, own_right, own_left, from_left, from_right, msg_pair, msg_cross, own_speed, rows
+    offset, own_right, own_left, from_near, from_far, msg_pair, msg_cross, own_speed, rows
 ):
     width_x = own_right.shape[1]
+    from_left, from_right = sort_sides("flow", from_near, from_far)
     grad_index = lax.axis_index("grad")
     at_top = grad_index == lax.axis_size("grad") - 1
     at_bottom = grad_index == 0
@@ -227,9 +244,9 @@
     pair_gap,
     pair_normal,
     bounced,
-    to_left,
+    to_near,
     to_self,
-    to_right,
+    to_far,
     link_table,
     *scratch,
 ):
@@ -241,6 +258,7 @@
     lane = lax.broadcasted_iota(jnp.int32, (1, LANES), 1)
     grad_index = lax.axis_index("grad")
     even = lax.rem(grad_index, 2) == 0
+    even_flow = lax.rem(lax.axis_index("flow"), 2) == 0
     at_edge = (grad_index == 0) | (grad_index == lax.axis_size("grad") - 1)
     sources = [[], [], []]
     for tile in range(2):
@@ -379,7 +397,7 @@
     lax.fori_loop(0, 4, two_groups, 0)
     add_up(8, even_buffers)
 
-    for out in (to_left, to_self, to_right):
+    for out in (to_near, to_self, to_far):
         out[...] = jnp.zeros(out.shape, F32)
     totals = []
     for k in range(3):
@@ -439,15 +457,17 @@
             if s:
                 piece = pltpu.roll(piece, 16 * s, axis=1)
             line = piece if line is None else line + piece
-        for code in range(NEAR):
-            row = SUBS * (code % 3) + k
-            [to_left, to_self, to_right][code // 3][row : row + 1, :] = line[code : code + 1]
-
-
-def stream_kernel(relaxed, bounced, from_left, from_right, from_pair, from_cross, out):
-    even = lax.rem(lax.axis_index("grad"), 2) == 0
-    low_rows = [jnp.where(even, from_cross[j], from_pair[j]) for j in range(5)]
-    high_rows = [jnp.where(even, from_pair[j], from_cross[j]) for j in range(5)]
+        for g in range(3):
+            row = SUBS * g + k
+            low, own, high = [line[3 * f + g : 3 * f + g + 1] for f in range(3)]
+            to_near[row : row + 1, :] = jnp.where(even_flow, high, low)
+            to_self[row : row + 1, :] = own
+            to_far[row : row + 1, :] = jnp.where(even_flow, low, high)
+
+
+def stream_kernel(relaxed, bounced, from_near, from_far, from_pair, from_cross, out):
+    from_left, from_right = sort_sides("flow", from_near, from_far)
+    low_rows, high_rows = sort_sides("grad", from_pair, from_cross)
     width_x, width_y = relaxed.shape[1], relaxed.shape[2]
     for direction, (cx, cy, cz) in enumerate(VELOCITIES):
         for x in range(width_x):
@@ -485,9 +505,14 @@
         moved[k, 0] = speed[k : k + 1, :slots] + INV_MASS * line
 
 
-def send(block, axis, distance):
+def swap(block, axis, far):
     count = lax.axis_size(axis)
-    return lax.ppermute(block, axis, [(i, (i + distance) % count) for i in range(count)])
+    assert count % 2 == 0
+    route = []
+    for i in range(count):
+        up = (i % 2 == 0) != far
+        route.append((i, (i + (1 if up else -1)) % count))
+    return lax.ppermute(block, axis, route)
 
 
 def shape_of(*dims):
@@ -518,7 +543,7 @@
     )(count, *link_arrays, *local(*before))
 
 
-def per_device(
+def one_step(
     populations,
     le_offset,
     sphere_velocity,
@@ -539,22 +564,24 @@
     assert depth == LANES and width_y == SUBS and width_x == SUBS and 2 * slots == LANES
     assert grad_count % 2 == 0
 
-    relaxed, density, right_msg, left_msg, own_line = pl.pallas_call(
+    relaxed, density, right_msg, left_msg, near_msg, far_msg, own_line = pl.pallas_call(
         collide_kernel,
         name="collide",
         in_specs=[VMEM, VMEM],
-        out_specs=[VMEM] * 5,
+        out_specs=[VMEM] * 7,
         out_shape=[
             local_of(19, width_x, width_y, depth),
             local_of(width_x, width_y, depth),
             local_of(11, SUBS, LANES),
             local_of(11, SUBS, LANES),
+            local_of(11, SUBS, LANES),
+            local_of(11, SUBS, LANES),
             local_of(3, LANES),
         ],
     )(populations, sphere_velocity)
 
-    from_right = send(left_msg, "flow", -1)
-    from_left = send(right_msg, "flow", 1)
+    from_far = swap(far_msg, "flow", True)
+    from_near = swap(near_msg, "flow", False)
 
     half_rows = 9 * width_x * width_y
     link_arrays = [link_cell, link_dir, link_sphere]
@@ -571,7 +598,7 @@
             local_of(2, SUBS, LANES),
         ],
         scratch_shapes=[pltpu.VMEM((10, 3 * SUBS, LANES), F32)],
-    )(le_offset.reshape(1, 1), *local(right_msg, left_msg, from_left, from_right))
+    )(le_offset.reshape(1, 1), *local(right_msg, left_msg, from_near, from_far))
 
     def exchange(hops, msg_pair, msg_cross, own_speed, marks, link_count, *link_arrays):
         top = grad_count - 1
@@ -603,7 +630,7 @@
         *link_arrays,
     )
 
-    bounced, to_left, to_self, to_right = pl.pallas_call(
+    bounced, to_near, to_self, to_far = pl.pallas_call(
         force_kernel,
         name="force",
         in_specs=[VMEM] * 12,
@@ -629,11 +656,13 @@
         in_specs=[VMEM] * 6,
         out_specs=VMEM,
         out_shape=shape_of(19, width_x, width_y, depth),
-    )(*local(relaxed, bounced, from_left, from_right, from_pair, from_cross))
-
-    column = to_self + send(to_left, "flow", -1) + send(to_right, "flow", 1)
-    from_above = send(column[:SUBS], "grad", -1)
-    from_below = send(column[2 * SUBS :], "grad", 1)
+    )(*local(relaxed, bounced, from_near, from_far, from_pair, from_cross))
+
+    column = to_self + swap(to_far, "flow", True) + swap(to_near, "flow", False)
+    even = lax.axis_index("grad") % 2 == 0
+    low, high = column[:SUBS], column[2 * SUBS :]
+    from_cross_force = swap(jnp.where(even, low, high), "grad", True)
+    from_pair_force = swap(jnp.where(even, high, low), "grad", False)
     line = shape_of(3, 1, 1, slots)
     sphere_force, velocity_next = pl.pallas_call(
         finish_kernel,
@@ -641,7 +670,7 @@
         in_specs=[VMEM] * 4,
         out_specs=[VMEM] * 2,
         out_shape=[line, line],
-    )(*local(column[SUBS : 2 * SUBS], from_above, from_below, own_line))
+    )(*local(column[SUBS : 2 * SUBS], from_pair_force, from_cross_force, own_line))
 
     return updated, sphere_force, velocity_next
 
@@ -667,5 +696,5 @@
         P(None, "flow", "grad", None),
     )
     return jax.shard_map(
-        per_device, mesh=mesh, in_specs=in_specs, out_specs=out_specs, check_vma=False
+        one_step, mesh=mesh, in_specs=in_specs, out_specs=out_specs, check_vma=False
     )

time: 39.3 us -> 38.3 us (0.975); the launches traced: 38.6 us -> 38 us
  waiting for transfers between devices: 6.8 us -> 4.57 us
  starting transfers between devices: 12.8 us -> 14.4 us
    ppermute x6, waiting for transfers between devices: 6.79 us -> 4.56 us  [swap(): return lax.ppermute(block, axis, route)]
    ppermute x6, starting transfers between devices: 8.71 us -> 9.92 us  [swap(): return lax.ppermute(block, axis, route)]
    ppermute x1, starting transfers between devices: 1.98 us -> 2.55 us  [exchange(): from_cross = lax.ppermute(msg_cross, axes, cross)]
  transfers between devices with their start and end apart: 9 -> 9, of which waited for: 3 -> 2; matrix products, arithmetic and copies ran while one was open for 0% -> 0% of each run, Pallas kernels for 20% -> 21%
where the time goes in v5:
time: 38.3 us; the launch traced here: 38 us
  Pallas kernels  16 us (42%)
  starting transfers between devices  14.4 us (38%)
  waiting for transfers between devices  4.57 us (12%)
  between operations  2.7 us (7%)
    ppermute x6, starting transfers between devices, swap(): return lax.ppermute(block, axis, route)  9.92 us
    pallas_call x2, Pallas kernels, mark_links(): pl.pallas_call(functools.partial(mark_kernel, first), name='mark', grid=(...  6.08 us
    pallas_call x1, Pallas kernels, one_step(): pl.pallas_call(force_kernel, name='force', in_specs=[VMEM] * 12, out_spec...  6.08 us
    ppermute x6, waiting for transfers between devices, swap(): return lax.ppermute(block, axis, route)  4.56 us
    ppermute x1, starting transfers between devices, exchange(): from_cross = lax.ppermute(msg_cross, axes, cross)  2.55 us
    ppermute x1, starting transfers between devices, exchange(): from_wrap = lax.ppermute(own_speed, axes, wrap)  1.91 us
    pallas_call x1, Pallas kernels, one_step(): pl.pallas_call(stream_kernel, name='stream', in_specs=[VMEM] * 6, out_spe...  1.76 us
    pallas_call x1, Pallas kernels, one_step(): pl.pallas_call(collide_kernel, name='collide', in_specs=[VMEM, VMEM], out...  1.41 us
  transfers between devices with their start and end apart: 9, of which 2 were waited for; matrix products, arithmetic and copies ran while one was open for 0% of the time, Pallas kernels for 21%

profile of v5, /device:TPU:0, one launch (start us, length us, event | category | flops | bytes accessed | tf_op | source)
XLA Modules:
  0.0 38.0 jit_solution(9692243839846824187)
XLA Ops:
  0.6 0.0 copy-start
  0.6 0.0 copy-start.1
  0.7 0.0 copy-start.2
  0.7 1.4 %collide.1 = (f32[19,8,8,128]{3,2,1,0:T(8,128)S(1)}, f32[8,8,128]{2,1,0:T(8,128)S(1)}, f32[11,8,128]{2,1,0:T(8,128)S(1)}, f32[11,8,128]{2,1,0:T(8,128)S(1)}, f32...) custom-call(f32[19,8,8,128]{3,2,1,0:T(8,128)} %pops.1, f32[3,1,1,64]{3,2,1,0:T(1,128)} %speed.1), custom_call_target="tpu_custom_call" | custom-call | tf_op jit(solution)/shard_map/collide/pallas_call | solution.py:567
  2.1 3.0 %collective-permute-start.24 = (f32[11,8,128]{2,1,0:T(8,128)S(1)}, f32[11,8,128]{2,1,0:T(8,128)S(1)}, u32[]{:S(2)}, u32[]{:S(2)}) collective-permute-start(f32[11,8,128]{2,1,0:T(8,128)S(1)} %get-tuple-element.219), channel_id=1, source_target_pairs={{0,4},{4,0},{8,12},{12,8},{16,20},{20,16},{24,28},{28,24},{1,5},{5... | collective-permute-start | bytes 135176 | tf_op jit(solution)/shard_map/ppermute | solution.py:515
  5.1 3.6 %collective-permute-start.25 = (f32[11,8,128]{2,1,0:T(8,128)S(1)}, f32[11,8,128]{2,1,0:T(8,128)S(1)}, u32[]{:S(2)}, u32[]{:S(2)}) collective-permute-start(f32[11,8,128]{2,1,0:T(8,128)S(1)} %get-tuple-element.220), channel_id=1, source_target_pairs={{0,28},{4,8},{8,4},{12,16},{16,12},{20,24},{24,20},{28,0},{1,29},{... | collective-permute-start | bytes 135176 | tf_op jit(solution)/shard_map/ppermute | solution.py:515
  10.6 0.0 copy-done
  10.6 0.0 copy-done.1
  10.7 0.0 copy-done.2
  10.7 2.7 %mark.17 = f32[576,256]{1,0:T(8,128)S(1)} custom-call(s32[1,1]{1,0:T(1,128)S(6)} %copy.48.count, s32[1,1,16384]{2,1,0:T(1,128)S(1)} %copy-done, s32[1,1,16384]{2,1,0:T(1,128)S(1)} %copy-done.1, s32[1,1,16384]{2,1,0:T(1,128)S(1)} %copy-done.2), custom_call_target="tpu_custom_call" | custom-call | tf_op jit(solution)/shard_map/mark/pallas_call | solution.py:536
  13.4 0.0 collective-permute-done.24.from_near
  13.4 0.0 collective-permute-done.25.from_far
  13.4 0.1 prepare.1
  13.5 8.2 %conditional.1 = (f32[7,8,128]{2,1,0:T(8,128)}, f32[7,8,128]{2,1,0:T(8,128)}, f32[2,8,128]{2,1,0:T(8,128)}, f32[576,256]{1,0:T(8,128)S(1)}) conditional(s32[]{:T(128)} %clamp.3, (f32[7,8,128]{2,1,0:T(8,128)S(1)}, f32[7,8,128]{2,1,0:T(8,128)S(1)}, f32[2,8,128]{2,1,0:T(8,128)S(1)}, s32[1,1]{1,0:T(1,128)}, ...), branch_computations={%region_0.0_spmd, %region_1.0_spmd, %region_2.0_spmd, %region_3.0_... | conditional | bytes 262296 | solution.py:622
  13.7 0.1 collective-permute-start.15
  13.8 2.5 %collective-permute-start.16 = (f32[7,8,128]{2,1,0:T(8,128)S(1)}, f32[7,8,128]{2,1,0:T(8,128)}, u32[]{:S(2)}, u32[]{:S(2)}) collective-permute-start(f32[7,8,128]{2,1,0:T(8,128)S(1)} %get-tuple-element.169), channel_id=1, source_target_pairs={{1,2},{2,1},{23,0},{12,3},{5,6},{6,5},{27,4},{16,7},{9,10},{10,9},... | collective-permute-start | bytes 86024 | tf_op jit(solution)/shard_map/cond/branch_5_fun/ppermute | solution.py:618
  16.4 1.9 %collective-permute-start.17 = (f32[2,8,128]{2,1,0:T(8,128)S(1)}, f32[2,8,128]{2,1,0:T(8,128)}, u32[]{:S(2)}, u32[]{:S(2)}) collective-permute-start(f32[2,8,128]{2,1,0:T(8,128)S(1)} %get-tuple-element.170), channel_id=1, source_target_pairs={{0,3},{3,0},{4,7},{7,4},{8,11},{11,8},{12,15},{15,12},{16,19},{19,... | collective-permute-start | bytes 24584 | tf_op jit(solution)/shard_map/cond/branch_5_fun/ppermute | solution.py:617
  18.3 3.4 %mark.14 = f32[576,256]{1,0:T(8,128)S(1)} custom-call(s32[1,1]{1,0:T(1,128)} %get-tuple-element.171.count, s32[1,1,16384]{2,1,0:T(1,128)S(1)} %get-tuple-element.172.cell, s32[1,1,16384]{2,1,0:T(1,128)S(1)} %get-tuple-element.173.direction, s32[1,1,16384]{2,1,0:T(1,128)S(1)} %get-tuple-element.174.sphere, f32[576,256]{1,0:T(8,128)S(1)} %get-tuple-element.175.refs_0_), custom_call_target="tpu_custom_call" | custom-call | tf_op jit(solution)/shard_map/cond/branch_5_fun/mark/pallas_call | solution.py:536
  21.7 0.0 collective-permute-done.17
  21.7 0.0 collective-permute-done.15
  21.7 0.0 collective-permute-done.16
  21.7 6.1 %force.1 = (f32[18,8,8,128]{3,2,1,0:T(8,128)S(1)}, f32[24,128]{1,0:T(8,128)S(1)}, f32[24,128]{1,0:T(8,128)S(1)}, f32[24,128]{1,0:T(8,128)S(1)}) custom-call(s32[1,1]{1,0:T(1,128)S(6)} %copy.49.pair_count, f32[19,8,8,128]{3,2,1,0:T(8,128)S(1)} %get-tuple-element.215.relaxed, f32[8,8,128]{2,1,0:T(8,128)S(1)} %get-tuple-element.216.density, ...), custom_call_target="tpu_custom_call" | custom-call | tf_op jit(solution)/shard_map/force/pallas_call | solution.py:633
  27.8 1.1 %collective-permute-start.26 = (f32[24,128]{1,0:T(8,128)S(1)}, f32[24,128]{1,0:T(8,128)S(1)}, u32[]{:S(2)}, u32[]{:S(2)}) collective-permute-start(f32[24,128]{1,0:T(8,128)S(1)} %get-tuple-element.230), channel_id=1, source_target_pairs={{0,28},{4,8},{8,4},{12,16},{16,12},{20,24},{24,20},{28,0},{1,29},{... | collective-permute-start | bytes 36872 | tf_op jit(solution)/shard_map/ppermute | solution.py:515
  28.9 1.5 %collective-permute-start.27 = (f32[24,128]{1,0:T(8,128)S(1)}, f32[24,128]{1,0:T(8,128)S(1)}, u32[]{:S(2)}, u32[]{:S(2)}) collective-permute-start(f32[24,128]{1,0:T(8,128)S(1)} %get-tuple-element.231), channel_id=1, source_target_pairs={{0,4},{4,0},{8,12},{12,8},{16,20},{20,16},{24,28},{28,24},{1,5},{5... | collective-permute-start | bytes 36872 | tf_op jit(solution)/shard_map/ppermute | solution.py:515
  30.4 3.9 %collective-permute-done.26 = f32[24,128]{1,0:T(8,128)S(1)} collective-permute-done((f32[24,128]{1,0:T(8,128)S(1)}, f32[24,128]{1,0:T(8,128)S(1)}, u32[]{:S(2)}, u32[]{:S(2)}) %collective-permute-start.26) | collective-permute-done | bytes 12320 | tf_op jit(solution)/shard_map/ppermute | solution.py:515
  34.2 0.0 collective-permute-done.27
  34.3 0.1 collective-permute-start.28
  34.3 0.6 %collective-permute-start.29 = (f32[8,128]{1,0:T(8,128)S(1)}, f32[8,128]{1,0:T(8,128)S(1)}, u32[]{:S(2)}, u32[]{:S(2)}) collective-permute-start(f32[8,128]{1,0:T(8,128)S(1)} %get-tuple-element.235), channel_id=1, source_target_pairs={{0,3},{1,2},{2,1},{3,0},{4,7},{5,6},{6,5},{7,4},{8,11},{9,10},{10,... | collective-permute-start | bytes 12296 | tf_op jit(solution)/shard_map/ppermute | solution.py:515
  35.0 1.8 %stream.1 = f32[19,8,8,128]{3,2,1,0:T(8,128)} custom-call(f32[19,8,8,128]{3,2,1,0:T(8,128)S(1)} %get-tuple-element.215.relaxed, f32[18,8,8,128]{3,2,1,0:T(8,128)S(1)} %get-tuple-element.228.bounced, f32[11,8,128]{2,1,0:T(8,128)S(1)} %collective-permute-done.24.from_near, f32[11,8,128]{2,1,0:T(8,128)S(1)} %collective-permute-done.25.from_far, ...), custom_call_target="tpu_custom_call" | custom-call | tf_op jit(solution)/shard_map/stream/pallas_call | solution.py:653
  36.7 0.0 collective-permute-done.28.one
  36.7 0.7 %collective-permute-done.29.other = f32[8,128]{1,0:T(8,128)S(1)} collective-permute-done((f32[8,128]{1,0:T(8,128)S(1)}, f32[8,128]{1,0:T(8,128)S(1)}, u32[]{:S(2)}, u32[]{:S(2)}) %collective-permute-start.29) | collective-permute-done | bytes 4128 | tf_op jit(solution)/shard_map/ppermute | solution.py:515
  37.4 0.6 %finish.1 = (f32[3,1,1,64]{3,2,1,0:T(1,128)}, f32[3,1,1,64]{3,2,1,0:T(1,128)}) custom-call(f32[8,128]{1,0:T(8,128)S(1)} %get-tuple-element.237.own, f32[8,128]{1,0:T(8,128)S(1)} %collective-permute-done.28.one, f32[8,128]{1,0:T(8,128)S(1)} %collective-permute-done.29.other, f32[3,128]{1,0:T(4,128)S(1)} %get-tuple-element.232.speed), custom_call_target="tpu_custom_call" | custom-call | tf_op jit(solution)/shard_map/finish/pallas_call | solution.py:667
  (2 shorter events, 0.0 us)
Async XLA Ops:
  0.6 10.0 %copy-start = (s32[1,1,16384]{2,1,0:T(1,128)S(1)}, s32[1,1,16384]{2,1,0:T(1,128)}, u32[]{:S(2)}) copy-start(s32[1,1,16384]{2,1,0:T(1,128)} %cell.1) | copy-start | bytes 196612
  0.6 10.0 %copy-start.1 = (s32[1,1,16384]{2,1,0:T(1,128)S(1)}, s32[1,1,16384]{2,1,0:T(1,128)}, u32[]{:S(2)}) copy-start(s32[1,1,16384]{2,1,0:T(1,128)} %direction.1) | copy-start | bytes 196612
  0.7 10.0 %copy-start.2 = (s32[1,1,16384]{2,1,0:T(1,128)S(1)}, s32[1,1,16384]{2,1,0:T(1,128)}, u32[]{:S(2)}) copy-start(s32[1,1,16384]{2,1,0:T(1,128)} %sphere.1) | copy-start | bytes 196612
  2.1 11.3 %collective-permute-start.24 = (f32[11,8,128]{2,1,0:T(8,128)S(1)}, f32[11,8,128]{2,1,0:T(8,128)S(1)}, u32[]{:S(2)}, u32[]{:S(2)}) collective-permute-start(f32[11,8,128]{2,1,0:T(8,128)S(1)} %get-tuple-element.219), channel_id=1, source_target_pairs={{0,4},{4,0},{8,12},{12,8},{16,20},{20,16},{24,28},{28,24},{1,5},{5... | collective-permute-start | bytes 135176 | tf_op jit(solution)/shard_map/ppermute | solution.py:515
  5.1 8.3 %collective-permute-start.25 = (f32[11,8,128]{2,1,0:T(8,128)S(1)}, f32[11,8,128]{2,1,0:T(8,128)S(1)}, u32[]{:S(2)}, u32[]{:S(2)}) collective-permute-start(f32[11,8,128]{2,1,0:T(8,128)S(1)} %get-tuple-element.220), channel_id=1, source_target_pairs={{0,28},{4,8},{8,4},{12,16},{16,12},{20,24},{24,20},{28,0},{1,29},{... | collective-permute-start | bytes 135176 | tf_op jit(solution)/shard_map/ppermute | solution.py:515
  13.7 7.9 %collective-permute-start.15 = (f32[7,8,128]{2,1,0:T(8,128)S(1)}, f32[7,8,128]{2,1,0:T(8,128)}, u32[]{:S(2)}, u32[]{:S(2)}) collective-permute-start(f32[7,8,128]{2,1,0:T(8,128)S(1)} %get-tuple-element.168), channel_id=1, source_target_pairs={{0,1},{1,0},{2,3},{3,2},{4,5},{5,4},{6,7},{7,6},{8,9},{9,8},{10,11... | collective-permute-start | bytes 86024 | tf_op jit(solution)/shard_map/cond/branch_5_fun/ppermute | solution.py:616
  13.8 7.9 %collective-permute-start.16 = (f32[7,8,128]{2,1,0:T(8,128)S(1)}, f32[7,8,128]{2,1,0:T(8,128)}, u32[]{:S(2)}, u32[]{:S(2)}) collective-permute-start(f32[7,8,128]{2,1,0:T(8,128)S(1)} %get-tuple-element.169), channel_id=1, source_target_pairs={{1,2},{2,1},{23,0},{12,3},{5,6},{6,5},{27,4},{16,7},{9,10},{10,9},... | collective-permute-start | bytes 86024 | tf_op jit(solution)/shard_map/cond/branch_5_fun/ppermute | solution.py:618
  16.4 5.3 %collective-permute-start.17 = (f32[2,8,128]{2,1,0:T(8,128)S(1)}, f32[2,8,128]{2,1,0:T(8,128)}, u32[]{:S(2)}, u32[]{:S(2)}) collective-permute-start(f32[2,8,128]{2,1,0:T(8,128)S(1)} %get-tuple-element.170), channel_id=1, source_target_pairs={{0,3},{3,0},{4,7},{7,4},{8,11},{11,8},{12,15},{15,12},{16,19},{19,... | collective-permute-start | bytes 24584 | tf_op jit(solution)/shard_map/cond/branch_5_fun/ppermute | solution.py:617
  27.8 6.5 %collective-permute-start.26 = (f32[24,128]{1,0:T(8,128)S(1)}, f32[24,128]{1,0:T(8,128)S(1)}, u32[]{:S(2)}, u32[]{:S(2)}) collective-permute-start(f32[24,128]{1,0:T(8,128)S(1)} %get-tuple-element.230), channel_id=1, source_target_pairs={{0,28},{4,8},{8,4},{12,16},{16,12},{20,24},{24,20},{28,0},{1,29},{... | collective-permute-start | bytes 36872 | tf_op jit(solution)/shard_map/ppermute | solution.py:515
  28.9 5.3 %collective-permute-start.27 = (f32[24,128]{1,0:T(8,128)S(1)}, f32[24,128]{1,0:T(8,128)S(1)}, u32[]{:S(2)}, u32[]{:S(2)}) collective-permute-start(f32[24,128]{1,0:T(8,128)S(1)} %get-tuple-element.231), channel_id=1, source_target_pairs={{0,4},{4,0},{8,12},{12,8},{16,20},{20,16},{24,28},{28,24},{1,5},{5... | collective-permute-start | bytes 36872 | tf_op jit(solution)/shard_map/ppermute | solution.py:515
  34.3 2.5 %collective-permute-start.28 = (f32[8,128]{1,0:T(8,128)S(1)}, f32[8,128]{1,0:T(8,128)S(1)}, u32[]{:S(2)}, u32[]{:S(2)}) collective-permute-start(f32[8,128]{1,0:T(8,128)S(1)} %get-tuple-element.236), channel_id=1, source_target_pairs={{0,1},{1,0},{2,3},{3,2},{4,5},{5,4},{6,7},{7,6},{8,9},{9,8},{10,11... | collective-permute-start | bytes 12296 | tf_op jit(solution)/shard_map/ppermute | solution.py:515
  34.3 3.1 %collective-permute-start.29 = (f32[8,128]{1,0:T(8,128)S(1)}, f32[8,128]{1,0:T(8,128)S(1)}, u32[]{:S(2)}, u32[]{:S(2)}) collective-permute-start(f32[8,128]{1,0:T(8,128)S(1)} %get-tuple-element.235), channel_id=1, source_target_pairs={{0,3},{1,2},{2,1},{3,0},{4,7},{5,6},{6,5},{7,4},{8,11},{9,10},{10,... | collective-permute-start | bytes 12296 | tf_op jit(solution)/shard_map/ppermute | solution.py:515

commit v6 on v5

--- a/solution.py
+++ b/solution.py
@@ -253,7 +253,7 @@
     width_x = relaxed.shape[1]
     slots = LANES // 2
     even_buffers, odd_buffers, sums = scratch[:4], scratch[4:8], scratch[8]
-    first_of = odd_buffers[0]
+    first_of, second_of = odd_buffers[:2]
     half_rows = marks.shape[0]
     lane = lax.broadcasted_iota(jnp.int32, (1, LANES), 1)
     grad_index = lax.axis_index("grad")
@@ -344,26 +344,23 @@
                     pl.ds(pl.multiple_of(half * LANES, LANES), LANES),
                 ]
                 live = mark > 0.0
-                scaled = mark
-                level = jnp.zeros((SUBS, LANES), F32)
-                for t in range(1, 5):
-                    above = mark > 2.0 ** (8 * t + 6)
-                    scaled = jnp.where(above, mark * 2.0 ** (-8 * t), scaled)
-                    level = jnp.where(above, float(t), level)
-                place = jnp.where(live, scaled - float(LANES), 0.0).astype(jnp.int32)
+                scale = jnp.ones((SUBS, LANES), F32)
+                first = jnp.zeros((SUBS, LANES), F32)
+                levels = [mark > 2.0 ** (8 * t + 6) for t in range(1, 5)]
+                for t, above in enumerate(levels, 1):
+                    scale = jnp.where(above, 2.0 ** (-8 * t), scale)
+                    first = jnp.where(above, 8.0 * t, first)
+                place = (mark * scale).astype(jnp.int32) & (LANES - 1)
                 speed = jnp.take_along_axis(lookup[0], place, axis=1)
-                for t in range(1, 5):
+                for t, above in enumerate(levels, 1):
                     found = jnp.take_along_axis(lookup[t], place, axis=1)
-                    speed = jnp.where(level == float(t), found, speed)
+                    speed = jnp.where(above, found, speed)
                 leaving = relaxed[index + 1, x]
                 back = leaving - weight6 * density[x] * speed
                 bounced[index, x] = jnp.where(live, back, NO_LINK)
                 force = leaving + back
-                if side == 1:
-                    force = -force
-                high_part = place // 16
-                first = jnp.where(live, level * 8.0 + high_part.astype(F32), -1.0)
-                second = (place - 16 * high_part).astype(F32)
+                first = first + (place >> 4).astype(F32)
+                second = (place & 15).astype(F32)
                 where = side * width_x * SUBS + SUBS * x
                 first_of[where : where + SUBS] = first
                 second_of[where : where + SUBS] = second
@@ -373,17 +370,18 @@
                 rest_of[where : where + SUBS] = force - high
 
     def add_up(g, buffers):
-        lefts, rights = [], []
-        for r in range(2 * width_x * SUBS):
-            left, right = slot_rows(buffers, r)
-            lefts.append(left)
-            rights.append(right)
-        sums[g] = lax.dot_general(
-            jnp.concatenate(lefts, axis=1),
-            jnp.concatenate(rights, axis=1),
-            NT,
-            preferred_element_type=F32,
-        )
+        for part in range(2):
+            lefts, rights = [], []
+            for r in range(part * 2 * width_x * SUBS // 2, (part + 1) * 2 * width_x * SUBS // 2):
+                left, right = slot_rows(buffers, r)
+                lefts.append(left)
+                rights.append(right)
+            sums[2 * g + part] = lax.dot_general(
+                jnp.concatenate(rights, axis=1),
+                jnp.concatenate(lefts, axis=1),
+                NT,
+                preferred_element_type=F32,
+            )
 
     look_up(0, even_buffers)
 
@@ -402,14 +400,15 @@
     totals = []
     for k in range(3):
         total = None
-        for g in range(9):
-            c = VELOCITIES[2 * g + 1][k]
+        for direction in range(1, 19):
+            c = VELOCITIES[direction][k]
             if c == 0:
                 continue
+            addend = sums[direction - 1]
             if total is None:
-                total = sums[g] if c > 0 else -sums[g]
+                total = addend if c > 0 else -addend
             else:
-                total = total + sums[g] if c > 0 else total - sums[g]
+                total = total + addend if c > 0 else total - addend
         totals.append(total)
 
     pairs = pair_first.shape[2]
@@ -447,16 +446,18 @@
     left = jnp.concatenate(lefts, axis=1)
     for k in range(3):
         total = totals[k] + lax.dot_general(
-            left, jnp.concatenate(rights[k], axis=1), NT, preferred_element_type=F32
+            jnp.concatenate(rights[k], axis=1), left, NT, preferred_element_type=F32
         )
-        value = total[:, :16] + total[:, 16:32]
-        first_of[0:48] = jnp.concatenate([value, jnp.zeros((48, LANES - 16), F32)], axis=1)
+        first_of[16 * k : 16 * k + 16, 0:48] = total[:16] + total[16:]
+    second_of[...] = first_of[...].T
+    for k in range(3):
         line = None
         for s in range(4):
-            piece = first_of[pl.ds(s, NEAR, stride=4), :]
-            if s:
-                piece = pltpu.roll(piece, 16 * s, axis=1)
-            line = piece if line is None else line + piece
+            piece = second_of[pl.ds(s, NEAR, stride=4), :]
+            shift = 16 * (s - k) % LANES
+            if shift:
+                piece = pltpu.roll(piece, shift, axis=1)
+            line = piece if line is None else jnp.where(lane >= 16 * s, piece, line)
         for g in range(3):
             row = SUBS * g + k
             low, own, high = [line[3 * f + g : 3 * f + g + 1] for f in range(3)]
@@ -639,7 +640,7 @@
         scratch_shapes=[
             pltpu.VMEM((18, SUBS, LANES), F32),
             *[pltpu.VMEM((2 * width_x * SUBS, LANES), F32)] * 8,
-            pltpu.VMEM((9, 48, 32), F32),
+            pltpu.VMEM((18, 32, 48), F32),
         ],
     )(
         pair_count,

time: 38.3 us -> 37.9 us (0.990)
  Pallas kernels: 16 us -> 15.6 us
    pallas_call x1, Pallas kernels: 6.08 us -> 5.69 us  [one_step(): pl.pallas_call(force_kernel, name='force', in_specs=[VMEM] * 12, out_spec...]
where the time goes in v6:
time: 37.9 us; the launch traced here: 37.6 us
  Pallas kernels  15.6 us (41%)
  starting transfers between devices  14.5 us (38%)
  waiting for transfers between devices  4.56 us (12%)
  between operations  2.7 us (7%)
    ppermute x6, starting transfers between devices, swap(): return lax.ppermute(block, axis, route)  9.93 us
    pallas_call x2, Pallas kernels, mark_links(): pl.pallas_call(functools.partial(mark_kernel, first), name='mark', grid=(...  6.08 us
    pallas_call x1, Pallas kernels, one_step(): pl.pallas_call(force_kernel, name='force', in_specs=[VMEM] * 12, out_spec...  5.69 us
    ppermute x6, waiting for transfers between devices, swap(): return lax.ppermute(block, axis, route)  4.55 us
    ppermute x1, starting transfers between devices, exchange(): from_cross = lax.ppermute(msg_cross, axes, cross)  2.55 us
    ppermute x1, starting transfers between devices, exchange(): from_wrap = lax.ppermute(own_speed, axes, wrap)  1.91 us
    pallas_call x1, Pallas kernels, one_step(): pl.pallas_call(stream_kernel, name='stream', in_specs=[VMEM] * 6, out_spe...  1.76 us
    pallas_call x1, Pallas kernels, one_step(): pl.pallas_call(collide_kernel, name='collide', in_specs=[VMEM, VMEM], out...  1.41 us
  transfers between devices with their start and end apart: 9, of which 2 were waited for; matrix products, arithmetic and copies ran while one was open for 0% of the time, Pallas kernels for 21%

profile of v6, /device:TPU:0, one launch (start us, length us, event | category | flops | bytes accessed | tf_op | source)
XLA Modules:
  0.0 37.6 jit_solution(2057198866161066048)
XLA Ops:
  0.6 0.0 copy-start
  0.6 0.0 copy-start.1
  0.7 0.0 copy-start.2
  0.7 1.4 %collide.1 = (f32[19,8,8,128]{3,2,1,0:T(8,128)S(1)}, f32[8,8,128]{2,1,0:T(8,128)S(1)}, f32[11,8,128]{2,1,0:T(8,128)S(1)}, f32[11,8,128]{2,1,0:T(8,128)S(1)}, f32...) custom-call(f32[19,8,8,128]{3,2,1,0:T(8,128)} %pops.1, f32[3,1,1,64]{3,2,1,0:T(1,128)} %speed.1), custom_call_target="tpu_custom_call" | custom-call | tf_op jit(solution)/shard_map/collide/pallas_call | solution.py:568
  2.1 3.0 %collective-permute-start.24 = (f32[11,8,128]{2,1,0:T(8,128)S(1)}, f32[11,8,128]{2,1,0:T(8,128)S(1)}, u32[]{:S(2)}, u32[]{:S(2)}) collective-permute-start(f32[11,8,128]{2,1,0:T(8,128)S(1)} %get-tuple-element.219), channel_id=1, source_target_pairs={{0,4},{4,0},{8,12},{12,8},{16,20},{20,16},{24,28},{28,24},{1,5},{5... | collective-permute-start | bytes 135176 | tf_op jit(solution)/shard_map/ppermute | solution.py:516
  5.1 3.6 %collective-permute-start.25 = (f32[11,8,128]{2,1,0:T(8,128)S(1)}, f32[11,8,128]{2,1,0:T(8,128)S(1)}, u32[]{:S(2)}, u32[]{:S(2)}) collective-permute-start(f32[11,8,128]{2,1,0:T(8,128)S(1)} %get-tuple-element.220), channel_id=1, source_target_pairs={{0,28},{4,8},{8,4},{12,16},{16,12},{20,24},{24,20},{28,0},{1,29},{... | collective-permute-start | bytes 135176 | tf_op jit(solution)/shard_map/ppermute | solution.py:516
  10.6 0.0 copy-done
  10.6 0.0 copy-done.1
  10.7 0.0 copy-done.2
  10.7 2.7 %mark.17 = f32[576,256]{1,0:T(8,128)S(1)} custom-call(s32[1,1]{1,0:T(1,128)S(6)} %copy.48.count, s32[1,1,16384]{2,1,0:T(1,128)S(1)} %copy-done, s32[1,1,16384]{2,1,0:T(1,128)S(1)} %copy-done.1, s32[1,1,16384]{2,1,0:T(1,128)S(1)} %copy-done.2), custom_call_target="tpu_custom_call" | custom-call | tf_op jit(solution)/shard_map/mark/pallas_call | solution.py:537
  13.4 0.0 collective-permute-done.24.from_near
  13.4 0.0 collective-permute-done.25.from_far
  13.4 0.1 prepare.1
  13.5 8.2 %conditional.1 = (f32[7,8,128]{2,1,0:T(8,128)}, f32[7,8,128]{2,1,0:T(8,128)}, f32[2,8,128]{2,1,0:T(8,128)}, f32[576,256]{1,0:T(8,128)S(1)}) conditional(s32[]{:T(128)} %clamp.3, (f32[7,8,128]{2,1,0:T(8,128)S(1)}, f32[7,8,128]{2,1,0:T(8,128)S(1)}, f32[2,8,128]{2,1,0:T(8,128)S(1)}, s32[1,1]{1,0:T(1,128)}, ...), branch_computations={%region_0.0_spmd, %region_1.0_spmd, %region_2.0_spmd, %region_3.0_... | conditional | bytes 262296 | solution.py:623
  13.7 0.1 collective-permute-start.15
  13.8 2.5 %collective-permute-start.16 = (f32[7,8,128]{2,1,0:T(8,128)S(1)}, f32[7,8,128]{2,1,0:T(8,128)}, u32[]{:S(2)}, u32[]{:S(2)}) collective-permute-start(f32[7,8,128]{2,1,0:T(8,128)S(1)} %get-tuple-element.169), channel_id=1, source_target_pairs={{1,2},{2,1},{23,0},{12,3},{5,6},{6,5},{27,4},{16,7},{9,10},{10,9},... | collective-permute-start | bytes 86024 | tf_op jit(solution)/shard_map/cond/branch_5_fun/ppermute | solution.py:619
  16.4 1.9 %collective-permute-start.17 = (f32[2,8,128]{2,1,0:T(8,128)S(1)}, f32[2,8,128]{2,1,0:T(8,128)}, u32[]{:S(2)}, u32[]{:S(2)}) collective-permute-start(f32[2,8,128]{2,1,0:T(8,128)S(1)} %get-tuple-element.170), channel_id=1, source_target_pairs={{0,3},{3,0},{4,7},{7,4},{8,11},{11,8},{12,15},{15,12},{16,19},{19,... | collective-permute-start | bytes 24584 | tf_op jit(solution)/shard_map/cond/branch_5_fun/ppermute | solution.py:618
  18.3 3.4 %mark.14 = f32[576,256]{1,0:T(8,128)S(1)} custom-call(s32[1,1]{1,0:T(1,128)} %get-tuple-element.171.count, s32[1,1,16384]{2,1,0:T(1,128)S(1)} %get-tuple-element.172.cell, s32[1,1,16384]{2,1,0:T(1,128)S(1)} %get-tuple-element.173.direction, s32[1,1,16384]{2,1,0:T(1,128)S(1)} %get-tuple-element.174.sphere, f32[576,256]{1,0:T(8,128)S(1)} %get-tuple-element.175.refs_0_), custom_call_target="tpu_custom_call" | custom-call | tf_op jit(solution)/shard_map/cond/branch_5_fun/mark/pallas_call | solution.py:537
  21.7 0.0 collective-permute-done.17
  21.7 0.0 collective-permute-done.15
  21.7 0.0 collective-permute-done.16
  21.7 5.7 %force.1 = (f32[18,8,8,128]{3,2,1,0:T(8,128)S(1)}, f32[24,128]{1,0:T(8,128)S(1)}, f32[24,128]{1,0:T(8,128)S(1)}, f32[24,128]{1,0:T(8,128)S(1)}) custom-call(s32[1,1]{1,0:T(1,128)S(6)} %copy.49.pair_count, f32[19,8,8,128]{3,2,1,0:T(8,128)S(1)} %get-tuple-element.215.relaxed, f32[8,8,128]{2,1,0:T(8,128)S(1)} %get-tuple-element.216.density, ...), custom_call_target="tpu_custom_call" | custom-call | tf_op jit(solution)/shard_map/force/pallas_call | solution.py:634
  27.4 1.1 %collective-permute-start.26 = (f32[24,128]{1,0:T(8,128)S(1)}, f32[24,128]{1,0:T(8,128)S(1)}, u32[]{:S(2)}, u32[]{:S(2)}) collective-permute-start(f32[24,128]{1,0:T(8,128)S(1)} %get-tuple-element.230), channel_id=1, source_target_pairs={{0,28},{4,8},{8,4},{12,16},{16,12},{20,24},{24,20},{28,0},{1,29},{... | collective-permute-start | bytes 36872 | tf_op jit(solution)/shard_map/ppermute | solution.py:516
  28.5 1.5 %collective-permute-start.27 = (f32[24,128]{1,0:T(8,128)S(1)}, f32[24,128]{1,0:T(8,128)S(1)}, u32[]{:S(2)}, u32[]{:S(2)}) collective-permute-start(f32[24,128]{1,0:T(8,128)S(1)} %get-tuple-element.231), channel_id=1, source_target_pairs={{0,4},{4,0},{8,12},{12,8},{16,20},{20,16},{24,28},{28,24},{1,5},{5... | collective-permute-start | bytes 36872 | tf_op jit(solution)/shard_map/ppermute | solution.py:516
  30.0 3.9 %collective-permute-done.26 = f32[24,128]{1,0:T(8,128)S(1)} collective-permute-done((f32[24,128]{1,0:T(8,128)S(1)}, f32[24,128]{1,0:T(8,128)S(1)}, u32[]{:S(2)}, u32[]{:S(2)}) %collective-permute-start.26) | collective-permute-done | bytes 12320 | tf_op jit(solution)/shard_map/ppermute | solution.py:516
  33.8 0.0 collective-permute-done.27
  33.9 0.1 collective-permute-start.28
  33.9 0.7 %collective-permute-start.29 = (f32[8,128]{1,0:T(8,128)S(1)}, f32[8,128]{1,0:T(8,128)S(1)}, u32[]{:S(2)}, u32[]{:S(2)}) collective-permute-start(f32[8,128]{1,0:T(8,128)S(1)} %get-tuple-element.235), channel_id=1, source_target_pairs={{0,3},{1,2},{2,1},{3,0},{4,7},{5,6},{6,5},{7,4},{8,11},{9,10},{10,... | collective-permute-start | bytes 12296 | tf_op jit(solution)/shard_map/ppermute | solution.py:516
  34.6 1.8 %stream.1 = f32[19,8,8,128]{3,2,1,0:T(8,128)} custom-call(f32[19,8,8,128]{3,2,1,0:T(8,128)S(1)} %get-tuple-element.215.relaxed, f32[18,8,8,128]{3,2,1,0:T(8,128)S(1)} %get-tuple-element.228.bounced, f32[11,8,128]{2,1,0:T(8,128)S(1)} %collective-permute-done.24.from_near, f32[11,8,128]{2,1,0:T(8,128)S(1)} %collective-permute-done.25.from_far, ...), custom_call_target="tpu_custom_call" | custom-call | tf_op jit(solution)/shard_map/stream/pallas_call | solution.py:654
  36.3 0.0 collective-permute-done.28.one
  36.4 0.7 %collective-permute-done.29.other = f32[8,128]{1,0:T(8,128)S(1)} collective-permute-done((f32[8,128]{1,0:T(8,128)S(1)}, f32[8,128]{1,0:T(8,128)S(1)}, u32[]{:S(2)}, u32[]{:S(2)}) %collective-permute-start.29) | collective-permute-done | bytes 4128 | tf_op jit(solution)/shard_map/ppermute | solution.py:516
  37.0 0.6 %finish.1 = (f32[3,1,1,64]{3,2,1,0:T(1,128)}, f32[3,1,1,64]{3,2,1,0:T(1,128)}) custom-call(f32[8,128]{1,0:T(8,128)S(1)} %get-tuple-element.237.own, f32[8,128]{1,0:T(8,128)S(1)} %collective-permute-done.28.one, f32[8,128]{1,0:T(8,128)S(1)} %collective-permute-done.29.other, f32[3,128]{1,0:T(4,128)S(1)} %get-tuple-element.232.speed), custom_call_target="tpu_custom_call" | custom-call | tf_op jit(solution)/shard_map/finish/pallas_call | solution.py:668
  (2 shorter events, 0.0 us)
Async XLA Ops:
  0.6 10.0 %copy-start = (s32[1,1,16384]{2,1,0:T(1,128)S(1)}, s32[1,1,16384]{2,1,0:T(1,128)}, u32[]{:S(2)}) copy-start(s32[1,1,16384]{2,1,0:T(1,128)} %cell.1) | copy-start | bytes 196612
  0.6 10.0 %copy-start.1 = (s32[1,1,16384]{2,1,0:T(1,128)S(1)}, s32[1,1,16384]{2,1,0:T(1,128)}, u32[]{:S(2)}) copy-start(s32[1,1,16384]{2,1,0:T(1,128)} %direction.1) | copy-start | bytes 196612
  0.7 10.0 %copy-start.2 = (s32[1,1,16384]{2,1,0:T(1,128)S(1)}, s32[1,1,16384]{2,1,0:T(1,128)}, u32[]{:S(2)}) copy-start(s32[1,1,16384]{2,1,0:T(1,128)} %sphere.1) | copy-start | bytes 196612
  2.1 11.3 %collective-permute-start.24 = (f32[11,8,128]{2,1,0:T(8,128)S(1)}, f32[11,8,128]{2,1,0:T(8,128)S(1)}, u32[]{:S(2)}, u32[]{:S(2)}) collective-permute-start(f32[11,8,128]{2,1,0:T(8,128)S(1)} %get-tuple-element.219), channel_id=1, source_target_pairs={{0,4},{4,0},{8,12},{12,8},{16,20},{20,16},{24,28},{28,24},{1,5},{5... | collective-permute-start | bytes 135176 | tf_op jit(solution)/shard_map/ppermute | solution.py:516
  5.1 8.3 %collective-permute-start.25 = (f32[11,8,128]{2,1,0:T(8,128)S(1)}, f32[11,8,128]{2,1,0:T(8,128)S(1)}, u32[]{:S(2)}, u32[]{:S(2)}) collective-permute-start(f32[11,8,128]{2,1,0:T(8,128)S(1)} %get-tuple-element.220), channel_id=1, source_target_pairs={{0,28},{4,8},{8,4},{12,16},{16,12},{20,24},{24,20},{28,0},{1,29},{... | collective-permute-start | bytes 135176 | tf_op jit(solution)/shard_map/ppermute | solution.py:516
  13.7 7.9 %collective-permute-start.15 = (f32[7,8,128]{2,1,0:T(8,128)S(1)}, f32[7,8,128]{2,1,0:T(8,128)}, u32[]{:S(2)}, u32[]{:S(2)}) collective-permute-start(f32[7,8,128]{2,1,0:T(8,128)S(1)} %get-tuple-element.168), channel_id=1, source_target_pairs={{0,1},{1,0},{2,3},{3,2},{4,5},{5,4},{6,7},{7,6},{8,9},{9,8},{10,11... | collective-permute-start | bytes 86024 | tf_op jit(solution)/shard_map/cond/branch_5_fun/ppermute | solution.py:617
  13.8 7.9 %collective-permute-start.16 = (f32[7,8,128]{2,1,0:T(8,128)S(1)}, f32[7,8,128]{2,1,0:T(8,128)}, u32[]{:S(2)}, u32[]{:S(2)}) collective-permute-start(f32[7,8,128]{2,1,0:T(8,128)S(1)} %get-tuple-element.169), channel_id=1, source_target_pairs={{1,2},{2,1},{23,0},{12,3},{5,6},{6,5},{27,4},{16,7},{9,10},{10,9},... | collective-permute-start | bytes 86024 | tf_op jit(solution)/shard_map/cond/branch_5_fun/ppermute | solution.py:619
  16.4 5.3 %collective-permute-start.17 = (f32[2,8,128]{2,1,0:T(8,128)S(1)}, f32[2,8,128]{2,1,0:T(8,128)}, u32[]{:S(2)}, u32[]{:S(2)}) collective-permute-start(f32[2,8,128]{2,1,0:T(8,128)S(1)} %get-tuple-element.170), channel_id=1, source_target_pairs={{0,3},{3,0},{4,7},{7,4},{8,11},{11,8},{12,15},{15,12},{16,19},{19,... | collective-permute-start | bytes 24584 | tf_op jit(solution)/shard_map/cond/branch_5_fun/ppermute | solution.py:618
  27.4 6.5 %collective-permute-start.26 = (f32[24,128]{1,0:T(8,128)S(1)}, f32[24,128]{1,0:T(8,128)S(1)}, u32[]{:S(2)}, u32[]{:S(2)}) collective-permute-start(f32[24,128]{1,0:T(8,128)S(1)} %get-tuple-element.230), channel_id=1, source_target_pairs={{0,28},{4,8},{8,4},{12,16},{16,12},{20,24},{24,20},{28,0},{1,29},{... | collective-permute-start | bytes 36872 | tf_op jit(solution)/shard_map/ppermute | solution.py:516
  28.5 5.3 %collective-permute-start.27 = (f32[24,128]{1,0:T(8,128)S(1)}, f32[24,128]{1,0:T(8,128)S(1)}, u32[]{:S(2)}, u32[]{:S(2)}) collective-permute-start(f32[24,128]{1,0:T(8,128)S(1)} %get-tuple-element.231), channel_id=1, source_target_pairs={{0,4},{4,0},{8,12},{12,8},{16,20},{20,16},{24,28},{28,24},{1,5},{5... | collective-permute-start | bytes 36872 | tf_op jit(solution)/shard_map/ppermute | solution.py:516
  33.9 2.5 %collective-permute-start.28 = (f32[8,128]{1,0:T(8,128)S(1)}, f32[8,128]{1,0:T(8,128)S(1)}, u32[]{:S(2)}, u32[]{:S(2)}) collective-permute-start(f32[8,128]{1,0:T(8,128)S(1)} %get-tuple-element.236), channel_id=1, source_target_pairs={{0,1},{1,0},{2,3},{3,2},{4,5},{5,4},{6,7},{7,6},{8,9},{9,8},{10,11... | collective-permute-start | bytes 12296 | tf_op jit(solution)/shard_map/ppermute | solution.py:516
  33.9 3.1 %collective-permute-start.29 = (f32[8,128]{1,0:T(8,128)S(1)}, f32[8,128]{1,0:T(8,128)S(1)}, u32[]{:S(2)}, u32[]{:S(2)}) collective-permute-start(f32[8,128]{1,0:T(8,128)S(1)} %get-tuple-element.235), channel_id=1, source_target_pairs={{0,3},{1,2},{2,1},{3,0},{4,7},{5,6},{6,5},{7,4},{8,11},{9,10},{10,... | collective-permute-start | bytes 12296 | tf_op jit(solution)/shard_map/ppermute | solution.py:516

commit v7 on v6

--- a/solution.py
+++ b/solution.py
@@ -178,8 +178,7 @@
     return value.astype(F32).astype(BF16)
 
 
-def mark_kernel(first_step, count, cell, direction, sphere, *refs):
-    marks = refs[-1]
+def mark_kernel(count, cell, direction, sphere, marks):
     step = pl.program_id(0)
     width = cell.shape[2]
     half_rows = marks.shape[0]
@@ -189,7 +188,7 @@
     z = q % LANES
     half = (row >= half_rows).astype(jnp.int32)
     row = row - half * half_rows
-    number = (first_step + step) * width + lax.broadcasted_iota(jnp.int32, (1, width), 1)
+    number = step * width + lax.broadcasted_iota(jnp.int32, (1, width), 1)
     level = ref // LANES
     scale = jnp.where(level == 0, 1.0, 0.0)
     for t in range(1, 5):
@@ -218,7 +217,7 @@
 
     @pl.when(step == 0)
     def _():
-        marks[...] = refs[0][...] + part if len(refs) == 2 else part
+        marks[...] = part
 
     @pl.when(step > 0)
     def _():
@@ -528,20 +527,18 @@
     return [pltpu.with_memory_space_constraint(array, pltpu.VMEM) for array in arrays]
 
 
-def mark_links(first, steps, half_rows, count, link_arrays, *before):
+def mark_links(half_rows, count, link_arrays):
     links = link_arrays[0].shape[2]
     width = links // 2
-    link_spec = pl.BlockSpec((1, 1, width), lambda i: (0, 0, i + first))
-    whole = pl.BlockSpec((half_rows, 2 * LANES), lambda i: (0, 0))
-    one = pl.BlockSpec((1, 1), lambda i: (0, 0))
+    link_spec = pl.BlockSpec((1, 1, width), lambda i: (0, 0, i))
     return pl.pallas_call(
-        functools.partial(mark_kernel, first),
+        mark_kernel,
         name="mark",
-        grid=(steps,),
-        in_specs=[one, link_spec, link_spec, link_spec] + [whole] * len(before),
-        out_specs=whole,
+        grid=(links // width,),
+        in_specs=[pl.BlockSpec((1, 1), lambda i: (0, 0)), link_spec, link_spec, link_spec],
+        out_specs=pl.BlockSpec((half_rows, 2 * LANES), lambda i: (0, 0)),
         out_shape=local_of(half_rows, 2 * LANES),
-    )(count, *link_arrays, *local(*before))
+    )(count, *link_arrays)
 
 
 def one_step(
@@ -586,8 +583,6 @@
 
     half_rows = 9 * width_x * width_y
     link_arrays = [link_cell, link_dir, link_sphere]
-    marks = mark_links(0, 1, half_rows, link_count, link_arrays)
-
     msg_pair, msg_cross, own_speed = pl.pallas_call(
         prepare_kernel,
         name="prepare",
@@ -601,7 +596,7 @@
         scratch_shapes=[pltpu.VMEM((10, 3 * SUBS, LANES), F32)],
     )(le_offset.reshape(1, 1), *local(right_msg, left_msg, from_near, from_far))
 
-    def exchange(hops, msg_pair, msg_cross, own_speed, marks, link_count, *link_arrays):
+    def exchange(hops, msg_pair, msg_cross, own_speed, link_count, *link_arrays):
         top = grad_count - 1
         pairs, cross, wrap = [], [], []
         for a in range(flow_count):
@@ -617,7 +612,7 @@
         from_pair = lax.ppermute(msg_pair, axes, pairs)
         from_wrap = lax.ppermute(own_speed, axes, wrap)
         from_cross = lax.ppermute(msg_cross, axes, cross)
-        marks = mark_links(1, 1, half_rows, link_count, link_arrays, marks)
+        marks = mark_links(half_rows, link_count, link_arrays)
         return from_pair, from_cross, from_wrap, marks
 
     from_pair, from_cross, from_wrap, marks = lax.switch(
@@ -626,7 +621,6 @@
         msg_pair,
         msg_cross,
         own_speed,
-        marks,
         link_count,
         *link_arrays,
     )

time: 37.9 us -> 40 us (1.055)
  starting transfers between devices: 14.5 us -> 15.4 us
  local copies, waits for them, and re-layouts: 0.01 us -> 0.77 us
  waiting for transfers between devices: 4.56 us -> 5.26 us
  between operations: 2.7 us -> 2.03 us
    ppermute x6, starting transfers between devices: 9.93 us -> 11.7 us  [swap(): return lax.ppermute(block, axis, route)]
    unnamed x6, local copies, waits for them, and re-layouts: 0.01 us -> 0.77 us
    ppermute x1, starting transfers between devices: 2.55 us -> 1.83 us  [exchange(): from_cross = lax.ppermute(msg_cross, axes, cross)]
    ppermute x6, waiting for transfers between devices: 4.55 us -> 5.26 us  [swap(): return lax.ppermute(block, axis, route)]
    pallas_call x2 -> x1, Pallas kernels: 6.08 us -> 6.18 us  [mark_links(): pl.pallas_call(mark_kernel, name='mark', grid=(links // width,), in_specs...]
  transfers between devices with their start and end apart: 9 -> 9, of which waited for: 2 -> 4; matrix products, arithmetic and copies ran while one was open for 0% -> 0% of each run, Pallas kernels for 21% -> 20%
where the time goes in v7:
time: 40 us; the launch traced here: 39.6 us
  Pallas kernels  15.6 us (39%)
  starting transfers between devices  15.4 us (38%)
  waiting for transfers between devices  5.26 us (13%)
  between operations  2.03 us (5%)
  local copies, waits for them, and re-layouts  0.77 us (2%)
  loops' own time  0.44 us (1%)
    ppermute x6, starting transfers between devices, swap(): return lax.ppermute(block, axis, route)  11.7 us
    pallas_call x1, Pallas kernels, mark_links(): pl.pallas_call(mark_kernel, name='mark', grid=(links // width,), in_specs...  6.18 us
    pallas_call x1, Pallas kernels, one_step(): pl.pallas_call(force_kernel, name='force', in_specs=[VMEM] * 12, out_spec...  5.68 us
    ppermute x6, waiting for transfers between devices, swap(): return lax.ppermute(block, axis, route)  5.26 us
    ppermute x1, starting transfers between devices, exchange(): from_wrap = lax.ppermute(own_speed, axes, wrap)  1.91 us
    ppermute x1, starting transfers between devices, exchange(): from_cross = lax.ppermute(msg_cross, axes, cross)  1.83 us
    pallas_call x1, Pallas kernels, one_step(): pl.pallas_call(stream_kernel, name='stream', in_specs=[VMEM] * 6, out_spe...  1.75 us
    pallas_call x1, Pallas kernels, one_step(): pl.pallas_call(collide_kernel, name='collide', in_specs=[VMEM, VMEM], out...  1.36 us
  transfers between devices with their start and end apart: 9, of which 4 were waited for; matrix products, arithmetic and copies ran while one was open for 0% of the time, Pallas kernels for 20%

profile of v7, /device:TPU:0, one launch (start us, length us, event | category | flops | bytes accessed | tf_op | source)
XLA Modules:
  0.0 39.6 jit_solution(2381642091439274669)
XLA Ops:
  0.6 1.4 %collide.1 = (f32[19,8,8,128]{3,2,1,0:T(8,128)S(1)}, f32[8,8,128]{2,1,0:T(8,128)S(1)}, f32[11,8,128]{2,1,0:T(8,128)S(1)}, f32[11,8,128]{2,1,0:T(8,128)S(1)}, f32...) custom-call(f32[19,8,8,128]{3,2,1,0:T(8,128)} %pops.1, f32[3,1,1,64]{3,2,1,0:T(1,128)} %speed.1), custom_call_target="tpu_custom_call" | custom-call | tf_op jit(solution)/shard_map/collide/pallas_call | solution.py:565
  2.0 3.0 %collective-permute-start.24 = (f32[11,8,128]{2,1,0:T(8,128)S(1)}, f32[11,8,128]{2,1,0:T(8,128)S(1)}, u32[]{:S(2)}, u32[]{:S(2)}) collective-permute-start(f32[11,8,128]{2,1,0:T(8,128)S(1)} %get-tuple-element.195), channel_id=1, source_target_pairs={{0,4},{4,0},{8,12},{12,8},{16,20},{20,16},{24,28},{28,24},{1,5},{5... | collective-permute-start | bytes 135176 | tf_op jit(solution)/shard_map/ppermute | solution.py:515
  5.0 3.6 %collective-permute-start.25 = (f32[11,8,128]{2,1,0:T(8,128)S(1)}, f32[11,8,128]{2,1,0:T(8,128)S(1)}, u32[]{:S(2)}, u32[]{:S(2)}) collective-permute-start(f32[11,8,128]{2,1,0:T(8,128)S(1)} %get-tuple-element.196), channel_id=1, source_target_pairs={{0,28},{4,8},{8,4},{12,16},{16,12},{20,24},{24,20},{28,0},{1,29},{... | collective-permute-start | bytes 135176 | tf_op jit(solution)/shard_map/ppermute | solution.py:515
  9.3 0.0 copy-start.2
  10.0 0.0 collective-permute-done.24.from_near
  10.0 1.8 %collective-permute-done.25.from_far = f32[11,8,128]{2,1,0:T(8,128)S(1)} collective-permute-done((f32[11,8,128]{2,1,0:T(8,128)S(1)}, f32[11,8,128]{2,1,0:T(8,128)S(1)}, u32[]{:S(2)}, u32[]{:S(2)}) %collective-permute-start.25) | collective-permute-done | bytes 45088 | tf_op jit(solution)/shard_map/ppermute | solution.py:515
  11.8 0.0 copy-start
  11.8 0.0 copy-start.1
  11.8 0.1 prepare.1
  11.9 0.0 copy-done.2
  11.9 0.7 %copy-done = s32[1,1,16384]{2,1,0:T(1,128)S(1)} copy-done((s32[1,1,16384]{2,1,0:T(1,128)S(1)}, s32[1,1,16384]{2,1,0:T(1,128)}, u32[]{:S(2)}) %copy-start) | copy-done | bytes 65560
  12.6 0.0 copy-done.1
  12.6 10.4 %conditional.1 = (f32[7,8,128]{2,1,0:T(8,128)}, f32[7,8,128]{2,1,0:T(8,128)}, f32[2,8,128]{2,1,0:T(8,128)}, f32[576,256]{1,0:T(8,128)S(1)}) conditional(s32[]{:T(128)} %clamp.3, (f32[7,8,128]{2,1,0:T(8,128)S(1)}, f32[7,8,128]{2,1,0:T(8,128)S(1)}, f32[2,8,128]{2,1,0:T(8,128)S(1)}, s32[1,1]{1,0:T(1,128)}, ...), branch_computations={%region_0.0_spmd, %region_1.0_spmd, %region_2.0_spmd, %region_3.0_... | conditional | bytes 262296 | solution.py:618
  12.6 0.0 collective-permute-start.15
  12.6 1.8 %collective-permute-start.16 = (f32[7,8,128]{2,1,0:T(8,128)S(1)}, f32[7,8,128]{2,1,0:T(8,128)}, u32[]{:S(2)}, u32[]{:S(2)}) collective-permute-start(f32[7,8,128]{2,1,0:T(8,128)S(1)} %get-tuple-element.148), channel_id=1, source_target_pairs={{1,2},{2,1},{23,0},{12,3},{5,6},{6,5},{27,4},{16,7},{9,10},{10,9},... | collective-permute-start | bytes 86024 | tf_op jit(solution)/shard_map/cond/branch_5_fun/ppermute | solution.py:614
  14.5 1.9 %collective-permute-start.17 = (f32[2,8,128]{2,1,0:T(8,128)S(1)}, f32[2,8,128]{2,1,0:T(8,128)}, u32[]{:S(2)}, u32[]{:S(2)}) collective-permute-start(f32[2,8,128]{2,1,0:T(8,128)S(1)} %get-tuple-element.149), channel_id=1, source_target_pairs={{0,3},{3,0},{4,7},{7,4},{8,11},{11,8},{12,15},{15,12},{16,19},{19,... | collective-permute-start | bytes 24584 | tf_op jit(solution)/shard_map/cond/branch_5_fun/ppermute | solution.py:613
  16.4 6.2 %mark.13 = f32[576,256]{1,0:T(8,128)S(1)} custom-call(s32[1,1]{1,0:T(1,128)} %get-tuple-element.150.count, s32[1,1,16384]{2,1,0:T(1,128)S(1)} %get-tuple-element.151.cell, s32[1,1,16384]{2,1,0:T(1,128)S(1)} %get-tuple-element.152.direction, s32[1,1,16384]{2,1,0:T(1,128)S(1)} %get-tuple-element.153.sphere), custom_call_target="tpu_custom_call" | custom-call | tf_op jit(solution)/shard_map/cond/branch_5_fun/mark/pallas_call | solution.py:534
  22.6 0.0 collective-permute-done.17
  22.6 0.0 collective-permute-done.15
  22.6 0.0 collective-permute-done.16
  23.0 5.7 %force.1 = (f32[18,8,8,128]{3,2,1,0:T(8,128)S(1)}, f32[24,128]{1,0:T(8,128)S(1)}, f32[24,128]{1,0:T(8,128)S(1)}, f32[24,128]{1,0:T(8,128)S(1)}) custom-call(s32[1,1]{1,0:T(1,128)S(6)} %copy.48.pair_count, f32[19,8,8,128]{3,2,1,0:T(8,128)S(1)} %get-tuple-element.191.relaxed, f32[8,8,128]{2,1,0:T(8,128)S(1)} %get-tuple-element.192.density, ...), custom_call_target="tpu_custom_call" | custom-call | tf_op jit(solution)/shard_map/force/pallas_call | solution.py:628
  28.7 3.4 %collective-permute-start.26 = (f32[24,128]{1,0:T(8,128)S(1)}, f32[24,128]{1,0:T(8,128)S(1)}, u32[]{:S(2)}, u32[]{:S(2)}) collective-permute-start(f32[24,128]{1,0:T(8,128)S(1)} %get-tuple-element.206), channel_id=1, source_target_pairs={{0,28},{4,8},{8,4},{12,16},{16,12},{20,24},{24,20},{28,0},{1,29},{... | collective-permute-start | bytes 36872 | tf_op jit(solution)/shard_map/ppermute | solution.py:515
  32.1 1.5 %collective-permute-start.27 = (f32[24,128]{1,0:T(8,128)S(1)}, f32[24,128]{1,0:T(8,128)S(1)}, u32[]{:S(2)}, u32[]{:S(2)}) collective-permute-start(f32[24,128]{1,0:T(8,128)S(1)} %get-tuple-element.207), channel_id=1, source_target_pairs={{0,4},{4,0},{8,12},{12,8},{16,20},{20,16},{24,28},{28,24},{1,5},{5... | collective-permute-start | bytes 36872 | tf_op jit(solution)/shard_map/ppermute | solution.py:515
  33.6 1.5 %collective-permute-done.26 = f32[24,128]{1,0:T(8,128)S(1)} collective-permute-done((f32[24,128]{1,0:T(8,128)S(1)}, f32[24,128]{1,0:T(8,128)S(1)}, u32[]{:S(2)}, u32[]{:S(2)}) %collective-permute-start.26) | collective-permute-done | bytes 12320 | tf_op jit(solution)/shard_map/ppermute | solution.py:515
  35.2 0.7 %collective-permute-done.27 = f32[24,128]{1,0:T(8,128)S(1)} collective-permute-done((f32[24,128]{1,0:T(8,128)S(1)}, f32[24,128]{1,0:T(8,128)S(1)}, u32[]{:S(2)}, u32[]{:S(2)}) %collective-permute-start.27) | collective-permute-done | bytes 12320 | tf_op jit(solution)/shard_map/ppermute | solution.py:515
  35.9 0.1 collective-permute-start.28
  35.9 0.1 collective-permute-start.29
  36.0 1.8 %stream.1 = f32[19,8,8,128]{3,2,1,0:T(8,128)} custom-call(f32[19,8,8,128]{3,2,1,0:T(8,128)S(1)} %get-tuple-element.191.relaxed, f32[18,8,8,128]{3,2,1,0:T(8,128)S(1)} %get-tuple-element.204.bounced, f32[11,8,128]{2,1,0:T(8,128)S(1)} %collective-permute-done.24.from_near, f32[11,8,128]{2,1,0:T(8,128)S(1)} %collective-permute-done.25.from_far, ...), custom_call_target="tpu_custom_call" | custom-call | tf_op jit(solution)/shard_map/stream/pallas_call | solution.py:648
  37.8 0.0 collective-permute-done.28.one
  37.8 1.2 %collective-permute-done.29.other = f32[8,128]{1,0:T(8,128)S(1)} collective-permute-done((f32[8,128]{1,0:T(8,128)S(1)}, f32[8,128]{1,0:T(8,128)S(1)}, u32[]{:S(2)}, u32[]{:S(2)}) %collective-permute-start.29) | collective-permute-done | bytes 4128 | tf_op jit(solution)/shard_map/ppermute | solution.py:515
  39.0 0.6 %finish.1 = (f32[3,1,1,64]{3,2,1,0:T(1,128)}, f32[3,1,1,64]{3,2,1,0:T(1,128)}) custom-call(f32[8,128]{1,0:T(8,128)S(1)} %get-tuple-element.213.own, f32[8,128]{1,0:T(8,128)S(1)} %collective-permute-done.28.one, f32[8,128]{1,0:T(8,128)S(1)} %collective-permute-done.29.other, f32[3,128]{1,0:T(4,128)S(1)} %get-tuple-element.208.speed), custom_call_target="tpu_custom_call" | custom-call | tf_op jit(solution)/shard_map/finish/pallas_call | solution.py:662
  (2 shorter events, 0.0 us)
Async XLA Ops:
  2.0 8.0 %collective-permute-start.24 = (f32[11,8,128]{2,1,0:T(8,128)S(1)}, f32[11,8,128]{2,1,0:T(8,128)S(1)}, u32[]{:S(2)}, u32[]{:S(2)}) collective-permute-start(f32[11,8,128]{2,1,0:T(8,128)S(1)} %get-tuple-element.195), channel_id=1, source_target_pairs={{0,4},{4,0},{8,12},{12,8},{16,20},{20,16},{24,28},{28,24},{1,5},{5... | collective-permute-start | bytes 135176 | tf_op jit(solution)/shard_map/ppermute | solution.py:515
  5.0 6.7 %collective-permute-start.25 = (f32[11,8,128]{2,1,0:T(8,128)S(1)}, f32[11,8,128]{2,1,0:T(8,128)S(1)}, u32[]{:S(2)}, u32[]{:S(2)}) collective-permute-start(f32[11,8,128]{2,1,0:T(8,128)S(1)} %get-tuple-element.196), channel_id=1, source_target_pairs={{0,28},{4,8},{8,4},{12,16},{16,12},{20,24},{24,20},{28,0},{1,29},{... | collective-permute-start | bytes 135176 | tf_op jit(solution)/shard_map/ppermute | solution.py:515
  9.3 2.6 %copy-start.2 = (s32[1,1,16384]{2,1,0:T(1,128)S(1)}, s32[1,1,16384]{2,1,0:T(1,128)}, u32[]{:S(2)}) copy-start(s32[1,1,16384]{2,1,0:T(1,128)} %param.25) | copy-start | bytes 196612
  11.8 0.8 %copy-start = (s32[1,1,16384]{2,1,0:T(1,128)S(1)}, s32[1,1,16384]{2,1,0:T(1,128)}, u32[]{:S(2)}) copy-start(s32[1,1,16384]{2,1,0:T(1,128)} %param.23) | copy-start | bytes 196612
  11.8 0.9 %copy-start.1 = (s32[1,1,16384]{2,1,0:T(1,128)S(1)}, s32[1,1,16384]{2,1,0:T(1,128)}, u32[]{:S(2)}) copy-start(s32[1,1,16384]{2,1,0:T(1,128)} %param.24) | copy-start | bytes 196612
  12.6 10.0 %collective-permute-start.15 = (f32[7,8,128]{2,1,0:T(8,128)S(1)}, f32[7,8,128]{2,1,0:T(8,128)}, u32[]{:S(2)}, u32[]{:S(2)}) collective-permute-start(f32[7,8,128]{2,1,0:T(8,128)S(1)} %get-tuple-element.147), channel_id=1, source_target_pairs={{0,1},{1,0},{2,3},{3,2},{4,5},{5,4},{6,7},{7,6},{8,9},{9,8},{10,11... | collective-permute-start | bytes 86024 | tf_op jit(solution)/shard_map/cond/branch_5_fun/ppermute | solution.py:612
  12.6 10.0 %collective-permute-start.16 = (f32[7,8,128]{2,1,0:T(8,128)S(1)}, f32[7,8,128]{2,1,0:T(8,128)}, u32[]{:S(2)}, u32[]{:S(2)}) collective-permute-start(f32[7,8,128]{2,1,0:T(8,128)S(1)} %get-tuple-element.148), channel_id=1, source_target_pairs={{1,2},{2,1},{23,0},{12,3},{5,6},{6,5},{27,4},{16,7},{9,10},{10,9},... | collective-permute-start | bytes 86024 | tf_op jit(solution)/shard_map/cond/branch_5_fun/ppermute | solution.py:614
  14.5 8.1 %collective-permute-start.17 = (f32[2,8,128]{2,1,0:T(8,128)S(1)}, f32[2,8,128]{2,1,0:T(8,128)}, u32[]{:S(2)}, u32[]{:S(2)}) collective-permute-start(f32[2,8,128]{2,1,0:T(8,128)S(1)} %get-tuple-element.149), channel_id=1, source_target_pairs={{0,3},{3,0},{4,7},{7,4},{8,11},{11,8},{12,15},{15,12},{16,19},{19,... | collective-permute-start | bytes 24584 | tf_op jit(solution)/shard_map/cond/branch_5_fun/ppermute | solution.py:613
  28.7 6.5 %collective-permute-start.26 = (f32[24,128]{1,0:T(8,128)S(1)}, f32[24,128]{1,0:T(8,128)S(1)}, u32[]{:S(2)}, u32[]{:S(2)}) collective-permute-start(f32[24,128]{1,0:T(8,128)S(1)} %get-tuple-element.206), channel_id=1, source_target_pairs={{0,28},{4,8},{8,4},{12,16},{16,12},{20,24},{24,20},{28,0},{1,29},{... | collective-permute-start | bytes 36872 | tf_op jit(solution)/shard_map/ppermute | solution.py:515
  32.1 3.7 %collective-permute-start.27 = (f32[24,128]{1,0:T(8,128)S(1)}, f32[24,128]{1,0:T(8,128)S(1)}, u32[]{:S(2)}, u32[]{:S(2)}) collective-permute-start(f32[24,128]{1,0:T(8,128)S(1)} %get-tuple-element.207), channel_id=1, source_target_pairs={{0,4},{4,0},{8,12},{12,8},{16,20},{20,16},{24,28},{28,24},{1,5},{5... | collective-permute-start | bytes 36872 | tf_op jit(solution)/shard_map/ppermute | solution.py:515
  35.9 1.9 %collective-permute-start.28 = (f32[8,128]{1,0:T(8,128)S(1)}, f32[8,128]{1,0:T(8,128)S(1)}, u32[]{:S(2)}, u32[]{:S(2)}) collective-permute-start(f32[8,128]{1,0:T(8,128)S(1)} %get-tuple-element.212), channel_id=1, source_target_pairs={{0,1},{1,0},{2,3},{3,2},{4,5},{5,4},{6,7},{7,6},{8,9},{9,8},{10,11... | collective-permute-start | bytes 12296 | tf_op jit(solution)/shard_map/ppermute | solution.py:515
  35.9 3.1 %collective-permute-start.29 = (f32[8,128]{1,0:T(8,128)S(1)}, f32[8,128]{1,0:T(8,128)S(1)}, u32[]{:S(2)}, u32[]{:S(2)}) collective-permute-start(f32[8,128]{1,0:T(8,128)S(1)} %get-tuple-element.211), channel_id=1, source_target_pairs={{0,3},{1,2},{2,1},{3,0},{4,7},{5,6},{6,5},{7,4},{8,11},{9,10},{10,... | collective-permute-start | bytes 12296 | tf_op jit(solution)/shard_map/ppermute | solution.py:515

commit v8 on v6

--- a/solution.py
+++ b/solution.py
@@ -111,8 +111,9 @@
 
 def sort_sides(axis, near, far):
     even = lax.rem(lax.axis_index(axis), 2) == 0
-    near = [near[i] for i in range(near.shape[0])]
-    far = [far[i] for i in range(far.shape[0])]
+    count = len(far) if isinstance(far, list) else far.shape[0]
+    near = [near[i] for i in range(count)]
+    far = [far[i] for i in range(count)]
     lower = [jnp.where(even, q, p) for p, q in zip(near, far)]
     higher = [jnp.where(even, p, q) for p, q in zip(near, far)]
     return lower, higher
@@ -238,7 +239,6 @@
     own_speed,
     from_pair,
     from_cross,
-    from_wrap,
     pair_first,
     pair_second,
     pair_gap,
@@ -259,11 +259,10 @@
     grad_index = lax.axis_index("grad")
     even = lax.rem(grad_index, 2) == 0
     even_flow = lax.rem(lax.axis_index("flow"), 2) == 0
-    at_edge = (grad_index == 0) | (grad_index == lax.axis_size("grad") - 1)
     sources = [[], [], []]
     for tile in range(2):
         near = from_pair[5 + tile]
-        far = jnp.where(at_edge, from_wrap[tile], from_cross[5 + tile])
+        far = from_cross[5 + tile]
         sources[0].append(jnp.where(even, far, near))
         sources[1].append(own_speed[tile])
         sources[2].append(jnp.where(even, near, far))
@@ -466,9 +465,13 @@
             to_far[row : row + 1, :] = jnp.where(even_flow, low, high)
 
 
-def stream_kernel(relaxed, bounced, from_near, from_far, from_pair, from_cross, out):
+def stream_kernel(relaxed, bounced, from_near, from_far, from_pair, from_cross, displaced, out):
     from_left, from_right = sort_sides("flow", from_near, from_far)
-    low_rows, high_rows = sort_sides("grad", from_pair, from_cross)
+    grad_index = lax.axis_index("grad")
+    at_edge = (grad_index == 0) | (grad_index == lax.axis_size("grad") - 1)
+    low_rows, high_rows = sort_sides(
+        "grad", from_pair, [jnp.where(at_edge, displaced[i], from_cross[i]) for i in range(5)]
+    )
     width_x, width_y = relaxed.shape[1], relaxed.shape[2]
     for direction, (cx, cy, cz) in enumerate(VELOCITIES):
         for x in range(width_x):
@@ -516,6 +519,16 @@
     return lax.ppermute(block, axis, route)
 
 
+def displaced_route(flow_count, grad_count, hops):
+    top = grad_count - 1
+    route = []
+    for a in range(flow_count):
+        line = a * grad_count
+        route.append(((a + hops) % flow_count * grad_count + top, line))
+        route.append(((a - hops) % flow_count * grad_count, line + top))
+    return route
+
+
 def shape_of(*dims):
     return jax.ShapeDtypeStruct(dims, F32)
 
@@ -601,40 +614,14 @@
         scratch_shapes=[pltpu.VMEM((10, 3 * SUBS, LANES), F32)],
     )(le_offset.reshape(1, 1), *local(right_msg, left_msg, from_near, from_far))
 
-    def exchange(hops, msg_pair, msg_cross, own_speed, marks, link_count, *link_arrays):
-        top = grad_count - 1
-        pairs, cross, wrap = [], [], []
-        for a in range(flow_count):
-            line = a * grad_count
-            for b in range(grad_count):
-                pairs.append((line + b, line + (b ^ 1)))
-                if 0 < b < top:
-                    cross.append((line + b, line + b + (1 if b % 2 else -1)))
-            cross.append(((a + hops) % flow_count * grad_count + top, line))
-            cross.append(((a - hops) % flow_count * grad_count, line + top))
-            wrap += [(line, line + top), (line + top, line)]
-        axes = ("flow", "grad")
-        from_pair = lax.ppermute(msg_pair, axes, pairs)
-        from_wrap = lax.ppermute(own_speed, axes, wrap)
-        from_cross = lax.ppermute(msg_cross, axes, cross)
-        marks = mark_links(1, 1, half_rows, link_count, link_arrays, marks)
-        return from_pair, from_cross, from_wrap, marks
-
-    from_pair, from_cross, from_wrap, marks = lax.switch(
-        lax.div(le_offset[0], width_x),
-        [functools.partial(exchange, hops) for hops in range(flow_count)],
-        msg_pair,
-        msg_cross,
-        own_speed,
-        marks,
-        link_count,
-        *link_arrays,
-    )
+    from_pair = swap(msg_pair, "grad", False)
+    from_cross = swap(msg_cross, "grad", True)
+    marks = mark_links(1, 1, half_rows, link_count, link_arrays, marks)
 
     bounced, to_near, to_self, to_far = pl.pallas_call(
         force_kernel,
         name="force",
-        in_specs=[VMEM] * 12,
+        in_specs=[VMEM] * 11,
         out_specs=[VMEM] * 4,
         out_shape=[local_of(18, width_x, width_y, depth)] + [local_of(3 * SUBS, LANES)] * 3,
         scratch_shapes=[
@@ -644,20 +631,22 @@
         ],
     )(
         pair_count,
-        *local(relaxed, density, marks, own_speed, from_pair, from_cross, from_wrap),
+        *local(relaxed, density, marks, own_speed, from_pair, from_cross),
         pair_first,
         pair_second,
         pair_gap,
         pair_normal,
     )
 
-    updated = pl.pallas_call(
-        stream_kernel,
-        name="stream",
-        in_specs=[VMEM] * 6,
-        out_specs=VMEM,
-        out_shape=shape_of(19, width_x, width_y, depth),
-    )(*local(relaxed, bounced, from_near, from_far, from_pair, from_cross))
+    def displace(hops, block):
+        return lax.ppermute(block, ("flow", "grad"), displaced_route(flow_count, grad_count, hops))
+
+    late_cross, _ = lax.optimization_barrier((msg_cross, to_self))
+    displaced = lax.switch(
+        lax.div(le_offset[0], width_x),
+        [functools.partial(displace, hops) for hops in range(flow_count)],
+        late_cross,
+    )
 
     column = to_self + swap(to_far, "flow", True) + swap(to_near, "flow", False)
     even = lax.axis_index("grad") % 2 == 0
@@ -672,6 +661,14 @@
         out_specs=[VMEM] * 2,
         out_shape=[line, line],
     )(*local(column[SUBS : 2 * SUBS], from_pair_force, from_cross_force, own_line))
+
+    updated = pl.pallas_call(
+        stream_kernel,
+        name="stream",
+        in_specs=[VMEM] * 7,
+        out_specs=VMEM,
+        out_shape=shape_of(19, width_x, width_y, depth),
+    )(*local(relaxed, bounced, from_near, from_far, from_pair, from_cross, displaced))
 
     return updated, sphere_force, velocity_next
 

time: 37.9 us -> 46.3 us (1.22)
  waiting for transfers between devices: 4.56 us -> 12 us
  Pallas kernels: 15.6 us -> 16.4 us
    ppermute x3 -> x1, waiting for transfers between devices: 0.01 us -> 5.74 us  [displace(): lax.ppermute(block, ('flow', 'grad'), displaced_route(flow_count, grad_co...]
    ppermute x6 -> x8, starting transfers between devices: 9.93 us -> 12.6 us  [swap(): return lax.ppermute(block, axis, route)]
    ppermute x3 -> x1, starting transfers between devices: 4.53 us -> 2.23 us  [displace(): lax.ppermute(block, ('flow', 'grad'), displaced_route(flow_count, grad_co...]
    ppermute x6 -> x8, waiting for transfers between devices: 4.55 us -> 6.21 us  [swap(): return lax.ppermute(block, axis, route)]
    pallas_call x2, Pallas kernels: 6.08 us -> 7.01 us  [mark_links(): pl.pallas_call(functools.partial(mark_kernel, first), name='mark', grid=(...]
  transfers between devices with their start and end apart: 9 -> 9, of which waited for: 2 -> 4; matrix products, arithmetic and copies ran while one was open for 0% -> 0% of each run, Pallas kernels for 21% -> 19%
where the time goes in v8:
time: 46.3 us; the launch traced here: 45.9 us
  Pallas kernels  16.4 us (35%)
  starting transfers between devices  14.8 us (32%)
  waiting for transfers between devices  12 us (26%)
  between operations  2.66 us (6%)
    ppermute x8, starting transfers between devices, swap(): return lax.ppermute(block, axis, route)  12.6 us
    pallas_call x2, Pallas kernels, mark_links(): pl.pallas_call(functools.partial(mark_kernel, first), name='mark', grid=(...  7.01 us
    ppermute x8, waiting for transfers between devices, swap(): return lax.ppermute(block, axis, route)  6.21 us
    ppermute x1, waiting for transfers between devices, displace(): lax.ppermute(block, ('flow', 'grad'), displaced_route(flow_count, grad_co...  5.74 us
    pallas_call x1, Pallas kernels, one_step(): pl.pallas_call(force_kernel, name='force', in_specs=[VMEM] * 11, out_spec...  5.61 us
    ppermute x1, starting transfers between devices, displace(): lax.ppermute(block, ('flow', 'grad'), displaced_route(flow_count, grad_co...  2.23 us
    pallas_call x1, Pallas kernels, one_step(): pl.pallas_call(stream_kernel, name='stream', in_specs=[VMEM] * 7, out_spe...  1.74 us
    pallas_call x1, Pallas kernels, one_step(): pl.pallas_call(collide_kernel, name='collide', in_specs=[VMEM, VMEM], out...  1.36 us
  transfers between devices with their start and end apart: 9, of which 4 were waited for; matrix products, arithmetic and copies ran while one was open for 0% of the time, Pallas kernels for 19%

profile of v8, /device:TPU:0, one launch (start us, length us, event | category | flops | bytes accessed | tf_op | source)
XLA Modules:
  0.0 45.9 jit_solution(16828234520354250595)
XLA Ops:
  0.6 1.4 %collide.1 = (f32[19,8,8,128]{3,2,1,0:T(8,128)S(1)}, f32[8,8,128]{2,1,0:T(8,128)S(1)}, f32[11,8,128]{2,1,0:T(8,128)S(1)}, f32[11,8,128]{2,1,0:T(8,128)S(1)}, f32...) custom-call(f32[19,8,8,128]{3,2,1,0:T(8,128)} %pops.1, f32[3,1,1,64]{3,2,1,0:T(1,128)} %speed.1), custom_call_target="tpu_custom_call" | custom-call | tf_op jit(solution)/shard_map/collide/pallas_call | solution.py:581
  2.0 3.0 %collective-permute-start.8 = (f32[11,8,128]{2,1,0:T(8,128)S(1)}, f32[11,8,128]{2,1,0:T(8,128)S(1)}, u32[]{:S(2)}, u32[]{:S(2)}) collective-permute-start(f32[11,8,128]{2,1,0:T(8,128)S(1)} %get-tuple-element.41), channel_id=1, source_target_pairs={{0,4},{4,0},{8,12},{12,8},{16,20},{20,16},{24,28},{28,24},{1,5},{5... | collective-permute-start | bytes 135176 | tf_op jit(solution)/shard_map/ppermute | solution.py:519
  5.0 3.6 %collective-permute-start.9 = (f32[11,8,128]{2,1,0:T(8,128)S(1)}, f32[11,8,128]{2,1,0:T(8,128)S(1)}, u32[]{:S(2)}, u32[]{:S(2)}) collective-permute-start(f32[11,8,128]{2,1,0:T(8,128)S(1)} %get-tuple-element.42), channel_id=1, source_target_pairs={{0,28},{4,8},{8,4},{12,16},{16,12},{20,24},{24,20},{28,0},{1,29},{... | collective-permute-start | bytes 135176 | tf_op jit(solution)/shard_map/ppermute | solution.py:519
  9.3 0.0 collective-permute-done.8.from_near
  9.3 2.5 %collective-permute-done.9.from_far = f32[11,8,128]{2,1,0:T(8,128)S(1)} collective-permute-done((f32[11,8,128]{2,1,0:T(8,128)S(1)}, f32[11,8,128]{2,1,0:T(8,128)S(1)}, u32[]{:S(2)}, u32[]{:S(2)}) %collective-permute-start.9) | collective-permute-done | bytes 45088 | tf_op jit(solution)/shard_map/ppermute | solution.py:519
  11.8 0.1 prepare.1
  11.9 0.1 collective-permute-start.11
  12.0 1.6 %collective-permute-start.10 = (f32[7,8,128]{2,1,0:T(8,128)S(1)}, f32[7,8,128]{2,1,0:T(8,128)S(1)}, u32[]{:S(2)}, u32[]{:S(2)}) collective-permute-start(f32[7,8,128]{2,1,0:T(8,128)S(1)} %get-tuple-element.44), channel_id=1, source_target_pairs={{0,1},{1,0},{2,3},{3,2},{4,5},{5,4},{6,7},{7,6},{8,9},{9,8},{10,11... | collective-permute-start | bytes 86024 | tf_op jit(solution)/shard_map/ppermute | solution.py:519
  14.2 3.5 %mark.2.refs_0_ = f32[576,256]{1,0:T(8,128)S(1)} custom-call(s32[1,1]{1,0:T(1,128)S(6)} %copy.24.count, s32[1,1,16384]{2,1,0:T(1,128)} %cell.3, s32[1,1,16384]{2,1,0:T(1,128)} %direction.3, s32[1,1,16384]{2,1,0:T(1,128)} %sphere.3), custom_call_target="tpu_custom_call" | custom-call | tf_op jit(solution)/shard_map/mark/pallas_call | solution.py:550
  17.7 3.5 %mark.3.marks = f32[576,256]{1,0:T(8,128)S(1)} custom-call(s32[1,1]{1,0:T(1,128)S(6)} %copy.24.count, s32[1,1,16384]{2,1,0:T(1,128)} %cell.3, s32[1,1,16384]{2,1,0:T(1,128)} %direction.3, s32[1,1,16384]{2,1,0:T(1,128)} %sphere.3, f32[576,256]{1,0:T(8,128)S(1)} %mark.2.refs_0_), custom_call_target="tpu_custom_call" | custom-call | tf_op jit(solution)/shard_map/mark/pallas_call | solution.py:550
  21.9 0.0 collective-permute-done.11.from_cross
  21.9 0.0 collective-permute-done.10.from_pair
  21.9 5.6 %force.1 = (f32[18,8,8,128]{3,2,1,0:T(8,128)S(1)}, f32[24,128]{1,0:T(8,128)S(1)}, f32[24,128]{1,0:T(8,128)S(1)}, f32[24,128]{1,0:T(8,128)S(1)}) custom-call(s32[1,1]{1,0:T(1,128)S(6)} %copy.25.pair_count, f32[19,8,8,128]{3,2,1,0:T(8,128)S(1)} %get-tuple-element.37.relaxed, f32[8,8,128]{2,1,0:T(8,128)S(1)} %get-tuple-element.38.density, ...), custom_call_target="tpu_custom_call" | custom-call | tf_op jit(solution)/shard_map/force/pallas_call | solution.py:621
  27.5 3.6 %collective-permute-start.12 = (f32[24,128]{1,0:T(8,128)S(1)}, f32[24,128]{1,0:T(8,128)S(1)}, u32[]{:S(2)}, u32[]{:S(2)}) collective-permute-start(f32[24,128]{1,0:T(8,128)S(1)} %get-tuple-element.49), channel_id=1, source_target_pairs={{0,28},{4,8},{8,4},{12,16},{16,12},{20,24},{24,20},{28,0},{1,29},{... | collective-permute-start | bytes 36872 | tf_op jit(solution)/shard_map/ppermute | solution.py:519
  31.2 0.0 collective-permute-start.13
  31.2 2.8 %collective-permute-done.12 = f32[24,128]{1,0:T(8,128)S(1)} collective-permute-done((f32[24,128]{1,0:T(8,128)S(1)}, f32[24,128]{1,0:T(8,128)S(1)}, u32[]{:S(2)}, u32[]{:S(2)}) %collective-permute-start.12) | collective-permute-done | bytes 12320 | tf_op jit(solution)/shard_map/ppermute | solution.py:519
  34.0 0.9 %collective-permute-done.13 = f32[24,128]{1,0:T(8,128)S(1)} collective-permute-done((f32[24,128]{1,0:T(8,128)S(1)}, f32[24,128]{1,0:T(8,128)S(1)}, u32[]{:S(2)}, u32[]{:S(2)}) %collective-permute-start.13) | collective-permute-done | bytes 12320 | tf_op jit(solution)/shard_map/ppermute | solution.py:519
  34.9 0.1 collective-permute-start.14
  35.0 0.6 %collective-permute-start.15 = (f32[8,128]{1,0:T(8,128)S(1)}, f32[8,128]{1,0:T(8,128)S(1)}, u32[]{:S(2)}, u32[]{:S(2)}) collective-permute-start(f32[8,128]{1,0:T(8,128)S(1)} %get-tuple-element.54), channel_id=1, source_target_pairs={{0,3},{1,2},{2,1},{3,0},{4,7},{5,6},{6,5},{7,4},{8,11},{9,10},{10,... | collective-permute-start | bytes 12296 | tf_op jit(solution)/shard_map/ppermute | solution.py:519
  35.6 8.0 %conditional.1 = (f32[7,8,128]{2,1,0:T(8,128)}) conditional(s32[]{:T(128)} %clamp.3, f32[7,8,128]{2,1,0:T(8,128)S(1)} %get-tuple-element.48, f32[7,8,128]{2,1,0:T(8,128)S(1)} %get-tuple-element.48, f32[7,8,128]{2,1,0:T(8,128)S(1)} %get-tuple-element.48, f32[7,8,128]{2,1,0:T(8,128)S(1)} %get-tuple-element.48, ...), branch_computations={%region_0.0_spmd, %region_1.0_spmd, %region_2.0_spmd, %region_3.0_... | conditional | bytes 114736 | solution.py:645
  35.6 2.2 %collective-permute-start.5 = (f32[7,8,128]{2,1,0:T(8,128)S(1)}, f32[7,8,128]{2,1,0:T(8,128)}, u32[]{:S(2)}, u32[]{:S(2)}) collective-permute-start(f32[7,8,128]{2,1,0:T(8,128)S(1)} %param.5), channel_id=1, source_target_pairs={{23,0},{12,3},{27,4},{16,7},{31,8},{20,11},{3,12},{24,15},{7,16},{... | collective-permute-start | bytes 86024 | tf_op jit(solution)/shard_map/cond/branch_5_fun/ppermute | solution.py:642
  37.8 5.7 %collective-permute-done.5 = f32[7,8,128]{2,1,0:T(8,128)} collective-permute-done((f32[7,8,128]{2,1,0:T(8,128)S(1)}, f32[7,8,128]{2,1,0:T(8,128)}, u32[]{:S(2)}, u32[]{:S(2)}) %collective-permute-start.5) | collective-permute-done | bytes 28704 | tf_op jit(solution)/shard_map/cond/branch_5_fun/ppermute | solution.py:642
  43.6 1.7 %stream.1 = f32[19,8,8,128]{3,2,1,0:T(8,128)} custom-call(f32[19,8,8,128]{3,2,1,0:T(8,128)S(1)} %get-tuple-element.37.relaxed, f32[18,8,8,128]{3,2,1,0:T(8,128)S(1)} %get-tuple-element.46.bounced, f32[11,8,128]{2,1,0:T(8,128)S(1)} %collective-permute-done.8.from_near, f32[11,8,128]{2,1,0:T(8,128)S(1)} %collective-permute-done.9.from_far, ...), custom_call_target="tpu_custom_call" | custom-call | tf_op jit(solution)/shard_map/stream/pallas_call | solution.py:665
  45.3 0.0 collective-permute-done.14.one
  45.3 0.0 collective-permute-done.15.other
  45.3 0.6 %finish.1 = (f32[3,1,1,64]{3,2,1,0:T(1,128)}, f32[3,1,1,64]{3,2,1,0:T(1,128)}) custom-call(f32[8,128]{1,0:T(8,128)S(1)} %get-tuple-element.56.own, f32[8,128]{1,0:T(8,128)S(1)} %collective-permute-done.14.one, f32[8,128]{1,0:T(8,128)S(1)} %collective-permute-done.15.other, f32[3,128]{1,0:T(4,128)S(1)} %get-tuple-element.51.speed), custom_call_target="tpu_custom_call" | custom-call | tf_op jit(solution)/shard_map/finish/pallas_call | solution.py:657
  (2 shorter events, 0.0 us)
Async XLA Ops:
  2.0 7.3 %collective-permute-start.8 = (f32[11,8,128]{2,1,0:T(8,128)S(1)}, f32[11,8,128]{2,1,0:T(8,128)S(1)}, u32[]{:S(2)}, u32[]{:S(2)}) collective-permute-start(f32[11,8,128]{2,1,0:T(8,128)S(1)} %get-tuple-element.41), channel_id=1, source_target_pairs={{0,4},{4,0},{8,12},{12,8},{16,20},{20,16},{24,28},{28,24},{1,5},{5... | collective-permute-start | bytes 135176 | tf_op jit(solution)/shard_map/ppermute | solution.py:519
  5.0 6.7 %collective-permute-start.9 = (f32[11,8,128]{2,1,0:T(8,128)S(1)}, f32[11,8,128]{2,1,0:T(8,128)S(1)}, u32[]{:S(2)}, u32[]{:S(2)}) collective-permute-start(f32[11,8,128]{2,1,0:T(8,128)S(1)} %get-tuple-element.42), channel_id=1, source_target_pairs={{0,28},{4,8},{8,4},{12,16},{16,12},{20,24},{24,20},{28,0},{1,29},{... | collective-permute-start | bytes 135176 | tf_op jit(solution)/shard_map/ppermute | solution.py:519
  11.9 10.0 %collective-permute-start.11 = (f32[7,8,128]{2,1,0:T(8,128)S(1)}, f32[7,8,128]{2,1,0:T(8,128)S(1)}, u32[]{:S(2)}, u32[]{:S(2)}) collective-permute-start(f32[7,8,128]{2,1,0:T(8,128)S(1)} %get-tuple-element.48), channel_id=1, source_target_pairs={{0,3},{1,2},{2,1},{3,0},{4,7},{5,6},{6,5},{7,4},{8,11},{9,10},{10,... | collective-permute-start | bytes 86024 | tf_op jit(solution)/shard_map/ppermute | solution.py:519
  12.0 10.0 %collective-permute-start.10 = (f32[7,8,128]{2,1,0:T(8,128)S(1)}, f32[7,8,128]{2,1,0:T(8,128)S(1)}, u32[]{:S(2)}, u32[]{:S(2)}) collective-permute-start(f32[7,8,128]{2,1,0:T(8,128)S(1)} %get-tuple-element.44), channel_id=1, source_target_pairs={{0,1},{1,0},{2,3},{3,2},{4,5},{5,4},{6,7},{7,6},{8,9},{9,8},{10,11... | collective-permute-start | bytes 86024 | tf_op jit(solution)/shard_map/ppermute | solution.py:519
  27.5 6.5 %collective-permute-start.12 = (f32[24,128]{1,0:T(8,128)S(1)}, f32[24,128]{1,0:T(8,128)S(1)}, u32[]{:S(2)}, u32[]{:S(2)}) collective-permute-start(f32[24,128]{1,0:T(8,128)S(1)} %get-tuple-element.49), channel_id=1, source_target_pairs={{0,28},{4,8},{8,4},{12,16},{16,12},{20,24},{24,20},{28,0},{1,29},{... | collective-permute-start | bytes 36872 | tf_op jit(solution)/shard_map/ppermute | solution.py:519
  31.2 3.7 %collective-permute-start.13 = (f32[24,128]{1,0:T(8,128)S(1)}, f32[24,128]{1,0:T(8,128)S(1)}, u32[]{:S(2)}, u32[]{:S(2)}) collective-permute-start(f32[24,128]{1,0:T(8,128)S(1)} %get-tuple-element.50), channel_id=1, source_target_pairs={{0,4},{4,0},{8,12},{12,8},{16,20},{20,16},{24,28},{28,24},{1,5},{5... | collective-permute-start | bytes 36872 | tf_op jit(solution)/shard_map/ppermute | solution.py:519
  34.9 10.4 %collective-permute-start.14 = (f32[8,128]{1,0:T(8,128)S(1)}, f32[8,128]{1,0:T(8,128)S(1)}, u32[]{:S(2)}, u32[]{:S(2)}) collective-permute-start(f32[8,128]{1,0:T(8,128)S(1)} %get-tuple-element.55), channel_id=1, source_target_pairs={{0,1},{1,0},{2,3},{3,2},{4,5},{5,4},{6,7},{7,6},{8,9},{9,8},{10,11... | collective-permute-start | bytes 12296 | tf_op jit(solution)/shard_map/ppermute | solution.py:519
  35.0 10.3 %collective-permute-start.15 = (f32[8,128]{1,0:T(8,128)S(1)}, f32[8,128]{1,0:T(8,128)S(1)}, u32[]{:S(2)}, u32[]{:S(2)}) collective-permute-start(f32[8,128]{1,0:T(8,128)S(1)} %get-tuple-element.54), channel_id=1, source_target_pairs={{0,3},{1,2},{2,1},{3,0},{4,7},{5,6},{6,5},{7,4},{8,11},{9,10},{10,... | collective-permute-start | bytes 12296 | tf_op jit(solution)/shard_map/ppermute | solution.py:519
  35.6 8.0 %collective-permute-start.5 = (f32[7,8,128]{2,1,0:T(8,128)S(1)}, f32[7,8,128]{2,1,0:T(8,128)}, u32[]{:S(2)}, u32[]{:S(2)}) collective-permute-start(f32[7,8,128]{2,1,0:T(8,128)S(1)} %param.5), channel_id=1, source_target_pairs={{23,0},{12,3},{27,4},{16,7},{31,8},{20,11},{3,12},{24,15},{7,16},{... | collective-permute-start | bytes 86024 | tf_op jit(solution)/shard_map/cond/branch_5_fun/ppermute | solution.py:642

commit v9 on v8

--- a/solution.py
+++ b/solution.py
@@ -638,39 +638,50 @@
         pair_normal,
     )
 
-    def displace(hops, block):
-        return lax.ppermute(block, ("flow", "grad"), displaced_route(flow_count, grad_count, hops))
-
-    late_cross, _ = lax.optimization_barrier((msg_cross, to_self))
-    displaced = lax.switch(
+    def tail(hops, to_near, to_self, to_far, msg_cross, own_line, *fields):
+        far = swap(to_far, "flow", True)
+        near = swap(to_near, "flow", False)
+        route = displaced_route(flow_count, grad_count, hops)
+        displaced = lax.ppermute(msg_cross, ("flow", "grad"), route)
+        column = to_self + far + near
+        even = lax.axis_index("grad") % 2 == 0
+        low, high = column[:SUBS], column[2 * SUBS :]
+        to_cross = jnp.where(even, low, high)
+        to_pair = jnp.where(even, high, low)
+        from_pair_force = swap(to_pair, "grad", False)
+        from_cross_force = swap(to_cross, "grad", True)
+        updated = pl.pallas_call(
+            stream_kernel,
+            name="stream",
+            in_specs=[VMEM] * 7,
+            out_specs=VMEM,
+            out_shape=shape_of(19, width_x, width_y, depth),
+        )(*local(*fields, displaced))
+        line = shape_of(3, 1, 1, slots)
+        sphere_force, velocity_next = pl.pallas_call(
+            finish_kernel,
+            name="finish",
+            in_specs=[VMEM] * 4,
+            out_specs=[VMEM] * 2,
+            out_shape=[line, line],
+        )(*local(column[SUBS : 2 * SUBS], from_pair_force, from_cross_force, own_line))
+        return updated, sphere_force, velocity_next
+
+    return lax.switch(
         lax.div(le_offset[0], width_x),
-        [functools.partial(displace, hops) for hops in range(flow_count)],
-        late_cross,
+        [functools.partial(tail, hops) for hops in range(flow_count)],
+        to_near,
+        to_self,
+        to_far,
+        msg_cross,
+        own_line,
+        relaxed,
+        bounced,
+        from_near,
+        from_far,
+        from_pair,
+        from_cross,
     )
-
-    column = to_self + swap(to_far, "flow", True) + swap(to_near, "flow", False)
-    even = lax.axis_index("grad") % 2 == 0
-    low, high = column[:SUBS], column[2 * SUBS :]
-    from_cross_force = swap(jnp.where(even, low, high), "grad", True)
-    from_pair_force = swap(jnp.where(even, high, low), "grad", False)
-    line = shape_of(3, 1, 1, slots)
-    sphere_force, velocity_next = pl.pallas_call(
-        finish_kernel,
-        name="finish",
-        in_specs=[VMEM] * 4,
-        out_specs=[VMEM] * 2,
-        out_shape=[line, line],
-    )(*local(column[SUBS : 2 * SUBS], from_pair_force, from_cross_force, own_line))
-
-    updated = pl.pallas_call(
-        stream_kernel,
-        name="stream",
-        in_specs=[VMEM] * 7,
-        out_specs=VMEM,
-        out_shape=shape_of(19, width_x, width_y, depth),
-    )(*local(relaxed, bounced, from_near, from_far, from_pair, from_cross, displaced))
-
-    return updated, sphere_force, velocity_next
 
 
 def solution(mesh):

time: 46.3 us -> 40.5 us (0.87)
  waiting for transfers between devices: 12 us -> 7.75 us
  Pallas kernels: 16.4 us -> 14.3 us
  local copies, waits for them, and re-layouts: 0 us -> 0.83 us
    ppermute x1, waiting for transfers between devices: 5.74 us -> 1.06 us  [tail(): displaced = lax.ppermute(msg_cross, ('flow', 'grad'), route)]
    pallas_call x2, Pallas kernels: 2.31 us -> 0.18 us  [the longest x1 0.18 us: tail(): pl.pallas_call(stream_kernel, name='stream', in_specs=[VMEM] * 7, out_spe...]
    unnamed x0 -> x6, local copies, waits for them, and re-layouts: none -> 0.83 us
    ppermute x8, waiting for transfers between devices: 6.21 us -> 6.69 us  [swap(): return lax.ppermute(block, axis, route)]
  transfers between devices with their start and end apart: 9 -> 9, of which waited for: 4 -> 5; matrix products, arithmetic and copies ran while one was open for 0% -> 0% of each run, Pallas kernels for 19% -> 17%
where the time goes in v9:
time: 40.5 us; the launch traced here: 40.2 us
  starting transfers between devices  14.5 us (36%)
  Pallas kernels  14.3 us (35%)
  waiting for transfers between devices  7.75 us (19%)
  between operations  2.69 us (7%)
  local copies, waits for them, and re-layouts  0.83 us (2%)
    ppermute x8, starting transfers between devices, swap(): return lax.ppermute(block, axis, route)  12.6 us
    pallas_call x2, Pallas kernels, mark_links(): pl.pallas_call(functools.partial(mark_kernel, first), name='mark', grid=(...  7.01 us
    ppermute x8, waiting for transfers between devices, swap(): return lax.ppermute(block, axis, route)  6.69 us
    pallas_call x1, Pallas kernels, one_step(): pl.pallas_call(force_kernel, name='force', in_specs=[VMEM] * 11, out_spec...  5.61 us
    ppermute x1, starting transfers between devices, tail(): displaced = lax.ppermute(msg_cross, ('flow', 'grad'), route)  1.91 us
    pallas_call x1, Pallas kernels, one_step(): pl.pallas_call(collide_kernel, name='collide', in_specs=[VMEM, VMEM], out...  1.36 us
    ppermute x1, waiting for transfers between devices, tail(): displaced = lax.ppermute(msg_cross, ('flow', 'grad'), route)  1.06 us
    unnamed x6, local copies, waits for them, and re-layouts  0.83 us
  transfers between devices with their start and end apart: 9, of which 5 were waited for; matrix products, arithmetic and copies ran while one was open for 0% of the time, Pallas kernels for 17%

profile of v9, /device:TPU:0, one launch (start us, length us, event | category | flops | bytes accessed | tf_op | source)
XLA Modules:
  0.0 40.2 jit_solution(3533114218987385319)
XLA Ops:
  0.6 1.4 %collide.1 = (f32[19,8,8,128]{3,2,1,0:T(8,128)S(1)}, f32[8,8,128]{2,1,0:T(8,128)S(1)}, f32[11,8,128]{2,1,0:T(8,128)S(1)}, f32[11,8,128]{2,1,0:T(8,128)S(1)}, f32...) custom-call(f32[19,8,8,128]{3,2,1,0:T(8,128)} %pops.1, f32[3,1,1,64]{3,2,1,0:T(1,128)} %speed.1), custom_call_target="tpu_custom_call" | custom-call | tf_op jit(solution)/shard_map/collide/pallas_call | solution.py:581
  2.0 3.0 %collective-permute-start.40 = (f32[11,8,128]{2,1,0:T(8,128)S(1)}, f32[11,8,128]{2,1,0:T(8,128)S(1)}, u32[]{:S(2)}, u32[]{:S(2)}) collective-permute-start(f32[11,8,128]{2,1,0:T(8,128)S(1)} %get-tuple-element.299), channel_id=1, source_target_pairs={{0,4},{4,0},{8,12},{12,8},{16,20},{20,16},{24,28},{28,24},{1,5},{5... | collective-permute-start | bytes 135176 | tf_op jit(solution)/shard_map/ppermute | solution.py:519
  5.0 3.6 %collective-permute-start.41 = (f32[11,8,128]{2,1,0:T(8,128)S(1)}, f32[11,8,128]{2,1,0:T(8,128)S(1)}, u32[]{:S(2)}, u32[]{:S(2)}) collective-permute-start(f32[11,8,128]{2,1,0:T(8,128)S(1)} %get-tuple-element.300), channel_id=1, source_target_pairs={{0,28},{4,8},{8,4},{12,16},{16,12},{20,24},{24,20},{28,0},{1,29},{... | collective-permute-start | bytes 135176 | tf_op jit(solution)/shard_map/ppermute | solution.py:519
  9.3 0.0 collective-permute-done.40.from_near
  9.3 2.5 %collective-permute-done.41.from_far = f32[11,8,128]{2,1,0:T(8,128)S(1)} collective-permute-done((f32[11,8,128]{2,1,0:T(8,128)S(1)}, f32[11,8,128]{2,1,0:T(8,128)S(1)}, u32[]{:S(2)}, u32[]{:S(2)}) %collective-permute-start.41) | collective-permute-done | bytes 45088 | tf_op jit(solution)/shard_map/ppermute | solution.py:519
  11.8 0.1 prepare.1
  11.9 0.1 collective-permute-start.42
  11.9 1.6 %collective-permute-start.43 = (f32[7,8,128]{2,1,0:T(8,128)S(1)}, f32[7,8,128]{2,1,0:T(8,128)S(1)}, u32[]{:S(2)}, u32[]{:S(2)}) collective-permute-start(f32[7,8,128]{2,1,0:T(8,128)S(1)} %get-tuple-element.301), channel_id=1, source_target_pairs={{0,3},{1,2},{2,1},{3,0},{4,7},{5,6},{6,5},{7,4},{8,11},{9,10},{10,... | collective-permute-start | bytes 86024 | tf_op jit(solution)/shard_map/ppermute | solution.py:519
  14.9 3.5 %mark.2.refs_0_ = f32[576,256]{1,0:T(8,128)S(1)} custom-call(s32[1,1]{1,0:T(1,128)S(6)} %copy.48.count, s32[1,1,16384]{2,1,0:T(1,128)} %cell.3, s32[1,1,16384]{2,1,0:T(1,128)} %direction.3, s32[1,1,16384]{2,1,0:T(1,128)} %sphere.3), custom_call_target="tpu_custom_call" | custom-call | tf_op jit(solution)/shard_map/mark/pallas_call | solution.py:550
  18.4 3.5 %mark.3.marks = f32[576,256]{1,0:T(8,128)S(1)} custom-call(s32[1,1]{1,0:T(1,128)S(6)} %copy.48.count, s32[1,1,16384]{2,1,0:T(1,128)} %cell.3, s32[1,1,16384]{2,1,0:T(1,128)} %direction.3, s32[1,1,16384]{2,1,0:T(1,128)} %sphere.3, f32[576,256]{1,0:T(8,128)S(1)} %mark.2.refs_0_), custom_call_target="tpu_custom_call" | custom-call | tf_op jit(solution)/shard_map/mark/pallas_call | solution.py:550
  21.9 0.0 collective-permute-done.42.from_pair
  21.9 0.0 collective-permute-done.43.from_cross
  21.9 5.6 %force.1 = (f32[18,8,8,128]{3,2,1,0:T(8,128)S(1)}, f32[24,128]{1,0:T(8,128)S(1)}, f32[24,128]{1,0:T(8,128)S(1)}, f32[24,128]{1,0:T(8,128)S(1)}) custom-call(s32[1,1]{1,0:T(1,128)S(6)} %copy.49.pair_count, f32[19,8,8,128]{3,2,1,0:T(8,128)S(1)} %get-tuple-element.302.relaxed, f32[8,8,128]{2,1,0:T(8,128)S(1)} %get-tuple-element.303.density, ...), custom_call_target="tpu_custom_call" | custom-call | tf_op jit(solution)/shard_map/force/pallas_call | solution.py:621
  27.6 11.7 %conditional.1 = (f32[3,1,1,64]{3,2,1,0:T(1,128)S(1)}, f32[3,1,1,64]{3,2,1,0:T(1,128)S(1)}, f32[19,8,8,128]{3,2,1,0:T(8,128)S(1)}) conditional(s32[]{:T(128)} %clamp.3, (f32[7,8,128]{2,1,0:T(8,128)S(1)}, f32[19,8,8,128]{3,2,1,0:T(8,128)S(1)}, f32[18,8,8,128]{3,2,1,0:T(8,128)S(1)}, f32[11,8,128]{2,1,0:T(8,128)S(1)}, ...), branch_computations={%region_0.1_spmd, %region_1.2_spmd, %region_2.3_spmd, %region_3.4_... | conditional | flops 8206 | bytes 319851 | solution.py:670
  27.6 3.6 %collective-permute-start.26 = (f32[24,128]{1,0:T(8,128)S(1)}, f32[24,128]{1,0:T(8,128)S(1)}, u32[]{:S(2)}, u32[]{:S(2)}) collective-permute-start(f32[24,128]{1,0:T(8,128)S(1)} %get-tuple-element.249), channel_id=1, source_target_pairs={{0,28},{4,8},{8,4},{12,16},{16,12},{20,24},{24,20},{28,0},{1,29},{... | collective-permute-start | bytes 36872 | tf_op jit(solution)/shard_map/cond/branch_5_fun/ppermute | solution.py:519
  31.2 0.0 collective-permute-start.27
  31.2 1.9 %collective-permute-start.25 = (f32[7,8,128]{2,1,0:T(8,128)S(1)}, f32[7,8,128]{2,1,0:T(8,128)S(1)}, u32[]{:S(2)}, u32[]{:S(2)}) collective-permute-start(f32[7,8,128]{2,1,0:T(8,128)S(1)} %get-tuple-element.247), channel_id=1, source_target_pairs={{23,0},{12,3},{27,4},{16,7},{31,8},{20,11},{3,12},{24,15},{7,16},{... | collective-permute-start | bytes 86024 | tf_op jit(solution)/shard_map/cond/branch_5_fun/ppermute | solution.py:645
  33.2 0.9 %collective-permute-done.26 = f32[24,128]{1,0:T(8,128)S(1)} collective-permute-done((f32[24,128]{1,0:T(8,128)S(1)}, f32[24,128]{1,0:T(8,128)S(1)}, u32[]{:S(2)}, u32[]{:S(2)}) %collective-permute-start.26) | collective-permute-done | bytes 12320 | tf_op jit(solution)/shard_map/cond/branch_5_fun/ppermute | solution.py:519
  34.1 0.9 %collective-permute-done.27 = f32[24,128]{1,0:T(8,128)S(1)} collective-permute-done((f32[24,128]{1,0:T(8,128)S(1)}, f32[24,128]{1,0:T(8,128)S(1)}, u32[]{:S(2)}, u32[]{:S(2)}) %collective-permute-start.27) | collective-permute-done | bytes 12320 | tf_op jit(solution)/shard_map/cond/branch_5_fun/ppermute | solution.py:519
  34.9 0.1 collective-permute-start.29
  35.0 0.6 %collective-permute-start.28 = (f32[8,128]{1,0:T(8,128)S(1)}, f32[8,128]{1,0:T(8,128)S(1)}, u32[]{:S(2)}, u32[]{:S(2)}) collective-permute-start(f32[8,128]{1,0:T(8,128)S(1)} %get-tuple-element.328), channel_id=1, source_target_pairs={{0,1},{1,0},{2,3},{3,2},{4,5},{5,4},{6,7},{7,6},{8,9},{9,8},{10,11... | collective-permute-start | bytes 12296 | tf_op jit(solution)/shard_map/cond/branch_5_fun/ppermute | solution.py:519
  35.6 2.4 %collective-permute-done.29.other = f32[8,128]{1,0:T(8,128)S(1)} collective-permute-done((f32[8,128]{1,0:T(8,128)S(1)}, f32[8,128]{1,0:T(8,128)S(1)}, u32[]{:S(2)}, u32[]{:S(2)}) %collective-permute-start.29) | collective-permute-done | bytes 4128 | tf_op jit(solution)/shard_map/cond/branch_5_fun/ppermute | solution.py:519
  38.0 0.0 collective-permute-done.28.one
  38.0 1.1 %collective-permute-done.25.displaced = f32[7,8,128]{2,1,0:T(8,128)S(1)} collective-permute-done((f32[7,8,128]{2,1,0:T(8,128)S(1)}, f32[7,8,128]{2,1,0:T(8,128)S(1)}, u32[]{:S(2)}, u32[]{:S(2)}) %collective-permute-start.25) | collective-permute-done | bytes 28704 | tf_op jit(solution)/shard_map/cond/branch_5_fun/ppermute | solution.py:645
  39.1 0.2 stream.13
  39.3 0.0 copy-start.1
  39.3 0.0 copy-start.2
  39.3 0.0 copy-start
  39.3 0.5 %copy-done.1 = f32[3,1,1,64]{3,2,1,0:T(1,128)} copy-done((f32[3,1,1,64]{3,2,1,0:T(1,128)}, f32[3,1,1,64]{3,2,1,0:T(1,128)S(1)}, u32[]{:S(2)}) %copy-start.1) | copy-done | bytes 792
  39.9 0.0 copy-done.2
  39.9 0.3 copy-done
  (3 shorter events, 0.0 us)
Async XLA Ops:
  2.0 7.3 %collective-permute-start.40 = (f32[11,8,128]{2,1,0:T(8,128)S(1)}, f32[11,8,128]{2,1,0:T(8,128)S(1)}, u32[]{:S(2)}, u32[]{:S(2)}) collective-permute-start(f32[11,8,128]{2,1,0:T(8,128)S(1)} %get-tuple-element.299), channel_id=1, source_target_pairs={{0,4},{4,0},{8,12},{12,8},{16,20},{20,16},{24,28},{28,24},{1,5},{5... | collective-permute-start | bytes 135176 | tf_op jit(solution)/shard_map/ppermute | solution.py:519
  5.0 6.7 %collective-permute-start.41 = (f32[11,8,128]{2,1,0:T(8,128)S(1)}, f32[11,8,128]{2,1,0:T(8,128)S(1)}, u32[]{:S(2)}, u32[]{:S(2)}) collective-permute-start(f32[11,8,128]{2,1,0:T(8,128)S(1)} %get-tuple-element.300), channel_id=1, source_target_pairs={{0,28},{4,8},{8,4},{12,16},{16,12},{20,24},{24,20},{28,0},{1,29},{... | collective-permute-start | bytes 135176 | tf_op jit(solution)/shard_map/ppermute | solution.py:519
  11.9 10.0 %collective-permute-start.42 = (f32[7,8,128]{2,1,0:T(8,128)S(1)}, f32[7,8,128]{2,1,0:T(8,128)S(1)}, u32[]{:S(2)}, u32[]{:S(2)}) collective-permute-start(f32[7,8,128]{2,1,0:T(8,128)S(1)} %get-tuple-element.305), channel_id=1, source_target_pairs={{0,1},{1,0},{2,3},{3,2},{4,5},{5,4},{6,7},{7,6},{8,9},{9,8},{10,11... | collective-permute-start | bytes 86024 | tf_op jit(solution)/shard_map/ppermute | solution.py:519
  11.9 10.0 %collective-permute-start.43 = (f32[7,8,128]{2,1,0:T(8,128)S(1)}, f32[7,8,128]{2,1,0:T(8,128)S(1)}, u32[]{:S(2)}, u32[]{:S(2)}) collective-permute-start(f32[7,8,128]{2,1,0:T(8,128)S(1)} %get-tuple-element.301), channel_id=1, source_target_pairs={{0,3},{1,2},{2,1},{3,0},{4,7},{5,6},{6,5},{7,4},{8,11},{9,10},{10,... | collective-permute-start | bytes 86024 | tf_op jit(solution)/shard_map/ppermute | solution.py:519
  27.6 6.5 %collective-permute-start.26 = (f32[24,128]{1,0:T(8,128)S(1)}, f32[24,128]{1,0:T(8,128)S(1)}, u32[]{:S(2)}, u32[]{:S(2)}) collective-permute-start(f32[24,128]{1,0:T(8,128)S(1)} %get-tuple-element.249), channel_id=1, source_target_pairs={{0,28},{4,8},{8,4},{12,16},{16,12},{20,24},{24,20},{28,0},{1,29},{... | collective-permute-start | bytes 36872 | tf_op jit(solution)/shard_map/cond/branch_5_fun/ppermute | solution.py:519
  31.2 3.7 %collective-permute-start.27 = (f32[24,128]{1,0:T(8,128)S(1)}, f32[24,128]{1,0:T(8,128)S(1)}, u32[]{:S(2)}, u32[]{:S(2)}) collective-permute-start(f32[24,128]{1,0:T(8,128)S(1)} %get-tuple-element.250), channel_id=1, source_target_pairs={{0,4},{4,0},{8,12},{12,8},{16,20},{20,16},{24,28},{28,24},{1,5},{5... | collective-permute-start | bytes 36872 | tf_op jit(solution)/shard_map/cond/branch_5_fun/ppermute | solution.py:519
  31.2 7.9 %collective-permute-start.25 = (f32[7,8,128]{2,1,0:T(8,128)S(1)}, f32[7,8,128]{2,1,0:T(8,128)S(1)}, u32[]{:S(2)}, u32[]{:S(2)}) collective-permute-start(f32[7,8,128]{2,1,0:T(8,128)S(1)} %get-tuple-element.247), channel_id=1, source_target_pairs={{23,0},{12,3},{27,4},{16,7},{31,8},{20,11},{3,12},{24,15},{7,16},{... | collective-permute-start | bytes 86024 | tf_op jit(solution)/shard_map/cond/branch_5_fun/ppermute | solution.py:645
  34.9 3.1 %collective-permute-start.29 = (f32[8,128]{1,0:T(8,128)S(1)}, f32[8,128]{1,0:T(8,128)S(1)}, u32[]{:S(2)}, u32[]{:S(2)}) collective-permute-start(f32[8,128]{1,0:T(8,128)S(1)} %get-tuple-element.327), channel_id=1, source_target_pairs={{0,3},{1,2},{2,1},{3,0},{4,7},{5,6},{6,5},{7,4},{8,11},{9,10},{10,... | collective-permute-start | bytes 12296 | tf_op jit(solution)/shard_map/cond/branch_5_fun/ppermute | solution.py:519
  35.0 3.0 %collective-permute-start.28 = (f32[8,128]{1,0:T(8,128)S(1)}, f32[8,128]{1,0:T(8,128)S(1)}, u32[]{:S(2)}, u32[]{:S(2)}) collective-permute-start(f32[8,128]{1,0:T(8,128)S(1)} %get-tuple-element.328), channel_id=1, source_target_pairs={{0,1},{1,0},{2,3},{3,2},{4,5},{5,4},{6,7},{7,6},{8,9},{9,8},{10,11... | collective-permute-start | bytes 12296 | tf_op jit(solution)/shard_map/cond/branch_5_fun/ppermute | solution.py:519
  39.3 0.6 %copy-start.1 = (f32[3,1,1,64]{3,2,1,0:T(1,128)}, f32[3,1,1,64]{3,2,1,0:T(1,128)S(1)}, u32[]{:S(2)}) copy-start(f32[3,1,1,64]{3,2,1,0:T(1,128)S(1)} %get-tuple-element.295) | copy-start | bytes 2308
  39.3 0.6 %copy-start.2 = (f32[3,1,1,64]{3,2,1,0:T(1,128)}, f32[3,1,1,64]{3,2,1,0:T(1,128)S(1)}, u32[]{:S(2)}) copy-start(f32[3,1,1,64]{3,2,1,0:T(1,128)S(1)} %get-tuple-element.296) | copy-start | bytes 2308
  39.3 0.8 %copy-start = (f32[19,8,8,128]{3,2,1,0:T(8,128)}, f32[19,8,8,128]{3,2,1,0:T(8,128)S(1)}, u32[]{:S(2)}) copy-start(f32[19,8,8,128]{3,2,1,0:T(8,128)S(1)} %get-tuple-element.311) | copy-start | bytes 1867780
